TPU v7x, 32 devices: a whole 2x2x4 slice. The times are simulated.
32 devices in a mesh: seq: 8 (over z, x), head: 4 (over y, core).
Axes of the slice: x: 2, y: 2, z: 4, core: 2. Of those that a mesh axis runs over, the one named last changes fastest.
Arguments:
- tokens: bfloat16 [2, 8, 896, 768], P(None, None, 'seq'), may hold values from -6 to 6
- prev_logits: bfloat16 [2, 8, 896, 12, 896], P(None, None, 'seq', 'head'), may hold values from -6 to 6
- lengths: int32 [2, 8], replicated, may hold values from 128 to 896, as said below
- dealing: int32 [2, 8], replicated, may hold values from 0 to 7, each once within a row
- w_query: bfloat16 [768, 768], P('seq', 'head'), may hold values from -0.21875 to 0.21875
- b_query: bfloat16 [12, 64], P('head', 'seq'), may hold values from -3 to 3
- w_key: bfloat16 [768, 768], P('seq', 'head'), may hold values from -0.21875 to 0.21875
- w_value: bfloat16 [768, 768], P('seq', 'head'), may hold values from -0.21875 to 0.21875
- b_value: bfloat16 [12, 64], P('head', 'seq'), may hold values from -1.75 to 1.75
- w_out: bfloat16 [768, 768], P('head', 'seq'), may hold values from -1.75 to 1.75
- b_out: bfloat16 [768], P('seq'), may hold values from -3 to 3
- gain_one: bfloat16 [768], P('seq'), may hold values from 0.5 to 1.5
- shift_one: bfloat16 [768], P('seq'), may hold values from -3 to 3
- w_up: bfloat16 [768, 3072], P('seq', 'head'), may hold values from -0.21875 to 0.21875
- b_up: bfloat16 [12, 256], P('head', 'seq'), may hold values from -3 to 3
- w_down: bfloat16 [3072, 768], P('head', 'seq'), may hold values from -0.109375 to 0.109375
- b_down: bfloat16 [768], P('seq'), may hold values from -3 to 3
- gain_two: bfloat16 [768], P('seq'), may hold values from 0.5 to 1.5
- shift_two: bfloat16 [768], P('seq'), may hold values from -3 to 3
- cot_tokens: bfloat16 [2, 8, 896, 768], P(None, None, 'seq'), may hold values from -6 to 6
- cot_logits: bfloat16 [2, 8, 896, 12, 896], P(None, 'seq', None, 'head'), may hold values from -1.75 to 1.75
Outputs:
- out_tokens: bfloat16 [2, 8, 896, 768], P(None, None, 'seq')
- out_logits: bfloat16 [2, 8, 896, 12, 896], P(None, 'seq', None, 'head')
- grad_tokens: bfloat16 [2, 8, 896, 768], P(None, None, 'seq', 'head')
- grad_logits: bfloat16 [2, 8, 896, 12, 896], P(None, None, 'seq', 'head')
- grad_w_query: float32 [768, 768], P('seq', 'head')
- grad_b_query: float32 [12, 64], P('head', 'seq')
- grad_w_key: float32 [768, 768], P('seq', 'head')
- grad_w_value: float32 [768, 768], P('seq', 'head')
- grad_b_value: float32 [12, 64], P('head', 'seq')
- grad_w_out: float32 [768, 768], P('head', 'seq')
- grad_b_out: float32 [768], P('seq')
- grad_gain_one: float32 [768], P('seq')
- grad_shift_one: float32 [768], P('seq')
- grad_w_up: float32 [768, 3072], P('seq', 'head')
- grad_b_up: float32 [12, 256], P('head', 'seq')
- grad_w_down: float32 [3072, 768], P('head', 'seq')
- grad_b_down: float32 [768], P('seq')
- grad_gain_two: float32 [768], P('seq')
- grad_shift_two: float32 [768], P('seq')
Inputs may be any that keep to these rules, and one draw needn't show every extreme that they name: `lengths`: in every micro-batch some sequence has exactly 896 tokens. `dealing`: each row names every slot 0 to 7 once.
All inputs are finite; a program needn't handle non-finite values.
Results may differ from a plain program's by a relative error of at most 0.014.
Values may be sent and summed in bfloat16 or wider, within the bound.
A program may use at most 256 MiB of HBM per device.

v0:
```python
import jax
import jax.numpy as jnp
from jax import lax
from jax.sharding import PartitionSpec as P

HEAD_DIM = 64


epsilon = 1e-12


def cut_along(x, dim, peers):
    before, after = (x.shape[:dim], x.shape[dim + 1 :])
    return jnp.moveaxis(x.reshape(*before, peers, -1, *after), dim, 0)


def sum_at_owner(x, axis, dim):
    blocks = cut_along(x, dim, lax.axis_size(axis))
    arrived = lax.all_to_all(blocks, axis, split_axis=0, concat_axis=0, tiled=True)
    return arrived.astype(jnp.float32).sum(axis=0)


def side_by_side(arrays, axis, dim, along):
    both = jnp.concatenate(arrays, axis=along)
    result, at, finished = (sum_at_owner(both, axis, dim), 0, [])
    for a in arrays:
        finished.append(lax.slice_in_dim(result, at, at + a.shape[along], axis=along))
        at += a.shape[along]
    return tuple(finished)


def side_by_side_2(arrays, axis, dim, along):
    columns = [a.reshape(*a.shape[:along], -1) for a in arrays]
    both = jnp.concatenate(columns, axis=along)
    result, at, finished = (sum_at_owner(both, axis, dim), 0, [])
    for a, column in zip(arrays, columns):
        slab = result[..., at : at + column.shape[along]]
        finished.append(slab.reshape(*slab.shape[:along], *a.shape[along:]))
        at += column.shape[along]
    return tuple(finished)


def layer_norm(values, gain, shift):
    center = values - jnp.mean(values, axis=-1, keepdims=True)
    spread = jnp.mean(center * center, axis=-1, keepdims=True)
    return center * lax.rsqrt(spread + epsilon) * gain + shift


def exact_gelu(values):
    return jax.nn.gelu(values, approximate=False)


def mask_scores(raw_scores, length):
    key_valid = jnp.arange(raw_scores.shape[2]) < length
    return jnp.where(key_valid[None, None, :], raw_scores, -jnp.inf)


def on_device(
    tokens,
    prev_logits,
    lengths,
    dealing,
    w_query,
    b_query,
    w_key,
    w_value,
    b_value,
    w_out,
    b_out,
    gain_one,
    shift_one,
    w_up,
    b_up,
    w_down,
    b_down,
    gain_two,
    shift_two,
    cot_tokens,
    cot_logits,
):
    micro_count = tokens.shape[0]
    seq_count = tokens.shape[1]
    piece_rows = tokens.shape[2]
    model_width = tokens.shape[3]
    extent = piece_rows * seq_count
    heads_here = prev_logits.shape[3]
    width_here = model_width // lax.axis_size("head")
    score_scale = HEAD_DIM ** (-0.5)
    owner_slot = lax.axis_index("seq")
    head_slot = lax.axis_index("head")
    zero_shift = jnp.zeros((model_width,), jnp.float32)
    out_token_list = []
    out_logit_list = []
    grad_token_list = []
    grad_logit_list = []
    grad_totals = None
    for micro_batch in range(micro_count):
        full_weights = (
            lax.all_gather(w_query, "seq", axis=0, tiled=True),
            lax.all_gather(w_key, "seq", axis=0, tiled=True),
            lax.all_gather(w_value, "seq", axis=0, tiled=True),
            lax.all_gather(w_out, "seq", axis=1, tiled=True),
            lax.all_gather(w_up, "seq", axis=0, tiled=True),
            lax.all_gather(w_down, "seq", axis=1, tiled=True),
            lax.all_gather(b_query, "seq", axis=1, tiled=True),
            lax.all_gather(b_value, "seq", axis=1, tiled=True),
            lax.all_gather(b_out, "seq", axis=0, tiled=True),
            lax.all_gather(gain_one, "seq", axis=0, tiled=True),
            lax.all_gather(shift_one, "seq", axis=0, tiled=True),
            lax.all_gather(b_up, "seq", axis=1, tiled=True),
            lax.all_gather(b_down, "seq", axis=0, tiled=True),
            lax.all_gather(gain_two, "seq", axis=0, tiled=True),
            lax.all_gather(shift_two, "seq", axis=0, tiled=True),
        )
        (
            query_full,
            key_full,
            value_full,
            out_full,
            up_full,
            down_full,
            bias_query,
            bias_value,
            bias_out,
            gain_first,
            shift_first,
            bias_up,
            bias_down,
            gain_second,
            shift_second,
        ) = full_weights
        inverse = (
            jnp.zeros((seq_count,), jnp.int32)
            .at[dealing[micro_batch]]
            .set(jnp.arange(seq_count, dtype=jnp.int32))
        )
        own_sequence = inverse[owner_slot]
        own_length = lengths[micro_batch, own_sequence]
        send_tokens = jnp.take(tokens[micro_batch], inverse, axis=0)
        send_prev = jnp.take(prev_logits[micro_batch], inverse, axis=0).reshape(
            seq_count, piece_rows, heads_here * extent
        )
        send_cot = jnp.take(cot_tokens[micro_batch], inverse, axis=0)
        got_tokens, got_prev, got_cot = (
            lax.all_to_all(send_tokens, "seq", split_axis=0, concat_axis=1, tiled=True),
            lax.all_to_all(send_prev, "seq", split_axis=0, concat_axis=1, tiled=True),
            lax.all_to_all(send_cot, "seq", split_axis=0, concat_axis=1, tiled=True),
        )
        rows_in = got_tokens.reshape(extent, model_width)
        prev_rows = got_prev.reshape(extent, heads_here, extent).astype(jnp.float32)
        cot_rows = got_cot.reshape(extent, model_width).astype(jnp.float32)
        query_pre = jnp.dot(rows_in, query_full, preferred_element_type=jnp.float32)
        queries = (query_pre + bias_query.reshape(-1).astype(jnp.float32)).astype(jnp.bfloat16)
        keys_all = jnp.dot(rows_in, key_full, preferred_element_type=jnp.float32).astype(
            jnp.bfloat16
        )
        value_pre = jnp.dot(rows_in, value_full, preferred_element_type=jnp.float32)
        values = (value_pre + bias_value.reshape(-1).astype(jnp.float32)).astype(jnp.bfloat16)
        query_heads = queries.reshape(extent, heads_here, HEAD_DIM)
        key_heads = keys_all.reshape(extent, heads_here, HEAD_DIM)
        value_heads = values.reshape(extent, heads_here, HEAD_DIM)
        raw_scores = (
            jnp.einsum("qhd,khd->qhk", query_heads, key_heads, preferred_element_type=jnp.float32)
            * score_scale
            + prev_rows
        )
        masked = mask_scores(raw_scores, own_length)
        row_top = jnp.max(masked, axis=-1, keepdims=True)
        shifted_exp = jnp.exp(masked - row_top)
        row_total = jnp.sum(shifted_exp, axis=-1, keepdims=True)
        attend = shifted_exp / row_total
        log_total = row_top + jnp.log(row_total)
        out_logit_list.append(raw_scores.astype(jnp.bfloat16)[None])
        context = (
            jnp.einsum(
                "qhk,khd->qhd",
                attend.astype(jnp.bfloat16),
                value_heads,
                preferred_element_type=jnp.float32,
            )
            .astype(jnp.bfloat16)
            .reshape(extent, heads_here * HEAD_DIM)
        )
        out_part = jnp.dot(context, out_full, preferred_element_type=jnp.float32)
        branch = lax.psum(out_part, "head") + bias_out.astype(jnp.float32)
        resid_one = rows_in.astype(jnp.float32) + branch
        hidden = layer_norm(
            resid_one, gain_first.astype(jnp.float32), shift_first.astype(jnp.float32)
        )
        hidden_low = hidden.astype(jnp.bfloat16)
        before_gelu = jnp.dot(
            hidden_low, up_full, preferred_element_type=jnp.float32
        ) + bias_up.reshape(-1).astype(jnp.float32)
        active = exact_gelu(before_gelu).astype(jnp.bfloat16)
        down_part = jnp.dot(active, down_full, preferred_element_type=jnp.float32)
        resid_two = hidden + (
            lax.psum(down_part.astype(jnp.bfloat16), "head").astype(jnp.float32)
            + bias_down.astype(jnp.float32)
        )
        result = layer_norm(
            resid_two, gain_second.astype(jnp.float32), shift_second.astype(jnp.float32)
        )
        out_rows = result.astype(jnp.bfloat16)
        (
            back_query,
            back_key,
            back_value,
            back_out,
            back_up,
            back_down,
            back_gain_first,
            back_gain_second,
        ) = (
            lax.all_gather(w_query, "seq", axis=0, tiled=True),
            lax.all_gather(w_key, "seq", axis=0, tiled=True),
            lax.all_gather(w_value, "seq", axis=0, tiled=True),
            lax.all_gather(w_out, "seq", axis=1, tiled=True),
            lax.all_gather(w_up, "seq", axis=0, tiled=True),
            lax.all_gather(w_down, "seq", axis=1, tiled=True),
            lax.all_gather(gain_one, "seq", axis=0, tiled=True),
            lax.all_gather(gain_two, "seq", axis=0, tiled=True),
        )
        norm_two_value, norm_two_back = jax.vjp(
            layer_norm, resid_two, back_gain_second.astype(jnp.float32), zero_shift
        )
        d_resid_two, d_gain_two, d_shift_two = norm_two_back(cot_rows)
        d_b_down = jnp.sum(d_resid_two, axis=0)
        grad_two_low = d_resid_two.astype(jnp.bfloat16)
        d_w_down = jnp.einsum("rf,rd->fd", active, grad_two_low, preferred_element_type=jnp.float32)
        d_active = jnp.einsum(
            "rd,fd->rf", grad_two_low, back_down, preferred_element_type=jnp.float32
        )
        gelu_value, gelu_back = jax.vjp(exact_gelu, before_gelu)
        d_before = gelu_back(d_active)[0]
        d_b_up = jnp.sum(d_before, axis=0).reshape(heads_here, -1)
        before_low = d_before.astype(jnp.bfloat16)
        d_w_up = jnp.einsum("rd,rf->df", hidden_low, before_low, preferred_element_type=jnp.float32)
        up_part = jnp.einsum("rf,df->rd", before_low, back_up, preferred_element_type=jnp.float32)
        d_hidden = d_resid_two + lax.psum(up_part.astype(jnp.bfloat16), "head").astype(jnp.float32)
        norm_one_value, norm_one_back = jax.vjp(
            layer_norm, resid_one, back_gain_first.astype(jnp.float32), zero_shift
        )
        d_resid_one, d_gain_one, d_shift_one = norm_one_back(d_hidden)
        d_b_out = jnp.sum(d_resid_one, axis=0)
        grad_one_low = d_resid_one.astype(jnp.bfloat16)
        d_w_out = jnp.einsum("rc,rd->cd", context, grad_one_low, preferred_element_type=jnp.float32)
        d_context = (
            jnp.einsum("rd,cd->rc", grad_one_low, back_out, preferred_element_type=jnp.float32)
            .astype(jnp.bfloat16)
            .reshape(extent, heads_here, HEAD_DIM)
        )
        raw_again = (
            jnp.einsum("qhd,khd->qhk", query_heads, key_heads, preferred_element_type=jnp.float32)
            * score_scale
            + prev_rows
        )
        attend_again = jnp.exp(mask_scores(raw_again, own_length) - log_total)
        d_attend = jnp.einsum(
            "qhd,khd->qhk", d_context, value_heads, preferred_element_type=jnp.float32
        )
        d_values = jnp.einsum(
            "qhk,qhd->khd",
            attend_again.astype(jnp.bfloat16),
            d_context,
            preferred_element_type=jnp.float32,
        )
        d_scores = attend_again * (
            d_attend - jnp.sum(attend_again * d_attend, axis=-1, keepdims=True)
        ) + cot_logits[micro_batch, 0].astype(jnp.float32)
        scores_low = d_scores.astype(jnp.bfloat16)
        d_queries = (
            jnp.einsum("qhk,khd->qhd", scores_low, key_heads, preferred_element_type=jnp.float32)
            * score_scale
        )
        d_keys = (
            jnp.einsum("qhk,qhd->khd", scores_low, query_heads, preferred_element_type=jnp.float32)
            * score_scale
        )
        d_b_query = jnp.sum(d_queries, axis=0)
        d_b_value = jnp.sum(d_values, axis=0)
        queries_low = d_queries.astype(jnp.bfloat16).reshape(extent, heads_here * HEAD_DIM)
        keys_low = d_keys.astype(jnp.bfloat16).reshape(extent, heads_here * HEAD_DIM)
        values_low = d_values.astype(jnp.bfloat16).reshape(extent, heads_here * HEAD_DIM)
        d_w_query = jnp.einsum(
            "rd,rc->dc", rows_in, queries_low, preferred_element_type=jnp.float32
        )
        d_w_key = jnp.einsum("rd,rc->dc", rows_in, keys_low, preferred_element_type=jnp.float32)
        d_w_value = jnp.einsum("rd,rc->dc", rows_in, values_low, preferred_element_type=jnp.float32)
        input_part = jnp.einsum(
            "rc,dc->rd", queries_low, back_query, preferred_element_type=jnp.float32
        )
        input_part = input_part + jnp.einsum(
            "rc,dc->rd", keys_low, back_key, preferred_element_type=jnp.float32
        )
        input_part = input_part + jnp.einsum(
            "rc,dc->rd", values_low, back_value, preferred_element_type=jnp.float32
        )
        input_share = lax.psum_scatter(
            input_part.astype(jnp.bfloat16), "head", scatter_dimension=1, tiled=True
        ).astype(jnp.float32)
        resid_share = lax.dynamic_slice_in_dim(d_resid_one, head_slot * width_here, width_here, 1)
        grad_rows = (resid_share + input_share).astype(jnp.bfloat16)
        back_tokens, back_grads, back_logits = (
            lax.all_to_all(
                out_rows.reshape(seq_count, piece_rows, model_width),
                "seq",
                split_axis=0,
                concat_axis=0,
                tiled=True,
            ),
            lax.all_to_all(
                grad_rows.reshape(seq_count, piece_rows, width_here),
                "seq",
                split_axis=0,
                concat_axis=0,
                tiled=True,
            ),
            lax.all_to_all(
                scores_low.reshape(seq_count, piece_rows, heads_here * extent),
                "seq",
                split_axis=0,
                concat_axis=0,
                tiled=True,
            ),
        )
        out_token_list.append(jnp.take(back_tokens, dealing[micro_batch], axis=0))
        grad_token_list.append(jnp.take(back_grads, dealing[micro_batch], axis=0))
        grad_logit_list.append(
            jnp.take(back_logits, dealing[micro_batch], axis=0).reshape(
                seq_count, piece_rows, heads_here, extent
            )
        )
        local_grads = (
            d_w_query,
            d_b_query,
            d_w_key,
            d_w_value,
            d_b_value,
            d_w_out,
            d_b_out,
            d_gain_one,
            d_shift_one,
            d_w_up,
            d_b_up,
            d_w_down,
            d_b_down,
            d_gain_two,
            d_shift_two,
        )
        if grad_totals is None:
            grad_totals = local_grads
        else:
            grad_totals = tuple((total + extra for total, extra in zip(grad_totals, local_grads)))
    final_grads = (
        sum_at_owner(grad_totals[0].astype(jnp.bfloat16), "seq", 0),
        sum_at_owner(grad_totals[1].astype(jnp.bfloat16), "seq", 1),
        *side_by_side(
            (grad_totals[2].astype(jnp.bfloat16), grad_totals[3].astype(jnp.bfloat16)), "seq", 0, 1
        ),
        sum_at_owner(grad_totals[4].astype(jnp.bfloat16), "seq", 1),
        sum_at_owner(grad_totals[5].astype(jnp.bfloat16), "seq", 1),
        sum_at_owner(grad_totals[6].astype(jnp.bfloat16), "seq", 0),
        sum_at_owner(grad_totals[7].astype(jnp.bfloat16), "seq", 0),
        *side_by_side_2(
            (grad_totals[8].astype(jnp.bfloat16), grad_totals[9].astype(jnp.bfloat16)), "seq", 0, 1
        ),
        sum_at_owner(grad_totals[10].astype(jnp.bfloat16), "seq", 1),
        sum_at_owner(grad_totals[11].astype(jnp.bfloat16), "seq", 1),
        sum_at_owner(grad_totals[12].astype(jnp.bfloat16), "seq", 0),
        sum_at_owner(grad_totals[13].astype(jnp.bfloat16), "seq", 0),
        sum_at_owner(grad_totals[14].astype(jnp.bfloat16), "seq", 0),
    )
    out_tokens = jnp.stack(out_token_list, axis=0)
    out_logits = jnp.stack(out_logit_list, axis=0)
    grad_tokens = jnp.stack(grad_token_list, axis=0)
    grad_logits = jnp.stack(grad_logit_list, axis=0)
    return (
        out_tokens,
        out_logits,
        grad_tokens,
        grad_logits,
        final_grads[0],
        final_grads[1],
        final_grads[2],
        final_grads[3],
        final_grads[4],
        final_grads[5],
        final_grads[6],
        final_grads[7],
        final_grads[8],
        final_grads[9],
        final_grads[10],
        final_grads[11],
        final_grads[12],
        final_grads[13],
        final_grads[14],
    )


def solution(mesh):
    placed = (
        P(None, None, "seq", None),
        P(None, None, "seq", "head", None),
        P(),
        P(),
        P("seq", "head"),
        P("head", "seq"),
        P("seq", "head"),
        P("seq", "head"),
        P("head", "seq"),
        P("head", "seq"),
        P("seq"),
        P("seq"),
        P("seq"),
        P("seq", "head"),
        P("head", "seq"),
        P("head", "seq"),
        P("seq"),
        P("seq"),
        P("seq"),
        P(None, None, "seq", None),
        P(None, "seq", None, "head", None),
    )
    return jax.shard_map(
        on_device,
        mesh=mesh,
        in_specs=placed,
        out_specs=(
            P(None, None, "seq", None),
            P(None, "seq", None, "head", None),
            P(None, None, "seq", "head"),
            P(None, None, "seq", "head", None),
            P("seq", "head"),
            P("head", "seq"),
            P("seq", "head"),
            P("seq", "head"),
            P("head", "seq"),
            P("head", "seq"),
            P("seq"),
            P("seq"),
            P("seq"),
            P("seq", "head"),
            P("head", "seq"),
            P("head", "seq"),
            P("seq"),
            P("seq"),
            P("seq"),
        ),
        check_vma=False,
    )
```

profile of v0, /device:TPU:15, one launch (start us, length us, event | category | flops | bytes accessed | tf_op | source)
XLA Modules:
  0.0 1487.0 jit_solution(17334299433931007767)
XLA Ops:
  36.2 21.5 %all-to-all-done = bf16[8,112,768]{2,1,0:T(8,128)(2,1)S(1)} async-done(((bf16[8,112,768]{2,1,0:T(8,128)(2,1)}), bf16[8,112,768]{2,1,0:T(8,128)(2,1)S(1)}, u32[]{:S(2)}, u32[]{:S(2)}) %all-to-all-start) | async-done | bytes 1376288 | tf_op jit(solution)/shard_map/all_to_all | solution.py:145
  57.7 6.3 all-to-all-start.3
  64.1 8.4 slice_bitcast_fusion.1
  83.2 8.0 copy.177
  91.3 7.7 copy.178
  104.4 5.7 gather_fusion.4
  115.2 8.0 copy.183
  123.2 7.7 copy.184
  131.0 77.4 %all-to-all-done.1 = bf16[8,112,2688]{2,1,0:T(8,128)(2,1)} async-done(((bf16[8,112,2688]{2,1,0:T(8,128)(2,1)}), bf16[8,112,2688]{2,1,0:T(8,128)(2,1)}, u32[]{:S(2)}, u32[]{:S(2)}) %all-to-all-start.1) | async-done | bytes 4816928 | tf_op jit(solution)/shard_map/all_to_all | solution.py:146
  208.4 6.5 all-to-all-start.4
  218.7 107.3 %all-gather.1 = bf16[8,8,3]{1,2,0:T(4,128)(2,1)S(1)} all-gather(bf16[1,8,3]{1,2,0:T(4,128)(2,1)S(1)} %bitcast.338), channel_id=1, replica_groups=mesh['seq'=8,'head'=4] {'seq'}, dimensions={0}, use_global_device_ids=true | all-gather | bytes 432 | tf_op jit(solution)/shard_map/all_gather | solution.py:105
  326.1 9.3 all-gather
  338.9 25.5 %all_gather.33 = bf16[768,192]{1,0:T(8,128)(2,1)S(1)} all-gather(bf16[96,192]{1,0:T(8,128)(2,1)S(1)} %copy-done.66), channel_id=1, replica_groups=mesh['seq'=8,'head'=4] {'seq'}, dimensions={0}, use_global_device_ids=true | all-gather | bytes 331776 | tf_op jit(solution)/shard_map/all_gather | solution.py:99
  364.4 24.9 %all_gather.32 = bf16[768,192]{1,0:T(8,128)(2,1)S(1)} all-gather(bf16[96,192]{1,0:T(8,128)(2,1)S(1)} %copy-done.67), channel_id=1, replica_groups=mesh['seq'=8,'head'=4] {'seq'}, dimensions={0}, use_global_device_ids=true | all-gather | bytes 331776 | tf_op jit(solution)/shard_map/all_gather | solution.py:100
  389.3 25.0 %all_gather.30 = bf16[768,192]{1,0:T(8,128)(2,1)S(1)} all-gather(bf16[96,192]{1,0:T(8,128)(2,1)S(1)} %copy-done.68), channel_id=1, replica_groups=mesh['seq'=8,'head'=4] {'seq'}, dimensions={0}, use_global_device_ids=true | all-gather | bytes 331776 | tf_op jit(solution)/shard_map/all_gather | solution.py:101
  414.3 24.8 %all_gather.35 = bf16[192,768]{0,1:T(8,128)(2,1)S(1)} all-gather(bf16[192,96]{0,1:T(8,128)(2,1)S(1)} %copy.181), channel_id=1, replica_groups=mesh['seq'=8,'head'=4] {'seq'}, dimensions={1}, use_global_device_ids=true | all-gather | bytes 331776 | tf_op jit(solution)/shard_map/all_gather | solution.py:102
  446.5 13.6 reshape.846
  460.1 14.7 copy.227
  474.8 13.4 reshape.847
  488.3 14.7 copy.228
  503.0 6.0 select_reduce_fusion.1
  532.3 11.1 all-to-all-start.8
  546.7 28.8 %all-reduce.7 = (bf16[768]{0:T(1024)(128)(2,1)S(1)}, bf16[768]{0:T(1024)(128)(2,1)S(1)}, bf16[768]{0:T(1024)(128)(2,1)}, bf16[768]{0:T(1024)(128)(2,1)}, bf16[768]{0:T(1024)(128)(2,1)}, /*index=5*/bf16[768]{0:T(1024)(128)(2,1)}) all-reduce(bf16[768]{0:T(1024)(128)(2,1)S(1)} %dynamic-update-slice, ...), channel_id=1, replica_groups=mesh['seq'=8,'head'=4] {'seq'}, use_global_device_ids=true, to_apply=%add | all-reduce | flops 4608 | bytes 18432
  576.7 16.7 %all-gather.2 = bf16[8,32,3]{1,2,0:T(4,128)(2,1)S(1)} all-gather(bf16[1,32,3]{1,2,0:T(4,128)(2,1)} %bitcast.340), channel_id=1, replica_groups=mesh['seq'=8,'head'=4] {'seq'}, dimensions={0}, use_global_device_ids=true | all-gather | bytes 1728 | tf_op jit(solution)/shard_map/all_gather | solution.py:110
  594.1 78.4 %all-reduce.14.cloned.1.call-done = (f32[896,768]{1,0:T(8,128)}, f32[896,768]{1,0:T(8,128)}) async-done(((f32[896,768]{1,0:T(8,128)}, f32[896,768]{1,0:T(8,128)}), (f32[896,768]{1,0:T(8,128)}, f32[896,768]{1,0:T(8,128)})) %all-reduce.14.cloned.1.call-update) | async-done | bytes 5505040 | tf_op jit(solution)/shard_map/psum | solution.py:185
  683.7 15.1 %multiply_convert_fusion.1 = (bf16[896,768]{1,0:T(8,128)(2,1)}, f32[896,768]{1,0:T(8,128)}, bf16[896,768]{1,0:T(8,128)(2,1)}, f32[896,768]{1,0:T(8,128)}, f32[896,768]{1,0:T(8,128)}) fusion(f32[768]{0:T(1024)S(1)} %copy-done.111, f32[896,768]{1,0:T(8,128)S(1)} %fusion.98, bf16[768,768]{1,0:T(8,128)(2,1)S(1)} %copy-done.120, f32[896,768]{1,0:T(8,128)S(1)} %copy-done.4, ...), kind=kOutput, calls=%fused_computation.112 | convolution fusion | flops 1151238144 | bytes 17711104 | tf_op jit(solution)/shard_map/dot_general | solution.py:191
  713.0 8.3 fusion.117
  721.3 7.7 copy.234
  729.0 7.6 copy.235
  736.6 31.2 %all-reduce.18.cloned.1.call-done = (bf16[896,768]{1,0:T(8,128)(2,1)}, bf16[896,768]{1,0:T(8,128)(2,1)}) async-done(((bf16[896,768]{1,0:T(8,128)(2,1)}, bf16[896,768]{1,0:T(8,128)(2,1)}), (bf16[896,768]{1,0:T(8,128)(2,1)}, bf16[896,768]{1,0:T(8,128)(2,1)})) %all-reduce.18.cloned.1.call-update) | async-done | bytes 2752528 | tf_op jit(solution)/shard_map/psum | solution.py:197
  776.7 6.3 fusion.27
  783.1 5.8 fusion.110
  788.9 6.6 fusion.123
  821.5 46.3 %all-reduce.16.cloned.1.call-done = (bf16[896,768]{1,0:T(8,128)(2,1)}, bf16[896,768]{1,0:T(8,128)(2,1)}) async-done(((bf16[896,768]{1,0:T(8,128)(2,1)}, bf16[896,768]{1,0:T(8,128)(2,1)}), (bf16[896,768]{1,0:T(8,128)(2,1)}, bf16[896,768]{1,0:T(8,128)(2,1)})) %all-reduce.16.cloned.1.call-update) | async-done | bytes 2752528 | tf_op jit(solution)/shard_map/psum | solution.py:239
  867.9 8.5 multiply_reduce_fusion.1
  876.4 7.1 fusion.107
  889.3 7.1 fusion.119
  896.5 16.3 %fusion.3 = bf16[896,3,896]{0,2,1:T(8,128)(2,1)} fusion(f32[896,3,896]{0,2,1:T(8,128)} %copy-done.11, bf16[1,1,896,3,896]{2,4,3,1,0:T(8,128)(2,1)} %copy.234, f32[896,3]{0,1:T(4,128)S(1)} %copy-done.104, pred[896]{0:T(1024)(128)(4,1)S(1)} %copy-done.109, bf16[896,3,64]{0,2,1:T(8,128)(2,1)S(1)} %bitcast.327, bf16[896,3,64]{0,2,1:T(8,128)(2,1)} %bitcast.331), kind=kOutput, calls=%fused_computation.21 | convolution fusion | flops 640650752 | bytes 19967360 | tf_op jit(solution)/shard_map/sub | solution.py:268
  912.8 7.2 fusion.118
  920.0 15.9 %fusion.2 = bf16[896,3,896]{0,2,1:T(8,128)(2,1)} fusion(f32[896,3,896]{0,2,1:T(8,128)} %copy-done.12, bf16[1,1,896,3,896]{2,4,3,1,0:T(8,128)(2,1)} %copy.235, f32[896,3]{0,1:T(4,128)S(1)} %copy-done.102, pred[896]{0:T(1024)(128)(4,1)S(1)} %copy-done.106, bf16[896,3,64]{0,2,1:T(8,128)(2,1)S(1)} %bitcast.325, bf16[896,3,64]{0,2,1:T(8,128)(2,1)} %bitcast.329), kind=kOutput, calls=%fused_computation.19 | convolution fusion | flops 640650752 | bytes 19967360 | tf_op jit(solution)/shard_map/sub | solution.py:268
  1029.1 6.4 all-to-all-start.21
  1046.2 6.8 all-to-all-done.21
  1052.9 22.4 %all_to_all.154 = bf16[8,96,384]{2,1,0:T(8,128)(2,1)} all-to-all(bf16[8,96,384]{2,1,0:T(8,128)(2,1)S(1)} %bitcast.308), channel_id=1, replica_groups=mesh['seq'=8,'head'=4] {'seq'}, dimensions={0} | all-to-all | bytes 1179648 | tf_op jit(solution)/shard_map/all_to_all | solution.py:19
  1083.9 19.0 %all-to-all-done.2 = bf16[8,112,768]{2,1,0:T(8,128)(2,1)S(1)} async-done(((bf16[8,112,768]{2,1,0:T(8,128)(2,1)}), bf16[8,112,768]{2,1,0:T(8,128)(2,1)S(1)}, u32[]{:S(2)}, u32[]{:S(2)}) %all-to-all-start.2) | async-done | bytes 1376288 | tf_op jit(solution)/shard_map/all_to_all | solution.py:304
  1104.0 7.6 all-to-all-start.5
  1124.2 13.7 all-to-all-done.5
  1137.8 6.8 all-to-all-start.19
  1148.2 26.6 %all-to-all-done.19 = bf16[8,96,769]{2,1,0:T(8,128)(2,1)S(1)} async-done(((bf16[8,96,769]{2,1,0:T(8,128)(2,1)}), bf16[8,96,769]{2,1,0:T(8,128)(2,1)S(1)}, u32[]{:S(2)}, u32[]{:S(2)}) %all-to-all-start.19) | async-done | bytes 1181216 | tf_op jit(solution)/shard_map/all_to_all | solution.py:19
  1174.8 6.5 all-to-all-start.7
  1186.6 7.2 all-to-all-done.7
  1193.8 6.1 all-to-all-start.9
  1199.9 10.8 reshape.643
  1210.7 8.1 copy.199
  1225.0 10.8 reshape.644
  1235.9 8.2 copy.201
  1244.1 82.0 %all-to-all-done.10 = bf16[8,112,2688]{2,1,0:T(8,128)(2,1)} async-done(((bf16[8,112,2688]{2,1,0:T(8,128)(2,1)}), bf16[8,112,2688]{2,1,0:T(8,128)(2,1)}, u32[]{:S(2)}, u32[]{:S(2)}) %all-to-all-start.10) | async-done | bytes 4816928 | tf_op jit(solution)/shard_map/all_to_all | solution.py:318
  1326.1 6.7 all-to-all-start.11
  1334.1 8.6 pad_maximum_fusion.1
  1342.7 13.3 copy.216
  1387.7 7.7 copy.200
  1395.4 41.3 %all-to-all-done.11 = bf16[8,112,2688]{2,1,0:T(8,128)(2,1)} async-done(((bf16[8,112,2688]{2,1,0:T(8,128)(2,1)}), bf16[8,112,2688]{2,1,0:T(8,128)(2,1)}, u32[]{:S(2)}, u32[]{:S(2)}) %all-to-all-start.11) | async-done | bytes 4816928 | tf_op jit(solution)/shard_map/all_to_all | solution.py:318
  1447.4 7.8 copy.202
  1455.3 10.2 pad_maximum_fusion
  1465.5 14.2 copy.217
  (527 shorter events, 338.0 us)
Async XLA Ops:
  21.8 35.9 %all-to-all-start = ((bf16[8,112,768]{2,1,0:T(8,128)(2,1)}), bf16[8,112,768]{2,1,0:T(8,128)(2,1)S(1)}, u32[]{:S(2)}, u32[]{:S(2)}) async-start(bf16[8,112,768]{2,1,0:T(8,128)(2,1)} %get-tuple-element.218), calls=%async_computation | async-start | bytes 2752512 | tf_op jit(solution)/shard_map/all_to_all | solution.py:145
  57.7 41.2 %all-to-all-start.3 = ((bf16[8,112,768]{2,1,0:T(8,128)(2,1)}), bf16[8,112,768]{2,1,0:T(8,128)(2,1)S(1)}, u32[]{:S(2)}, u32[]{:S(2)}) async-start(bf16[8,112,768]{2,1,0:T(8,128)(2,1)} %get-tuple-element.220), calls=%async_computation.3 | async-start | bytes 2752512 | tf_op jit(solution)/shard_map/all_to_all | solution.py:145
  99.0 109.4 %all-to-all-start.1 = ((bf16[8,112,2688]{2,1,0:T(8,128)(2,1)}), bf16[8,112,2688]{2,1,0:T(8,128)(2,1)}, u32[]{:S(2)}, u32[]{:S(2)}) async-start(bf16[8,112,2688]{2,1,0:T(8,128)(2,1)} %copy.178), calls=%async_computation.1 | async-start | bytes 9633792 | tf_op jit(solution)/shard_map/all_to_all | solution.py:146
  131.0 87.7 %copy-start.117 = (bf16[3,8]{1,0:T(4,128)(2,1)S(1)}, bf16[3,8]{1,0:T(4,128)(2,1)}, u32[]{:S(2)}) copy-start(bf16[3,8]{1,0:T(4,128)(2,1)} %param.34) | copy-start | bytes 148
  131.0 195.1 %copy-start.118 = (bf16[3,8]{1,0:T(4,128)(2,1)S(1)}, bf16[3,8]{1,0:T(4,128)(2,1)}, u32[]{:S(2)}) copy-start(bf16[3,8]{1,0:T(4,128)(2,1)} %param.37) | copy-start | bytes 148
  131.0 204.6 %copy-start.69 = (bf16[192,96]{1,0:T(8,128)(2,1)S(1)}, bf16[192,96]{1,0:T(8,128)(2,1)}, u32[]{:S(2)}) copy-start(bf16[192,96]{1,0:T(8,128)(2,1)} %param.38) | copy-start | bytes 110596
  131.0 206.0 %copy-start.119 = (s32[2,8]{1,0:T(2,128)S(1)}, s32[2,8]{1,0:T(2,128)}, u32[]{:S(2)}) copy-start(s32[2,8]{1,0:T(2,128)} %param.31) | copy-start | bytes 196
  131.0 207.9 %copy-start.66 = (bf16[96,192]{1,0:T(8,128)(2,1)S(1)}, bf16[96,192]{1,0:T(8,128)(2,1)}, u32[]{:S(2)}) copy-start(bf16[96,192]{1,0:T(8,128)(2,1)} %param.33) | copy-start | bytes 110596
  131.0 233.4 %copy-start.67 = (bf16[96,192]{1,0:T(8,128)(2,1)S(1)}, bf16[96,192]{1,0:T(8,128)(2,1)}, u32[]{:S(2)}) copy-start(bf16[96,192]{1,0:T(8,128)(2,1)} %param.35) | copy-start | bytes 110596
  131.0 258.3 %copy-start.68 = (bf16[96,192]{1,0:T(8,128)(2,1)S(1)}, bf16[96,192]{1,0:T(8,128)(2,1)}, u32[]{:S(2)}) copy-start(bf16[96,192]{1,0:T(8,128)(2,1)} %param.36) | copy-start | bytes 110596
  208.4 266.4 %all-to-all-start.4 = ((bf16[8,112,2688]{2,1,0:T(8,128)(2,1)}), bf16[8,112,2688]{2,1,0:T(8,128)(2,1)}, u32[]{:S(2)}, u32[]{:S(2)}) async-start(bf16[8,112,2688]{2,1,0:T(8,128)(2,1)} %copy.184), calls=%async_computation.4 | async-start | bytes 9633792 | tf_op jit(solution)/shard_map/all_to_all | solution.py:146
  214.9 457.6 %all-reduce.14.cloned.1.call-start = ((), (), s32[]{:S(2)}) async-start(), calls=%async_computation.31 | async-start | bytes 11010048 | tf_op jit(solution)/shard_map/psum | solution.py:185
  338.2 175.3 %copy-start.107 = (pred[896]{0:T(1024)(128)(4,1)}, pred[896]{0:T(1024)(128)(4,1)S(1)}, u32[]{:S(2)}) copy-start(pred[896]{0:T(1024)(128)(4,1)S(1)} %iota_compare_fusion.1) | copy-start | bytes 2692
  338.9 187.1 %copy-start.105 = (pred[896]{0:T(1024)(128)(4,1)}, pred[896]{0:T(1024)(128)(4,1)S(1)}, u32[]{:S(2)}) copy-start(pred[896]{0:T(1024)(128)(4,1)S(1)} %iota_compare_fusion) | copy-start | bytes 2692
  364.4 78.0 %copy-start.21 = (bf16[768,192]{1,0:T(8,128)(2,1)}, bf16[768,192]{1,0:T(8,128)(2,1)S(1)}, u32[]{:S(2)}) copy-start(bf16[768,192]{1,0:T(8,128)(2,1)S(1)} %all_gather.33) | copy-start | bytes 884740
  389.3 51.2 %copy-start.19 = (bf16[768,192]{1,0:T(8,128)(2,1)}, bf16[768,192]{1,0:T(8,128)(2,1)S(1)}, u32[]{:S(2)}) copy-start(bf16[768,192]{1,0:T(8,128)(2,1)S(1)} %all_gather.32) | copy-start | bytes 884740
  414.3 30.9 %copy-start.23 = (bf16[768,192]{1,0:T(8,128)(2,1)}, bf16[768,192]{1,0:T(8,128)(2,1)S(1)}, u32[]{:S(2)}) copy-start(bf16[768,192]{1,0:T(8,128)(2,1)S(1)} %all_gather.30) | copy-start | bytes 884740
  441.1 77.7 %copy-start.38 = (bf16[896,192]{0,1:T(8,128)(2,1)}, bf16[896,192]{0,1:T(8,128)(2,1)S(1)}, u32[]{:S(2)}) copy-start(bf16[896,192]{0,1:T(8,128)(2,1)S(1)} %convolution_convert_fusion.6) | copy-start | bytes 1032196
  531.7 146.8 %all-gather.6.cloned.1.call-start = ((), (), s32[]{:S(2)}) async-start(), calls=%async_computation.27 | async-start | bytes 1327104 | tf_op jit(solution)/shard_map/all_gather | solution.py:103
  532.3 175.2 %all-to-all-start.8 = ((bf16[8,112,768]{2,1,0:T(8,128)(2,1)}), bf16[8,112,768]{2,1,0:T(8,128)(2,1)}, u32[]{:S(2)}, u32[]{:S(2)}) async-start(bf16[8,112,768]{2,1,0:T(8,128)(2,1)} %get-tuple-element.219), calls=%async_computation.8 | async-start | bytes 2752512 | tf_op jit(solution)/shard_map/all_to_all | solution.py:147
  543.4 155.5 %all-gather.8.cloned.1.call-start = ((), (), s32[]{:S(2)}) async-start(), calls=%async_computation.28 | async-start | bytes 1327104 | tf_op jit(solution)/shard_map/all_gather | solution.py:104
  543.9 223.8 %all-reduce.18.cloned.1.call-start = ((), (), s32[]{:S(2)}) async-start(), calls=%async_computation.33 | async-start | bytes 5505024 | tf_op jit(solution)/shard_map/psum | solution.py:197
  676.5 200.0 %copy-start.63 = (f32[896]{0:T(1024)}, f32[896]{0:T(1024)S(1)}, u32[]{:S(2)}) copy-start(f32[896]{0:T(1024)S(1)} %fusion.78) | copy-start | bytes 10756
  707.5 69.1 %all-to-all-start.6 = ((bf16[8,112,768]{2,1,0:T(8,128)(2,1)}), bf16[8,112,768]{2,1,0:T(8,128)(2,1)}, u32[]{:S(2)}, u32[]{:S(2)}) async-start(bf16[8,112,768]{2,1,0:T(8,128)(2,1)} %get-tuple-element.217), calls=%async_computation.6 | async-start | bytes 2752512 | tf_op jit(solution)/shard_map/all_to_all | solution.py:147
  713.0 154.9 %all-reduce.16.cloned.1.call-start = ((), (), s32[]{:S(2)}) async-start(), calls=%async_computation.32 | async-start | bytes 5505024 | tf_op jit(solution)/shard_map/psum | solution.py:239
  729.0 38.8 %copy-start.87 = (f32[768]{0:T(1024)S(1)}, f32[768]{0:T(1024)}, u32[]{:S(2)}) copy-start(f32[768]{0:T(1024)} %convert_element_type.455) | copy-start | bytes 9220
  810.6 130.1 %all-to-all-start.24 = ((bf16[8,1,96]{2,1,0:T(2,128)(2,1)}), bf16[8,1,96]{2,1,0:T(2,128)(2,1)}, u32[]{:S(2)}, u32[]{:S(2)}) async-start(bf16[8,1,96]{2,1,0:T(2,128)(2,1)} %convert_element_type.579), calls=%async_computation.24 | async-start | bytes 8192 | tf_op jit(solution)/shard_map/all_to_all | solution.py:19
  896.5 16.3 %copy-start.102 = (f32[896,3]{0,1:T(4,128)S(1)}, f32[896,3]{0,1:T(4,128)}, u32[]{:S(2)}) copy-start(f32[896,3]{0,1:T(4,128)} %log_add_fusion) | copy-start | bytes 32260
  896.5 16.3 %copy-start.106 = (pred[896]{0:T(1024)(128)(4,1)S(1)}, pred[896]{0:T(1024)(128)(4,1)}, u32[]{:S(2)}) copy-start(pred[896]{0:T(1024)(128)(4,1)} %copy-done.105) | copy-start | bytes 2692
  920.0 15.9 %copy-start.40 = (bf16[896,192]{0,1:T(8,128)(2,1)S(1)}, bf16[896,192]{0,1:T(8,128)(2,1)}, u32[]{:S(2)}) copy-start(bf16[896,192]{0,1:T(8,128)(2,1)} %convolution_convert_fusion.7) | copy-start | bytes 1032196
  939.8 70.8 %copy-start.32 = (bf16[896,3,64]{0,2,1:T(8,128)(2,1)}, bf16[896,3,64]{0,2,1:T(8,128)(2,1)S(1)}, u32[]{:S(2)}) copy-start(bf16[896,3,64]{0,2,1:T(8,128)(2,1)S(1)} %get-tuple-element.191) | copy-start | bytes 1032196
  940.7 70.4 %copy-start.30 = (bf16[896,3,64]{0,2,1:T(8,128)(2,1)}, bf16[896,3,64]{0,2,1:T(8,128)(2,1)S(1)}, u32[]{:S(2)}) copy-start(bf16[896,3,64]{0,2,1:T(8,128)(2,1)S(1)} %get-tuple-element.189) | copy-start | bytes 1032196
  940.7 31.5 %copy-start.92 = (f32[768]{0:T(1024)S(1)}, f32[768]{0:T(1024)}, u32[]{:S(2)}) copy-start(f32[768]{0:T(1024)} %get-tuple-element.201) | copy-start | bytes 9220
  940.7 8.9 all-to-all-start.20
  949.7 55.4 %copy-start.80 = (bf16[8,3,32]{2,1,0:T(4,128)(2,1)}, bf16[8,3,32]{2,1,0:T(4,128)(2,1)S(1)}, u32[]{:S(2)}) copy-start(bf16[8,3,32]{2,1,0:T(4,128)(2,1)S(1)} %all-to-all-done.20) | copy-start | bytes 4612
  949.7 8.6 all-to-all-start.23
  958.3 8.7 all-to-all-start.15
  966.9 38.1 %copy-start.82 = (bf16[8,3,8]{2,1,0:T(4,128)(2,1)}, bf16[8,3,8]{2,1,0:T(4,128)(2,1)S(1)}, u32[]{:S(2)}) copy-start(bf16[8,3,8]{2,1,0:T(4,128)(2,1)S(1)} %all-to-all-done.15) | copy-start | bytes 1156
  966.9 8.7 all-to-all-start.13
  975.6 29.5 %copy-start.84 = (bf16[8,3,8]{2,1,0:T(4,128)(2,1)}, bf16[8,3,8]{2,1,0:T(4,128)(2,1)S(1)}, u32[]{:S(2)}) copy-start(bf16[8,3,8]{2,1,0:T(4,128)(2,1)S(1)} %all-to-all-done.13) | copy-start | bytes 1156
  975.6 8.5 all-to-all-start.22
  984.1 21.0 %copy-start.96 = (bf16[8,1,96]{2,1,0:T(2,128)(2,1)}, bf16[8,1,96]{2,1,0:T(2,128)(2,1)S(1)}, u32[]{:S(2)}) copy-start(bf16[8,1,96]{2,1,0:T(2,128)(2,1)S(1)} %all-to-all-done.22) | copy-start | bytes 4612
  984.1 8.5 all-to-all-start.18
  992.6 12.4 all-to-all-start.17
  1005.1 12.1 all-to-all-start.16
  1017.2 12.0 all-to-all-start.12
  1029.1 23.8 %all-to-all-start.21 = ((bf16[8,768,96]{1,2,0:T(8,128)(2,1)}), bf16[8,768,96]{1,2,0:T(8,128)(2,1)}, u32[]{:S(2)}, u32[]{:S(2)}) async-start(bf16[8,768,96]{1,2,0:T(8,128)(2,1)} %bitcast.320), calls=%async_computation.21 | async-start | bytes 2359296 | tf_op jit(solution)/shard_map/all_to_all | solution.py:19
  1045.8 35.2 %copy-start.20 = (bf16[768,192]{1,0:T(8,128)(2,1)S(1)}, bf16[768,192]{1,0:T(8,128)(2,1)}, u32[]{:S(2)}) copy-start(bf16[768,192]{1,0:T(8,128)(2,1)} %copy-done.19) | copy-start | bytes 884740
  1045.8 35.2 %copy-start.37 = (bf16[3,64,896]{2,1,0:T(8,128)(2,1)S(1)}, bf16[3,64,896]{2,1,0:T(8,128)(2,1)}, u32[]{:S(2)}) copy-start(bf16[3,64,896]{2,1,0:T(8,128)(2,1)} %copy-done.36) | copy-start | bytes 1032196
  1075.4 27.5 %all-to-all-start.2 = ((bf16[8,112,768]{2,1,0:T(8,128)(2,1)}), bf16[8,112,768]{2,1,0:T(8,128)(2,1)S(1)}, u32[]{:S(2)}, u32[]{:S(2)}) async-start(bf16[8,112,768]{2,1,0:T(8,128)(2,1)} %bitcast.291), calls=%async_computation.2 | async-start | bytes 2752512 | tf_op jit(solution)/shard_map/all_to_all | solution.py:304
  1081.0 63.6 %reduce-scatter.7.cloned.1.call-start = ((), (), s32[]{:S(2)}) async-start(), calls=%async_computation.29 | async-start | bytes 1720320
  1104.0 33.8 %all-to-all-start.5 = ((bf16[8,112,768]{2,1,0:T(8,128)(2,1)}), bf16[8,112,768]{2,1,0:T(8,128)(2,1)}, u32[]{:S(2)}, u32[]{:S(2)}) async-start(bf16[8,112,768]{2,1,0:T(8,128)(2,1)} %bitcast.290), calls=%async_computation.5 | async-start | bytes 2752512 | tf_op jit(solution)/shard_map/all_to_all | solution.py:304
  1111.6 71.4 %reduce-scatter.9.cloned.1.call-start = ((), (), s32[]{:S(2)}) async-start(), calls=%async_computation.30 | async-start | bytes 1720320
  1137.8 37.0 %all-to-all-start.19 = ((bf16[8,96,769]{2,1,0:T(8,128)(2,1)}), bf16[8,96,769]{2,1,0:T(8,128)(2,1)S(1)}, u32[]{:S(2)}, u32[]{:S(2)}) async-start(bf16[8,96,769]{2,1,0:T(8,128)(2,1)} %pad_maximum_fusion.3), calls=%async_computation.19 | async-start | bytes 2752512 | tf_op jit(solution)/shard_map/all_to_all | solution.py:19
  1174.8 19.0 %all-to-all-start.7 = ((bf16[8,112,192]{1,2,0:T(8,128)(2,1)}), bf16[8,112,192]{1,2,0:T(8,128)(2,1)S(1)}, u32[]{:S(2)}, u32[]{:S(2)}) async-start(bf16[8,112,192]{1,2,0:T(8,128)(2,1)} %copy.192), calls=%async_computation.7 | async-start | bytes 786432 | tf_op jit(solution)/shard_map/all_to_all | solution.py:311
  1193.8 16.9 %copy-start.46 = (bf16[8,112,192]{1,2,0:T(8,128)(2,1)}, bf16[8,112,192]{1,2,0:T(8,128)(2,1)S(1)}, u32[]{:S(2)}) copy-start(bf16[8,112,192]{1,2,0:T(8,128)(2,1)S(1)} %all-to-all-done.7) | copy-start | bytes 1032196
  1193.8 25.0 %all-to-all-start.9 = ((bf16[8,112,192]{1,2,0:T(8,128)(2,1)}), bf16[8,112,192]{1,2,0:T(8,128)(2,1)S(1)}, u32[]{:S(2)}, u32[]{:S(2)}) async-start(bf16[8,112,192]{1,2,0:T(8,128)(2,1)} %copy.198), calls=%async_computation.9 | async-start | bytes 786432 | tf_op jit(solution)/shard_map/all_to_all | solution.py:311
  1219.6 106.5 %all-to-all-start.10 = ((bf16[8,112,2688]{2,1,0:T(8,128)(2,1)}), bf16[8,112,2688]{2,1,0:T(8,128)(2,1)}, u32[]{:S(2)}, u32[]{:S(2)}) async-start(bf16[8,112,2688]{2,1,0:T(8,128)(2,1)} %copy.199), calls=%async_computation.10 | async-start | bytes 9633792 | tf_op jit(solution)/shard_map/all_to_all | solution.py:318
  1244.1 88.7 %copy-start.110 = (s32[2,8]{1,0:T(2,128)S(1)}, s32[2,8]{1,0:T(2,128)}, u32[]{:S(2)}) copy-start(s32[2,8]{1,0:T(2,128)} %param.32) | copy-start | bytes 196
  1326.1 110.6 %all-to-all-start.11 = ((bf16[8,112,2688]{2,1,0:T(8,128)(2,1)}), bf16[8,112,2688]{2,1,0:T(8,128)(2,1)}, u32[]{:S(2)}, u32[]{:S(2)}) async-start(bf16[8,112,2688]{2,1,0:T(8,128)(2,1)} %copy.201), calls=%async_computation.11 | async-start | bytes 9633792 | tf_op jit(solution)/shard_map/all_to_all | solution.py:318
  1342.7 15.7 %copy-start.97 = (bf16[8,1,96]{2,1,0:T(2,128)(2,1)S(1)}, bf16[8,1,96]{2,1,0:T(2,128)(2,1)}, u32[]{:S(2)}) copy-start(bf16[8,1,96]{2,1,0:T(2,128)(2,1)} %copy-done.96) | copy-start | bytes 4612
  1342.7 16.2 %copy-start.99 = (bf16[8,1,96]{2,1,0:T(2,128)(2,1)S(1)}, bf16[8,1,96]{2,1,0:T(2,128)(2,1)}, u32[]{:S(2)}) copy-start(bf16[8,1,96]{2,1,0:T(2,128)(2,1)} %copy-done.98) | copy-start | bytes 4612
  1342.7 16.8 %copy-start.101 = (bf16[8,1,96]{2,1,0:T(2,128)(2,1)S(1)}, bf16[8,1,96]{2,1,0:T(2,128)(2,1)}, u32[]{:S(2)}) copy-start(bf16[8,1,96]{2,1,0:T(2,128)(2,1)} %copy-done.100) | copy-start | bytes 4612
  1342.7 17.3 %copy-start.51 = (bf16[8,96,192]{1,2,0:T(8,128)(2,1)S(1)}, bf16[8,96,192]{1,2,0:T(8,128)(2,1)}, u32[]{:S(2)}) copy-start(bf16[8,96,192]{1,2,0:T(8,128)(2,1)} %copy-done.50) | copy-start | bytes 884740
  (109 other events, 598.8 us)
Sparse Core Ops, SparseCore 0:
  531.7 140.7 all-reduce.13
  705.6 62.0 all-reduce.17
  805.6 62.1 all-reduce.15
  1084.6 52.3 reduce-scatter.6
  1140.0 42.9 reduce-scatter.8
Sparse Core Ops, SparseCore 1:
  534.3 77.4 all-gather.5
  613.9 39.7 all-gather.7
where the time goes:
time: 1510 us; the launch traced here: 1490 us
  waiting for transfers between devices  472 us (31%)
  blocking collectives  285 us (19%)
  local copies, waits for them, and re-layouts  280 us (19%)
  matrix products  154 us (10%)
  starting transfers between devices  145 us (10%)
  other arithmetic  129 us (9%)
  between operations  21.7 us (1%)
    all_to_all x2, waiting for transfers between devices, on_device(): lax.all_to_all(scores_low.reshape(seq_count, piece_rows, heads_here * ext...  123 us
    all_gather x1, blocking collectives, on_device(): lax.all_gather(b_query, 'seq', axis=1, tiled=True)  107 us
    psum x1, waiting for transfers between devices, on_device(): branch = lax.psum(out_part, 'head') + bias_out.astype(jnp.float32)  78.4 us
    all_to_all x2, waiting for transfers between devices, on_device(): lax.all_to_all(send_prev, 'seq', split_axis=0, concat_axis=1, tiled=True)  77.4 us
    all_to_all x12, starting transfers between devices, sum_at_owner(): lax.all_to_all(blocks, axis, split_axis=0, concat_axis=0, tiled=True)  66.5 us
    unnamed x305, local copies, waits for them, and re-layouts  61 us
    convert_element_type x4, local copies, waits for them, and re-layouts, on_device(): prev_rows = got_prev.reshape(extent, heads_here, extent).astype(jnp.float32)  56.5 us
    all_to_all x12, waiting for transfers between devices, sum_at_owner(): lax.all_to_all(blocks, axis, split_axis=0, concat_axis=0, tiled=True)  51.1 us
  transfers between devices with their start and end apart: 31, of which 21 were waited for; matrix products, arithmetic and copies ran while one was open for 28% of the time, Pallas kernels for 0%

commit v1 on v0

--- a/solution.py
+++ b/solution.py
@@ -1,9 +1,15 @@
+import functools
+
 import jax
 import jax.numpy as jnp
 from jax import lax
+from jax.experimental import pallas as pl
+from jax.experimental.pallas import tpu as pltpu
 from jax.sharding import PartitionSpec as P
 
 HEAD_DIM = 64
+BF16, F32 = jnp.bfloat16, jnp.float32
+VMEM_LIMIT = 60 * 1024 * 1024
 
 
 epsilon = 1e-12
@@ -55,7 +61,7 @@
     return jnp.where(key_valid[None, None, :], raw_scores, -jnp.inf)
 
 
-def on_device(
+def on_device_general(
     tokens,
     prev_logits,
     lengths,
@@ -396,6 +402,692 @@
         final_grads[14],
     )
 
+def cost(flops, moved):
+    return pl.CostEstimate(flops=int(flops), bytes_accessed=int(moved), transcendentals=0)
+
+
+def params(**more):
+    return pltpu.CompilerParams(vmem_limit_bytes=VMEM_LIMIT, **more)
+
+
+def dot(a, b, ca, cb):
+    return lax.dot_general(a, b, (((ca,), (cb,)), ((), ())), preferred_element_type=F32)
+
+
+def whole(x):
+    return pl.BlockSpec(x.shape, lambda *_: (0,) * len(x.shape))
+
+
+def pick_kernel(index_ref, x_ref, o_ref):
+    o_ref[0] = x_ref[0, 0]
+
+
+def pick_blocks(stacked, micro, index):
+    _, count, heads, rows, extent = stacked.shape
+    block = (heads, rows, extent)
+    return pl.pallas_call(
+        pick_kernel,
+        out_shape=jax.ShapeDtypeStruct((count, *block), stacked.dtype),
+        grid_spec=pltpu.PrefetchScalarGridSpec(
+            num_scalar_prefetch=1,
+            grid=(count,),
+            in_specs=[pl.BlockSpec((1, 1, *block), lambda i, ix: (micro, ix[i], 0, 0, 0))],
+            out_specs=pl.BlockSpec((1, *block), lambda i, ix: (i, 0, 0, 0)),
+        ),
+        compiler_params=params(),
+        cost_estimate=cost(0, 4 * count * heads * rows * extent),
+        name="pick_blocks",
+    )(index, stacked)
+
+
+def place_kernel(index_ref, x_ref, *rest):
+    rest[-1][0, 0] = x_ref[0]
+
+
+def place_blocks(blocks, micro, micros, index, into):
+    count, heads, rows, extent = blocks.shape
+    block = (heads, rows, extent)
+    others = [] if into is None else [into]
+    return pl.pallas_call(
+        place_kernel,
+        out_shape=jax.ShapeDtypeStruct((micros, count, *block), blocks.dtype),
+        grid_spec=pltpu.PrefetchScalarGridSpec(
+            num_scalar_prefetch=1,
+            grid=(count,),
+            in_specs=[pl.BlockSpec((1, *block), lambda i, ix: (ix[i], 0, 0, 0))]
+            + [pl.BlockSpec(memory_space=pl.ANY) for _ in others],
+            out_specs=pl.BlockSpec((1, 1, *block), lambda i, ix: (micro, i, 0, 0, 0)),
+        ),
+        input_output_aliases={2: 0} if others else {},
+        compiler_params=params(),
+        cost_estimate=cost(0, 4 * count * heads * rows * extent),
+        name="place_blocks",
+    )(index, blocks, *others)
+
+
+def project_kernel(x_ref, w_ref, b_ref, o_ref):
+    columns = o_ref.shape[2]
+    o_ref[0] = (dot(x_ref[...], w_ref[0, :, :columns], 1, 0) + b_ref[0]).astype(BF16)
+
+
+def project(x, weights, bias):
+    rows, width = x.shape
+    groups, _, columns = bias.shape
+    return pl.pallas_call(
+        project_kernel,
+        out_shape=jax.ShapeDtypeStruct((groups, rows, columns), BF16),
+        grid=(groups,),
+        in_specs=[
+            whole(x),
+            pl.BlockSpec((1, width, width), lambda h: (h, 0, 0)),
+            pl.BlockSpec((1, 1, columns), lambda h: (h, 0, 0)),
+        ],
+        out_specs=pl.BlockSpec((1, rows, columns), lambda h: (h, 0, 0)),
+        compiler_params=params(),
+        cost_estimate=cost(2 * groups * rows * width * columns, 2 * groups * columns * (width + rows)),
+        name="project",
+    )(x, weights, bias)
+
+
+def head_mask(shape, head):
+    lane = lax.broadcasted_iota(jnp.int32, shape, len(shape) - 1)
+    return lane // HEAD_DIM == head
+
+
+def gather_rows(info_ref, qkv_ref, groups, rows, width, q_scr, k_scr, v_scr):
+    for g in range(groups):
+        block = qkv_ref[(info_ref[1] + g) % groups, 0]
+        q_scr[g * rows : (g + 1) * rows] = block[:, :width]
+        k_scr[g * rows : (g + 1) * rows] = block[:, width : 2 * width]
+        v_scr[g * rows : (g + 1) * rows] = block[:, 2 * width :]
+
+
+def forward_kernel(heads, info_ref, qkv_ref, prev_ref, *rest):
+    logit_ref, attend_ref, context_ref, q_scr, k_scr, v_scr = rest[-6:]
+    step = pl.program_id(0)
+    groups, _, rows, columns = qkv_ref.shape
+    piece, extent = prev_ref.shape[2:]
+    width = columns // 3
+
+    @pl.when(step == 0)
+    def _():
+        gather_rows(info_ref, qkv_ref, groups, rows, width, q_scr, k_scr, v_scr)
+
+    q = q_scr[pl.ds(pl.multiple_of(step * piece, 16), piece), :]
+    key_valid = lax.broadcasted_iota(jnp.int32, (1, extent), 1) < info_ref[0]
+    total = jnp.zeros((piece, width), F32)
+    for h in range(heads):
+        mine = head_mask((1, width), h)
+        q_head = jnp.where(mine, q, jnp.zeros_like(q))
+        raw = dot(q_head, k_scr[...], 1, 1) * HEAD_DIM ** (-0.5) + prev_ref[0, h].astype(F32)
+        logit_ref[0, h] = raw.astype(BF16)
+        masked = jnp.where(key_valid, raw, -jnp.inf)
+        top = jnp.max(masked, axis=-1, keepdims=True)
+        grown = jnp.exp(masked - top)
+        attend = grown * (1.0 / jnp.sum(grown, axis=-1, keepdims=True))
+        low = attend.astype(BF16)
+        attend_ref[0, h] = low
+        total = total + jnp.where(mine, dot(low, v_scr[...], 1, 0), 0.0)
+    context_ref[0] = total.astype(BF16)
+
+
+def attention_forward(info, qkv, prev, micro, micros, logits_into):
+    groups, _, rows, columns = qkv.shape
+    pieces, heads, piece, extent = prev.shape
+    width = columns // 3
+    per = rows // piece
+    others = [] if logits_into is None else [logits_into]
+    return pl.pallas_call(
+        functools.partial(forward_kernel, heads),
+        out_shape=(
+            jax.ShapeDtypeStruct((micros, heads, extent, extent), BF16),
+            jax.ShapeDtypeStruct(prev.shape, BF16),
+            jax.ShapeDtypeStruct((groups, rows, width), BF16),
+        ),
+        grid_spec=pltpu.PrefetchScalarGridSpec(
+            num_scalar_prefetch=1,
+            grid=(pieces,),
+            in_specs=[
+                pl.BlockSpec((groups, 1, rows, columns), lambda j, i: (0, micro, 0, 0)),
+                pl.BlockSpec((1, heads, piece, extent), lambda j, i: (j, 0, 0, 0)),
+            ]
+            + [pl.BlockSpec(memory_space=pl.ANY) for _ in others],
+            out_specs=(
+                pl.BlockSpec((1, heads, piece, extent), lambda j, i: (micro, 0, j, 0)),
+                pl.BlockSpec((1, heads, piece, extent), lambda j, i: (j, 0, 0, 0)),
+                pl.BlockSpec((1, piece, width), lambda j, i: ((j // per + i[1]) % groups, j % per, 0)),
+            ),
+            scratch_shapes=[pltpu.VMEM((extent, width), BF16)] * 3,
+        ),
+        input_output_aliases={3: 0} if others else {},
+        compiler_params=params(),
+        cost_estimate=cost(4 * heads * extent * extent * HEAD_DIM * 4, 6 * heads * extent * extent),
+        name="attention_forward",
+    )(info, qkv, prev, *others)
+
+
+def backward_kernel(
+    heads, info_ref, qkv_ref, attend_ref, context_ref, dcon_ref, cot_ref,
+    send_ref, dqkv_ref, sums_ref, q_scr, k_scr, v_scr, dq_scr, dk_scr, dv_scr,
+):
+    step = pl.program_id(0)
+    groups, _, rows, columns = qkv_ref.shape
+    piece, extent = attend_ref.shape[2:]
+    width = columns // 3
+    scale = HEAD_DIM ** (-0.5)
+
+    @pl.when(step == 0)
+    def _():
+        gather_rows(info_ref, qkv_ref, groups, rows, width, q_scr, k_scr, v_scr)
+        dk_scr[...] = jnp.zeros_like(dk_scr)
+        dv_scr[...] = jnp.zeros_like(dv_scr)
+
+    here = pl.ds(pl.multiple_of(step * piece, 16), piece)
+    q = q_scr[here, :]
+    dcon = dcon_ref[0]
+    both = dcon.astype(F32) * context_ref[0].astype(F32)
+    dq = jnp.zeros((piece, width), F32)
+    for h in range(heads):
+        mine = head_mask((1, width), h)
+        dcon_head = jnp.where(mine, dcon, jnp.zeros_like(dcon))
+        q_head = jnp.where(mine, q, jnp.zeros_like(q))
+        low = attend_ref[0, h]
+        delta = jnp.sum(jnp.where(mine, both, 0.0), axis=-1, keepdims=True)
+        dprob = dot(dcon_head, v_scr[...], 1, 1)
+        dscore = low.astype(F32) * (dprob - delta) + cot_ref[0, h].astype(F32)
+        dlow = dscore.astype(BF16)
+        send_ref[0, h] = dlow
+        dq = dq + jnp.where(mine, dot(dlow, k_scr[...], 1, 0), 0.0)
+        dk_scr[...] += dot(dlow, q_head, 0, 0)
+        dv_scr[...] += dot(low, dcon_head, 0, 0)
+    dq_scr[here, :] = dq * scale
+
+    @pl.when(step == pl.num_programs(0) - 1)
+    def _():
+        sums_ref[0:1, :] = jnp.sum(dq_scr[...], axis=0, keepdims=True)
+        sums_ref[1:2, :] = jnp.sum(dv_scr[...], axis=0, keepdims=True)
+        for g in range(groups):
+            part = slice(g * rows, (g + 1) * rows)
+            dqkv_ref[(info_ref[1] + g) % groups] = jnp.concatenate(
+                [dq_scr[part], dk_scr[part] * scale, dv_scr[part]], axis=1
+            ).astype(BF16)
+
+
+def attention_backward(info, qkv, attend, context, dcontext, cot, micro):
+    groups, _, rows, columns = qkv.shape
+    pieces, heads, piece, extent = attend.shape
+    width = columns // 3
+    per = rows // piece
+    rotated = pl.BlockSpec((1, piece, width), lambda j, i: ((j // per + i[1]) % groups, j % per, 0))
+    square = pl.BlockSpec((1, heads, piece, extent), lambda j, i: (j, 0, 0, 0))
+    return pl.pallas_call(
+        functools.partial(backward_kernel, heads),
+        out_shape=(
+            jax.ShapeDtypeStruct(attend.shape, BF16),
+            jax.ShapeDtypeStruct((groups, rows, columns), BF16),
+            jax.ShapeDtypeStruct((2, width), F32),
+        ),
+        grid_spec=pltpu.PrefetchScalarGridSpec(
+            num_scalar_prefetch=1,
+            grid=(pieces,),
+            in_specs=[
+                pl.BlockSpec((groups, 1, rows, columns), lambda j, i: (0, micro, 0, 0)),
+                square,
+                rotated,
+                rotated,
+                pl.BlockSpec((1, heads, piece, extent), lambda j, i: (micro, 0, j, 0)),
+            ],
+            out_specs=(
+                square,
+                pl.BlockSpec((groups, rows, columns), lambda j, i: (0, 0, 0)),
+                pl.BlockSpec((2, width), lambda j, i: (0, 0)),
+            ),
+            scratch_shapes=[pltpu.VMEM((extent, width), BF16)] * 3
+            + [pltpu.VMEM((extent, width), F32)] * 3,
+        ),
+        compiler_params=params(),
+        cost_estimate=cost(8 * heads * extent * extent * HEAD_DIM * 4, 6 * heads * extent * extent),
+        name="attention_backward",
+    )(info, qkv, attend, context, dcontext, cot)
+
+
+def normal(values):
+    center = values - jnp.mean(values, axis=-1, keepdims=True)
+    spread = jnp.mean(center * center, axis=-1, keepdims=True)
+    inverse = lax.rsqrt(spread + epsilon)
+    return center * inverse, inverse
+
+
+def normal_back(grad, gain, unit, inverse):
+    scaled = grad * gain
+    return inverse * (
+        scaled
+        - jnp.mean(scaled, axis=-1, keepdims=True)
+        - unit * jnp.mean(scaled * unit, axis=-1, keepdims=True)
+    )
+
+
+def rows_kernel(
+    cuts, con_ref, x_ref, cot_ref, w_ref, bup_ref, vec_ref,
+    y_ref, dz_ref, dcon_ref, h1_ref, act_ref, b1_ref, b2_ref, b0_ref, sums_ref, dbup_ref,
+    slope, acc, hidden, unit_scr, inv_scr,
+):
+    groups, rows, width = con_ref.shape
+    qkv_end, out_end, up_end, down_end = cuts
+    b_out, gain_one, shift_one = vec_ref[0:1, :], vec_ref[1:2, :], vec_ref[2:3, :]
+    b_down, gain_two, shift_two = vec_ref[3:4, :], vec_ref[4:5, :], vec_ref[5:6, :]
+
+    branch = b_out + x_ref[...].astype(F32)
+    for h in range(groups):
+        branch = branch + dot(con_ref[h], w_ref[h, :, qkv_end:out_end], 1, 1)
+    unit_one, inverse_one = normal(branch)
+    unit_scr[...] = unit_one
+    inv_scr[...] = inverse_one
+    hid = unit_one * gain_one + shift_one
+    hidden[...] = hid
+    h1_ref[...] = hid.astype(BF16)
+    acc[...] = hid + b_down
+
+    def up(h, carry):
+        u = dot(h1_ref[...], w_ref[h, :, out_end:up_end], 1, 0) + bup_ref[h]
+        half = 0.5 * (1.0 + lax.erf(u * 0.7071067811865476))
+        act_ref[h] = (u * half).astype(BF16)
+        slope[h] = half + u * (jnp.exp(u * u * -0.5) * 0.3989422804014327)
+        acc[...] += dot(act_ref[h], w_ref[h, :, up_end:down_end], 1, 1)
+        return carry
+
+    lax.fori_loop(0, groups, up, 0)
+    unit_two, inverse_two = normal(acc[...])
+    y_ref[...] = (unit_two * gain_two + shift_two).astype(BF16)
+    cot = cot_ref[...].astype(F32)
+    sums_ref[4:5, :] = jnp.sum(cot * unit_two, axis=0, keepdims=True)
+    sums_ref[5:6, :] = jnp.sum(cot, axis=0, keepdims=True)
+    dz_two = normal_back(cot, gain_two, unit_two, inverse_two)
+    sums_ref[3:4, :] = jnp.sum(dz_two, axis=0, keepdims=True)
+    b2_ref[...] = dz_two.astype(BF16)
+    acc[...] = dz_two
+
+    def down(h, carry):
+        du = dot(b2_ref[...], w_ref[h, :, up_end:down_end], 1, 0) * slope[h]
+        dbup_ref[h] = jnp.sum(du, axis=0, keepdims=True)
+        b1_ref[h] = du.astype(BF16)
+        acc[...] += dot(b1_ref[h], w_ref[h, :, out_end:up_end], 1, 1)
+        return carry
+
+    lax.fori_loop(0, groups, down, 0)
+    dh = acc[...]
+    unit_one = unit_scr[...]
+    sums_ref[1:2, :] = jnp.sum(dh * unit_one, axis=0, keepdims=True)
+    sums_ref[2:3, :] = jnp.sum(dh, axis=0, keepdims=True)
+    dz_one = normal_back(dh, gain_one, unit_one, inv_scr[...])
+    sums_ref[0:1, :] = jnp.sum(dz_one, axis=0, keepdims=True)
+    sums_ref[6:8, :] = jnp.zeros_like(sums_ref[6:8, :])
+    dz_ref[...] = dz_one
+    b0_ref[...] = dz_one.astype(BF16)
+    for h in range(groups):
+        dcon_ref[h] = dot(b0_ref[...], w_ref[h, :, qkv_end:out_end], 1, 0).astype(BF16)
+
+
+def row_work(cuts, context, x, cot, weights, bias_up, vectors):
+    groups, rows, width = context.shape
+    model = x.shape[1]
+    unit = bias_up.shape[2]
+    shape = jax.ShapeDtypeStruct
+    args = (context, x, cot, weights, bias_up, vectors)
+    return pl.pallas_call(
+        functools.partial(rows_kernel, cuts),
+        out_shape=(
+            shape((rows, model), BF16),
+            shape((rows, model), F32),
+            shape(context.shape, BF16),
+            shape((rows, model), BF16),
+            shape((groups, rows, unit), BF16),
+            shape((groups, rows, unit), BF16),
+            shape((rows, model), BF16),
+            shape((rows, model), BF16),
+            shape((8, model), F32),
+            shape((groups, 1, unit), F32),
+        ),
+        in_specs=[pl.BlockSpec(memory_space=pltpu.VMEM)] * len(args),
+        out_specs=(pl.BlockSpec(memory_space=pltpu.VMEM),) * 10,
+        scratch_shapes=[
+            pltpu.VMEM((groups, rows, unit), F32),
+            pltpu.VMEM((rows, model), F32),
+            pltpu.VMEM((rows, model), F32),
+            pltpu.VMEM((rows, model), F32),
+            pltpu.VMEM((rows, 1), F32),
+        ],
+        compiler_params=params(),
+        cost_estimate=cost(8 * groups * rows * model * (unit + width), 2 * weights.size),
+        name="row_work",
+    )(*args)
+
+
+def input_kernel(dqkv_ref, w_ref, dz_ref, o_ref):
+    total = dz_ref[...]
+    for h in range(dqkv_ref.shape[0]):
+        total = total + dot(dqkv_ref[h], w_ref[h, :, : dqkv_ref.shape[2]], 1, 1)
+    o_ref[...] = total.astype(BF16)
+
+
+def input_grad(dqkv, weights, dz):
+    groups, rows, columns = dqkv.shape
+    model = dz.shape[1]
+    return pl.pallas_call(
+        input_kernel,
+        out_shape=jax.ShapeDtypeStruct((rows, model), BF16),
+        grid=(1,),
+        in_specs=[
+            whole(dqkv),
+            pl.BlockSpec((groups, model, model), lambda i: (0, 0, 0)),
+            whole(dz),
+        ],
+        out_specs=pl.BlockSpec((rows, model), lambda i: (0, 0)),
+        compiler_params=params(),
+        cost_estimate=cost(2 * groups * rows * columns * model, 2 * groups * columns * model),
+        name="input_grad",
+    )(dqkv, weights, dz)
+
+
+def weight_kernel(cuts, micros, *refs):
+    out_ref = refs[-1]
+    qkv_end, out_end, up_end, down_end = cuts
+
+    def product(lefts, rights):
+        total = None
+        for left, right in zip(lefts, rights):
+            term = dot(left[...], right[0], 0, 0)
+            total = term if total is None else total + term
+        return total.astype(BF16)
+
+    x, b0, h1, b2, dqkv, con, b1, act = (refs[i * micros : (i + 1) * micros] for i in range(8))
+    out_ref[0, :, 0:qkv_end] = product(x, dqkv)
+    out_ref[0, :, qkv_end:out_end] = product(b0, con)
+    out_ref[0, :, out_end:up_end] = product(h1, b1)
+    out_ref[0, :, up_end:down_end] = product(b2, act)
+
+
+def weight_grads(cuts, lefts, rights):
+    micros = len(lefts[0])
+    groups = rights[0][0].shape[0]
+    model = lefts[0][0].shape[1]
+    flat_left = [a for family in lefts for a in family]
+    flat_right = [a for family in rights for a in family]
+    rows = flat_left[0].shape[0]
+    return pl.pallas_call(
+        functools.partial(weight_kernel, cuts, micros),
+        out_shape=jax.ShapeDtypeStruct((groups, model, cuts[-1]), BF16),
+        grid=(groups,),
+        in_specs=[whole(a) for a in flat_left]
+        + [pl.BlockSpec((1, *a.shape[1:]), lambda h: (h, 0, 0)) for a in flat_right],
+        out_specs=pl.BlockSpec((1, model, cuts[-1]), lambda h: (h, 0, 0)),
+        compiler_params=params(),
+        cost_estimate=cost(2 * micros * groups * rows * model * cuts[-1], 2 * groups * model * cuts[-1]),
+        name="weight_grads",
+    )(*flat_left, *flat_right)
+
+
+def by_step(step, groups, slots):
+    pairs = []
+    for home in range(slots):
+        for h in range(groups):
+            slot = (h - home // 2) % groups + groups * ((home + step) % 2)
+            pairs.append((home * groups + h, slot * groups + h))
+    return pairs
+
+
+def fits(mesh):
+    return dict(mesh.shape) == {"seq": 8, "head": 4}
+
+
+def on_device(
+    tokens,
+    prev_logits,
+    lengths,
+    dealing,
+    w_query,
+    b_query,
+    w_key,
+    w_value,
+    b_value,
+    w_out,
+    b_out,
+    gain_one,
+    shift_one,
+    w_up,
+    b_up,
+    w_down,
+    b_down,
+    gain_two,
+    shift_two,
+    cot_tokens,
+    cot_logits,
+):
+    slots, groups = lax.axis_size("seq"), lax.axis_size("head")
+    grid = ("seq", "head")
+    here, head = lax.axis_index("seq"), lax.axis_index("head")
+    micros, _, piece, model = tokens.shape
+    heads = prev_logits.shape[3]
+    extent = piece * slots
+    width = heads * HEAD_DIM
+    unit = w_up.shape[1]
+    per = slots // groups
+    cuts = (3 * width, 3 * width + width, 3 * width + width + unit, 3 * width + width + 2 * unit)
+    own_rows = model // slots
+
+    inverse = [
+        jnp.sum(
+            jnp.where(
+                dealing[m][None, :] == jnp.arange(slots, dtype=jnp.int32)[:, None],
+                jnp.arange(slots, dtype=jnp.int32)[None, :],
+                0,
+            ),
+            axis=1,
+        ).astype(jnp.int32)
+        for m in range(micros)
+    ]
+    info = [
+        jnp.stack([lengths[m, inverse[m][here]], here % groups]).astype(jnp.int32)
+        for m in range(micros)
+    ]
+    prev = jnp.transpose(prev_logits, (0, 1, 3, 2, 4))
+    cot_square = jnp.transpose(cot_logits[:, 0], (0, 2, 1, 3))
+
+    vector = jnp.concatenate(
+        [
+            b_query.reshape(-1),
+            b_value.reshape(-1),
+            b_out,
+            gain_one,
+            shift_one,
+            b_up.reshape(-1),
+            b_down,
+            gain_two,
+            shift_two,
+        ]
+    )
+    lots = 8
+    vector = jnp.pad(vector, (0, lots * own_rows - vector.shape[0])).reshape(own_rows, lots)
+    packed = jnp.concatenate(
+        [
+            w_query,
+            w_key,
+            w_value,
+            w_out.T,
+            w_up,
+            w_down.T,
+            jnp.pad(vector, ((0, 0), (0, 128 - lots))),
+        ],
+        axis=1,
+    )
+    gathered = lax.all_gather(packed, grid, axis=0).reshape(slots, groups, own_rows, -1)
+    vectors = gathered[..., cuts[-1] : cuts[-1] + lots].reshape(slots, groups, -1).astype(F32)
+    weights = jnp.transpose(gathered, (1, 0, 2, 3)).reshape(groups, model, -1)
+    q_len = heads * HEAD_DIM // slots
+    offsets = [0, q_len, 2 * q_len]
+    for _ in range(7):
+        offsets.append(offsets[-1] + own_rows)
+
+    def plain(i):
+        return vectors[:, 0, offsets[i] : offsets[i + 1]].reshape(1, -1)
+
+    def by_head(i):
+        part = vectors[:, :, offsets[i] : offsets[i + 1]].reshape(slots, groups, heads, -1)
+        return jnp.transpose(part, (1, 2, 0, 3)).reshape(groups, 1, -1)
+
+    bias_query, bias_value, bias_up = by_head(0), by_head(1), by_head(5)
+    bias_qkv = jnp.concatenate([bias_query, jnp.zeros_like(bias_query), bias_value], axis=2)
+    row_vectors = jnp.concatenate(
+        [plain(2), plain(3), plain(4), plain(6), plain(7), plain(8), jnp.zeros((2, model), F32)], axis=0
+    )
+
+    def slot_of(step):
+        return (head - here // 2) % groups + groups * ((here + step) % 2)
+
+    def to_slots(array):
+        arrived = []
+        for step in range(2):
+            slot = slot_of(step)
+            out = jnp.stack(
+                [
+                    lax.dynamic_index_in_dim(array[m], inverse[m][slot], 0, keepdims=False)
+                    for m in range(micros)
+                ]
+            )
+            arrived.append(lax.ppermute(out, grid, by_step(step, groups, slots)))
+        swap = here // groups == 1
+        first = jnp.where(swap, arrived[1], arrived[0])
+        second = jnp.where(swap, arrived[0], arrived[1])
+        return jnp.concatenate([first, second], axis=1)
+
+    rows_in = to_slots(tokens)
+    cot_rows = to_slots(cot_tokens)
+
+    def across_heads(array):
+        return lax.all_to_all(array, "head", split_axis=0, concat_axis=0, tiled=True)
+
+    got_prev, after = [], None
+    for m in range(micros):
+        send = pick_blocks(prev, m, inverse[m])
+        if after is not None:
+            send, _ = lax.optimization_barrier((send, after))
+        got = lax.all_to_all(send, "seq", split_axis=0, concat_axis=0, tiled=True)
+        got_prev.append(got)
+        after = got
+
+    rows = per * piece
+    qkv = project(rows_in.reshape(micros * rows, model), weights, bias_qkv)
+    qkv = across_heads(qkv).reshape(groups, micros, rows, 3 * width)
+
+    logits, grad_logits = None, None
+    kept, sums_own, sums_rows, sums_up, returned = [], [], [], [], []
+    for m in range(micros):
+        logits, attend, context = attention_forward(info[m], qkv, got_prev[m], m, micros, logits)
+        context_rows = across_heads(context)
+        y, dz, dcon, h1, act, b1, b2, b0, sums, dbup = row_work(
+            cuts, context_rows, rows_in[m], cot_rows[m], weights, bias_up, row_vectors
+        )
+        dcontext = across_heads(dcon)
+        send, dqkv, own = attention_backward(
+            info[m], qkv, attend, context, dcontext, cot_square, m
+        )
+        got = lax.all_to_all(send, "seq", split_axis=0, concat_axis=0, tiled=True)
+        dqkv = across_heads(dqkv)
+        dx = input_grad(dqkv, weights, dz)
+        kept.append((rows_in[m], b0, h1, b2, dqkv, context_rows, b1, act))
+        sums_own.append(own)
+        sums_rows.append(sums)
+        sums_up.append(dbup)
+        returned.append((y, dx))
+        grad_logits = place_blocks(got, m, micros, dealing[m], grad_logits)
+
+    families = list(zip(*kept))
+    part = weight_grads(cuts, families[:4], families[4:])
+    part = lax.psum_scatter(part, "head", scatter_dimension=0, tiled=True).reshape(slots, own_rows, -1)
+    part = lax.all_to_all(part, "seq", split_axis=0, concat_axis=0, tiled=True)
+    part = part.astype(F32).sum(axis=0)
+
+    own = sums_own[0]
+    rows_sum = sums_rows[0]
+    up_sum = sums_up[0]
+    for m in range(1, micros):
+        own, rows_sum, up_sum = own + sums_own[m], rows_sum + sums_rows[m], up_sum + sums_up[m]
+    mine = (jnp.arange(groups) == head)[None, :, None]
+
+    def spread_own(row):
+        piece_of = jnp.transpose(row.reshape(heads, slots, -1), (1, 0, 2)).reshape(slots, 1, -1)
+        return jnp.where(mine, piece_of, 0.0)
+
+    def spread_plain(row):
+        return jnp.broadcast_to(row.reshape(slots, 1, -1), (slots, groups, own_rows))
+
+    up_part = jnp.transpose(up_sum.reshape(groups, heads, slots, -1), (2, 0, 1, 3))
+    out_vectors = jnp.concatenate(
+        [
+            spread_own(own[0]),
+            spread_own(own[1]),
+            spread_plain(rows_sum[0]),
+            spread_plain(rows_sum[1]),
+            spread_plain(rows_sum[2]),
+            up_part.reshape(slots, groups, own_rows),
+            spread_plain(rows_sum[3]),
+            spread_plain(rows_sum[4]),
+            spread_plain(rows_sum[5]),
+        ],
+        axis=2,
+    ).reshape(slots * groups, -1)
+    out_vectors = lax.all_to_all(out_vectors, grid, split_axis=0, concat_axis=0, tiled=True).sum(axis=0)
+
+    def vector_out(i):
+        return out_vectors[offsets[i] : offsets[i + 1]]
+
+    sent = []
+    for m in range(micros):
+        y, dx = returned[m]
+        sent.append(jnp.stack([y.reshape(per, piece, model), dx.reshape(per, piece, model)], axis=1))
+    sent = jnp.stack(sent, axis=1)
+    back = []
+    for step in range(2):
+        block = lax.dynamic_index_in_dim(sent, (here // groups + step) % 2, 0, keepdims=False)
+        pairs = [(b, a) for a, b in by_step(step, groups, slots)]
+        back.append(lax.ppermute(block, grid, pairs))
+    back = jnp.stack(back)
+    all_y = lax.all_gather(back[:, :, 0], "head", axis=0).reshape(-1, micros, piece, model)
+    dx_send = back[:, :, 1].reshape(2, micros, piece, groups, -1)
+    dx_send = jnp.transpose(dx_send, (3, 0, 1, 2, 4))
+    all_dx = across_heads(dx_send).reshape(-1, micros, piece, model // groups)
+    out_tokens, grad_tokens = [], []
+    for m in range(micros):
+        slot = dealing[m]
+        which = ((slot + here // 2) % groups) * 2 + (slot // groups + here) % 2
+        out_tokens.append(jnp.take(all_y[:, m], which, axis=0, mode="clip"))
+        grad_tokens.append(jnp.take(all_dx[:, m], which, axis=0, mode="clip"))
+
+    def columns(start, count):
+        return part[:, start : start + count]
+
+    return (
+        jnp.stack(out_tokens),
+        jnp.transpose(logits, (0, 2, 1, 3))[:, None],
+        jnp.stack(grad_tokens),
+        jnp.transpose(grad_logits, (0, 1, 3, 2, 4)),
+        columns(0, width),
+        vector_out(0).reshape(heads, -1),
+        columns(width, width),
+        columns(2 * width, width),
+        vector_out(1).reshape(heads, -1),
+        columns(3 * width, width).T,
+        vector_out(2),
+        vector_out(3),
+        vector_out(4),
+        columns(cuts[1], unit),
+        vector_out(5).reshape(heads, -1),
+        columns(cuts[2], unit).T,
+        vector_out(6),
+        vector_out(7),
+        vector_out(8),
+    )
+
 
 def solution(mesh):
     placed = (
@@ -422,7 +1114,7 @@
         P(None, "seq", None, "head", None),
     )
     return jax.shard_map(
-        on_device,
+        on_device if fits(mesh) else on_device_general,
         mesh=mesh,
         in_specs=placed,
         out_specs=(

time: 1510 us -> 971 us (0.64); the launches traced: 1490 us -> 963 us
  local copies, waits for them, and re-layouts: 280 us -> 69 us
  Pallas kernels: 0 us -> 167 us
  matrix products: 154 us -> 0 us
  waiting for transfers between devices: 472 us -> 348 us
  other arithmetic: 129 us -> 17.1 us
  starting transfers between devices: 145 us -> 73 us
  blocking collectives: 285 us -> 263 us
    ppermute x0 -> x6, waiting for transfers between devices: none -> 290 us  [the longest x4 271 us: to_slots(): arrived.append(lax.ppermute(out, grid, by_step(step, groups, slots)))]
    all_to_all x24 -> x10, waiting for transfers between devices: 313 us -> 42.1 us  [the longest x6 18.4 us: across_heads(): lax.all_to_all(array, 'head', split_axis=0, concat_axis=0, tiled=True)]
    all_to_all x1 -> x4, blocking collectives: 22.4 us -> 263 us  [the longest x2 221 us: on_device(): got = lax.all_to_all(send, 'seq', split_axis=0, concat_axis=0, tiled=True)]
    all_gather x7 -> x0, blocking collectives: 233 us -> none  [the longest x1 107 us: on_device(): lax.all_gather(b_query, 'seq', axis=1, tiled=True)]
    pallas_call x0 -> x14, Pallas kernels: none -> 167 us  [the longest x2 36.6 us: attention_backward(): pl.pallas_call(functools.partial(backward_kernel, heads), out_shape=(jax....]
    psum x3 -> x0, waiting for transfers between devices: 156 us -> none  [the longest x1 78.4 us: on_device(): branch = lax.psum(out_part, 'head') + bias_out.astype(jnp.float32)]
    dot_general x46 -> x0, matrix products: 122 us -> none  [the longest x2 18.8 us: on_device(): jnp.dot(hidden_low, up_full, preferred_element_type=jnp.float32)]
    all_to_all x24 -> x10, starting transfers between devices: 145 us -> 50.1 us  [the longest x6 23 us: across_heads(): lax.all_to_all(array, 'head', split_axis=0, concat_axis=0, tiled=True)]
  transfers between devices with their start and end apart: 31 -> 19, of which waited for: 21 -> 10; matrix products, arithmetic and copies ran while one was open for 28% -> 7% of each run, Pallas kernels for 0% -> 16%
where the time goes in v1:
time: 971 us; the launch traced here: 963 us
  waiting for transfers between devices  348 us (36%)
  blocking collectives  263 us (27%)
  Pallas kernels  167 us (17%)
  starting transfers between devices  73 us (8%)
  local copies, waits for them, and re-layouts  69 us (7%)
  between operations  26.1 us (3%)
  other arithmetic  17.1 us (2%)
    ppermute x4, waiting for transfers between devices, to_slots(): arrived.append(lax.ppermute(out, grid, by_step(step, groups, slots)))  271 us
    all_to_all x2, blocking collectives, on_device(): got = lax.all_to_all(send, 'seq', split_axis=0, concat_axis=0, tiled=True)  221 us
    all_to_all x2, blocking collectives, across_heads(): lax.all_to_all(array, 'head', split_axis=0, concat_axis=0, tiled=True)  41.7 us
    pallas_call x2, Pallas kernels, attention_backward(): pl.pallas_call(functools.partial(backward_kernel, heads), out_shape=(jax....  36.6 us
    pallas_call x2, Pallas kernels, attention_forward(): pl.pallas_call(functools.partial(forward_kernel, heads), out_shape=(jax.S...  36.1 us
    pallas_call x2, Pallas kernels, row_work(): pl.pallas_call(functools.partial(rows_kernel, cuts), out_shape=(shape((ro...  33.1 us
    all_to_all x6, starting transfers between devices, across_heads(): lax.all_to_all(array, 'head', split_axis=0, concat_axis=0, tiled=True)  23 us
  transfers between devices with their start and end apart: 19, of which 10 were waited for; matrix products, arithmetic and copies ran while one was open for 7% of the time, Pallas kernels for 16%

profile of v1, /device:TPU:15, one launch (start us, length us, event | category | flops | bytes accessed | tf_op | source)
XLA Modules:
  0.0 963.2 jit_solution(16114045767619428929)
XLA Ops:
  10.4 4.1 concatenate.37
  14.6 2.0 concatenate.38
  17.3 7.7 pick_blocks.2
  25.0 5.9 all-to-all-start.1
  39.7 2.2 collective-permute-start
  42.0 4.0 collective-permute-start.1
  46.1 97.6 %collective-permute-done = bf16[2,112,768]{2,1,0:T(8,128)(2,1)S(1)} collective-permute-done((bf16[2,112,768]{2,1,0:T(8,128)(2,1)S(1)}, bf16[2,112,768]{2,1,0:T(8,128)(2,1)S(1)}, u32[]{:S(2)}, u32[]{:S(2)}) %collective-permute-start) | collective-permute-done | bytes 344096 | tf_op jit(solution)/shard_map/ppermute | solution.py:957
  143.7 70.8 %collective-permute-done.1 = bf16[2,112,768]{2,1,0:T(8,128)(2,1)S(1)} collective-permute-done((bf16[2,112,768]{2,1,0:T(8,128)(2,1)S(1)}, bf16[2,112,768]{2,1,0:T(8,128)(2,1)S(1)}, u32[]{:S(2)}, u32[]{:S(2)}) %collective-permute-start.1) | collective-permute-done | bytes 344096 | tf_op jit(solution)/shard_map/ppermute | solution.py:957
  216.6 10.9 %copy.96 = bf16[8,4,96,2432]{3,2,0,1:T(8,128)(2,1)} copy(bf16[8,4,96,2432]{3,2,1,0:T(8,128)(2,1)} %bitcast.186) | data formatting | bytes 29884416 | tf_op jit(solution)/shard_map/reshape | solution.py:923
  227.5 1.3 slice_convert_fusion
  230.7 6.4 project.1
  237.1 4.1 all-to-all-start
  241.2 7.7 pick_blocks.3
  248.9 18.4 %all-to-all-done = bf16[4,448,576]{2,1,0:T(8,128)(2,1)S(1)} async-done(((bf16[4,448,576]{2,1,0:T(8,128)(2,1)}), bf16[4,448,576]{2,1,0:T(8,128)(2,1)S(1)}, u32[]{:S(2)}, u32[]{:S(2)}) %all-to-all-start) | async-done | bytes 2064416 | tf_op jit(solution)/shard_map/all_to_all | solution.py:967
  267.3 1.4 copy-done.1
  268.7 10.3 %all-to-all-start.5 = ((bf16[8,3,112,896]{3,2,1,0:T(8,128)(2,1)}), bf16[8,3,112,896]{3,2,1,0:T(8,128)(2,1)}, u32[]{:S(2)}, u32[]{:S(2)}) async-start(bf16[8,3,112,896]{3,2,1,0:T(8,128)(2,1)} %pick_blocks.3), calls=%async_computation.5 | async-start | bytes 9633792 | tf_op jit(solution)/shard_map/all_to_all | solution.py:974
  279.0 1.9 fusion.22
  281.1 4.0 collective-permute-start.3
  285.1 1.9 collective-permute-start.2
  291.6 1.2 pad_add_fusion.info_ref
  294.9 102.7 %collective-permute-done.3 = bf16[2,112,768]{2,1,0:T(8,128)(2,1)S(1)} collective-permute-done((bf16[2,112,768]{2,1,0:T(8,128)(2,1)S(1)}, bf16[2,112,768]{2,1,0:T(8,128)(2,1)S(1)}, u32[]{:S(2)}, u32[]{:S(2)}) %collective-permute-start.3) | collective-permute-done | bytes 344096 | tf_op jit(solution)/shard_map/ppermute | solution.py:957
  398.6 18.1 %attention_forward.2 = (bf16[2,3,896,896]{3,2,1,0:T(8,128)(2,1)}, bf16[8,3,112,896]{3,2,1,0:T(8,128)(2,1)}, bf16[4,224,192]{2,1,0:T(8,128)(2,1)}) custom-call(s32[2]{0:T(128)} %pad_add_fusion.info_ref, bf16[4,2,224,576]{3,2,1,0:T(8,128)(2,1)} %bitcast.189, bf16[8,3,112,896]{3,2,1,0:T(8,128)(2,1)} %all-to-all-done.1.prev_ref), custom_call_target="tpu_custom_call" | custom-call | flops 2466250752 | bytes 14450688 | tf_op jit(solution)/shard_map/attention_forward/pallas_call | solution.py:540
  416.7 2.0 copy.100
  418.7 4.8 all-to-all-start.2
  425.5 18.0 %attention_forward.3 = (bf16[2,3,896,896]{3,2,1,0:T(8,128)(2,1)}, bf16[8,3,112,896]{3,2,1,0:T(8,128)(2,1)}, bf16[4,224,192]{2,1,0:T(8,128)(2,1)}) custom-call(s32[2]{0:T(128)} %pad_add_fusion.1.info_ref, bf16[4,2,224,576]{3,2,1,0:T(8,128)(2,1)} %bitcast.190, bf16[8,3,112,896]{3,2,1,0:T(8,128)(2,1)} %all-to-all-done.5.prev_ref, ...), custom_call_target="tpu_custom_call", output_to_operand_aliasing={{0}: (3, {})} | custom-call | flops 2466250752 | bytes 14450688 | tf_op jit(solution)/shard_map/attention_forward/pallas_call | solution.py:540
  443.6 2.0 copy.105
  445.6 3.6 all-to-all-start.6
  450.2 16.6 %row_work.2 = (bf16[224,768]{1,0:T(8,128)(2,1)}, f32[224,768]{1,0:T(8,128)}, bf16[4,224,192]{2,1,0:T(8,128)(2,1)}, bf16[224,768]{1,0:T(8,128)(2,1)}, bf16[4,224,...) custom-call(bf16[4,224,192]{2,1,0:T(8,128)(2,1)} %copy.102.con_ref.r, ...), custom_call_target="tpu_custom_call" | custom-call | flops 5284823040 | bytes 14942208 | tf_op jit(solution)/shard_map/row_work/pallas_call | solution.py:737
  466.8 2.0 copy.103
  468.7 3.5 all-to-all-start.3
  473.2 16.5 %row_work.3 = (bf16[224,768]{1,0:T(8,128)(2,1)}, f32[224,768]{1,0:T(8,128)}, bf16[4,224,192]{2,1,0:T(8,128)(2,1)}, bf16[224,768]{1,0:T(8,128)(2,1)}, bf16[4,224,...) custom-call(bf16[4,224,192]{2,1,0:T(8,128)(2,1)} %copy.106.con_ref.r, ...), custom_call_target="tpu_custom_call" | custom-call | flops 5284823040 | bytes 14942208 | tf_op jit(solution)/shard_map/row_work/pallas_call | solution.py:737
  489.7 2.0 copy.107
  491.7 3.5 all-to-all-start.7
  496.2 18.3 %attention_backward.2 = (bf16[8,3,112,896]{3,2,1,0:T(8,128)(2,1)}, bf16[4,224,576]{2,1,0:T(8,128)(2,1)}, f32[2,192]{1,0:T(2,128)}) custom-call(s32[2]{0:T(128)} %pad_add_fusion.info_ref, bf16[4,2,224,576]{3,2,1,0:T(8,128)(2,1)} %bitcast.191, bf16[8,3,112,896]{3,2,1,0:T(8,128)(2,1)} %get-tuple-element.54.attend_ref, ...), custom_call_target="tpu_custom_call" | custom-call | flops 4932501504 | bytes 14450688 | tf_op jit(solution)/shard_map/attention_backward/pallas_call | solution.py:623
  514.4 3.5 all-to-all-start.4
  519.2 18.3 %attention_backward.3 = (bf16[8,3,112,896]{3,2,1,0:T(8,128)(2,1)}, bf16[4,224,576]{2,1,0:T(8,128)(2,1)}, f32[2,192]{1,0:T(2,128)}) custom-call(s32[2]{0:T(128)} %pad_add_fusion.1.info_ref, bf16[4,2,224,576]{3,2,1,0:T(8,128)(2,1)} %bitcast.192, bf16[8,3,112,896]{3,2,1,0:T(8,128)(2,1)} %get-tuple-element.62.attend_ref, ...), custom_call_target="tpu_custom_call" | custom-call | flops 4932501504 | bytes 14450688 | tf_op jit(solution)/shard_map/attention_backward/pallas_call | solution.py:623
  537.6 18.5 %all_to_all.74.dqkv_ref.refs_9_ = bf16[4,224,576]{2,1,0:T(8,128)(2,1)} all-to-all(bf16[4,224,576]{2,1,0:T(8,128)(2,1)} %get-tuple-element.64), channel_id=1, replica_groups=mesh['seq'=8,'head'=4] {'head'}, dimensions={0} | all-to-all | bytes 2064384 | tf_op jit(solution)/shard_map/all_to_all | solution.py:967
  556.0 14.3 %weight_grads.1 = bf16[4,768,2304]{2,1,0:T(8,128)(2,1)} custom-call(bf16[224,768]{1,0:T(8,128)(2,1)} %get-tuple-element.198.x_ref.refs_0_, bf16[224,768]{1,0:T(8,128)(2,1)} %get-tuple-element.197.x_ref.refs_1_, bf16[224,768]{1,0:T(8,128)(2,1)} %get-tuple-element.69.refs_2_, bf16[224,768]{1,0:T(8,128)(2,1)} %get-tuple-element.70.refs_3_, ...), custom_call_target="tpu_custom_call" | custom-call | flops 6341787648 | bytes 14155776 | tf_op jit(solution)/shard_map/weight_grads/pallas_call | solution.py:817
  570.4 5.0 input_grad.2
  575.4 5.0 input_grad.3
  581.7 4.1 collective-permute-start.5
  585.9 6.4 collective-permute-start.4
  594.6 5.2 all-to-all-start.13
  599.8 9.7 %collective-permute-done.5 = bf16[2,2,112,768]{3,2,1,0:T(8,128)(2,1)S(1)} collective-permute-done((bf16[2,2,112,768]{3,2,1,0:T(8,128)(2,1)S(1)}, bf16[2,2,112,768]{3,2,1,0:T(8,128)(2,1)S(1)}, u32[]{:S(2)}, u32[]{:S(2)}) %collective-permute-start.5) | collective-permute-done | bytes 688160 | tf_op jit(solution)/shard_map/ppermute | solution.py:1053
  609.9 9.3 collective-permute-done.4
  620.9 6.6 all-to-all-done.13
  627.5 23.3 %all_to_all.75 = bf16[4,2,2,112,192]{3,4,2,1,0:T(8,128)(2,1)} all-to-all(bf16[4,2,2,112,192]{3,4,2,1,0:T(8,128)(2,1)S(1)} %copy.112), channel_id=1, replica_groups=mesh['seq'=8,'head'=4] {'head'}, dimensions={0} | all-to-all | bytes 1376256 | tf_op jit(solution)/shard_map/all_to_all | solution.py:967
  650.8 111.1 %all_to_all.76.x_ref = bf16[8,3,112,896]{3,2,1,0:T(8,128)(2,1)} all-to-all(bf16[8,3,112,896]{3,2,1,0:T(8,128)(2,1)} %get-tuple-element.67), channel_id=1, replica_groups=mesh['seq'=8,'head'=4] {'seq'}, dimensions={0} | all-to-all | bytes 9633792 | tf_op jit(solution)/shard_map/all_to_all | solution.py:994
  761.9 109.7 %all_to_all.77.x_ref = bf16[8,3,112,896]{3,2,1,0:T(8,128)(2,1)} all-to-all(bf16[8,3,112,896]{3,2,1,0:T(8,128)(2,1)S(1)} %bitcast.196), channel_id=1, replica_groups=mesh['seq'=8,'head'=4] {'seq'}, dimensions={0} | all-to-all | bytes 9633792 | tf_op jit(solution)/shard_map/all_to_all | solution.py:994
  871.6 5.6 all-to-all-start.12
  877.2 2.2 copy.111
  881.0 1.3 reshape.486
  884.2 2.0 slice_bitcast_fusion.3
  886.3 2.4 gather_fusion.3
  888.6 2.4 gather_fusion.2
  891.0 2.3 pad_maximum_fusion.3
  893.3 15.0 %all-gather.7.cloned.1.call-done = bf16[8,2,1,112,768]{4,3,2,1,0:T(8,128)(2,1)} async-done(((bf16[2,2,1,112,768]{4,3,2,1,0:T(8,128)(2,1)}), bf16[8,2,1,112,768]{4,3,2,1,0:T(8,128)(2,1)}) %all-gather.7.cloned.1.call-update) | async-done | bytes 2752528 | tf_op jit(solution)/shard_map/all_gather | solution.py:1055
  908.3 3.5 slice_bitcast_fusion.1
  911.8 3.1 gather_fusion.1
  914.9 3.0 gather_fusion
  917.9 3.5 pad_maximum_fusion
  921.4 7.7 place_blocks.2.rest_0_
  929.1 7.7 place_blocks.3
  936.7 17.0 %all-to-all-done.12 = bf16[8,96,2304]{2,1,0:T(8,128)(2,1)S(1)} async-done(((bf16[8,96,2304]{2,1,0:T(8,128)(2,1)}), bf16[8,96,2304]{2,1,0:T(8,128)(2,1)S(1)}, u32[]{:S(2)}, u32[]{:S(2)}) %all-to-all-start.12) | async-done | bytes 3538976 | tf_op jit(solution)/shard_map/all_to_all | solution.py:1007
  (167 shorter events, 31.0 us)
Async XLA Ops:
  7.2 9.4 copy-start.14
  7.2 209.4 %all-gather.5.cloned.1.call-start = ((), (), s32[]{:S(2)}) async-start(), calls=%async_computation.16 | async-start | bytes 15409152 | tf_op jit(solution)/shard_map/all_gather | solution.py:923
  16.6 8.3 copy-start.16
  16.7 14.2 %copy-start.15 = (s32[8]{0:T(128)}, s32[8]{0:T(128)S(1)}, u32[]{:S(2)}) copy-start(s32[8]{0:T(128)S(1)} %get-tuple-element.224.index_ref) | copy-start | bytes 100
  25.0 6.1 copy-start.13
  25.0 14.5 %copy-start.2 = (bf16[2,8,112,768]{3,2,1,0:T(8,128)(2,1)S(1)}, bf16[2,8,112,768]{3,2,1,0:T(8,128)(2,1)}, u32[]{:S(2)}) copy-start(bf16[2,8,112,768]{3,2,1,0:T(8,128)(2,1)} %param.21) | copy-start | bytes 8257540
  25.0 212.2 %all-to-all-start.1 = ((bf16[8,3,112,896]{3,2,1,0:T(8,128)(2,1)}), bf16[8,3,112,896]{3,2,1,0:T(8,128)(2,1)}, u32[]{:S(2)}, u32[]{:S(2)}) async-start(bf16[8,3,112,896]{3,2,1,0:T(8,128)(2,1)} %pick_blocks.2), calls=%async_computation.1 | async-start | bytes 9633792 | tf_op jit(solution)/shard_map/all_to_all | solution.py:974
  31.0 8.6 copy-start.12
  39.7 104.0 %collective-permute-start = (bf16[2,112,768]{2,1,0:T(8,128)(2,1)S(1)}, bf16[2,112,768]{2,1,0:T(8,128)(2,1)S(1)}, u32[]{:S(2)}, u32[]{:S(2)}) collective-permute-start(bf16[2,112,768]{2,1,0:T(8,128)(2,1)S(1)} %pad_maximum_fusion.5), channel_id=1, source_target_pairs={{0,16},{1,21},{2,26},{3,31},{4,0},{5,5},{6,10},{7,15},{8,28},{9,17... | collective-permute-start | bytes 1032200 | tf_op jit(solution)/shard_map/ppermute | solution.py:957
  42.0 172.5 %collective-permute-start.1 = (bf16[2,112,768]{2,1,0:T(8,128)(2,1)S(1)}, bf16[2,112,768]{2,1,0:T(8,128)(2,1)S(1)}, u32[]{:S(2)}, u32[]{:S(2)}) collective-permute-start(bf16[2,112,768]{2,1,0:T(8,128)(2,1)S(1)} %pad_maximum_fusion.6), channel_id=1, source_target_pairs={{0,0},{1,5},{2,10},{3,15},{4,16},{5,21},{6,26},{7,31},{8,12},{9,1}... | collective-permute-start | bytes 1032200 | tf_op jit(solution)/shard_map/ppermute | solution.py:957
  237.1 30.2 %all-to-all-start = ((bf16[4,448,576]{2,1,0:T(8,128)(2,1)}), bf16[4,448,576]{2,1,0:T(8,128)(2,1)S(1)}, u32[]{:S(2)}, u32[]{:S(2)}) async-start(bf16[4,448,576]{2,1,0:T(8,128)(2,1)} %project.1), calls=%async_computation | async-start | bytes 4587520 | tf_op jit(solution)/shard_map/all_to_all | solution.py:967
  267.3 1.4 copy-start.1
  268.7 150.0 %all-to-all-start.5 = ((bf16[8,3,112,896]{3,2,1,0:T(8,128)(2,1)}), bf16[8,3,112,896]{3,2,1,0:T(8,128)(2,1)}, u32[]{:S(2)}, u32[]{:S(2)}) async-start(bf16[8,3,112,896]{3,2,1,0:T(8,128)(2,1)} %pick_blocks.3), calls=%async_computation.5 | async-start | bytes 9633792 | tf_op jit(solution)/shard_map/all_to_all | solution.py:974
  280.9 10.0 %copy-start.19 = (s32[2,8]{1,0:T(2,128)S(1)}, s32[2,8]{1,0:T(2,128)}, u32[]{:S(2)}) copy-start(s32[2,8]{1,0:T(2,128)} %param.23) | copy-start | bytes 196
  281.1 116.5 %collective-permute-start.3 = (bf16[2,112,768]{2,1,0:T(8,128)(2,1)S(1)}, bf16[2,112,768]{2,1,0:T(8,128)(2,1)S(1)}, u32[]{:S(2)}, u32[]{:S(2)}) collective-permute-start(bf16[2,112,768]{2,1,0:T(8,128)(2,1)S(1)} %pad_maximum_fusion.8), channel_id=1, source_target_pairs={{0,0},{1,5},{2,10},{3,15},{4,16},{5,21},{6,26},{7,31},{8,12},{9,1}... | collective-permute-start | bytes 1032200 | tf_op jit(solution)/shard_map/ppermute | solution.py:957
  285.1 112.5 %collective-permute-start.2 = (bf16[2,112,768]{2,1,0:T(8,128)(2,1)S(1)}, bf16[2,112,768]{2,1,0:T(8,128)(2,1)S(1)}, u32[]{:S(2)}, u32[]{:S(2)}) collective-permute-start(bf16[2,112,768]{2,1,0:T(8,128)(2,1)S(1)} %pad_maximum_fusion.7), channel_id=1, source_target_pairs={{0,16},{1,21},{2,26},{3,31},{4,0},{5,5},{6,10},{7,15},{8,28},{9,17... | collective-permute-start | bytes 1032200 | tf_op jit(solution)/shard_map/ppermute | solution.py:957
  418.7 26.9 %all-to-all-start.2 = ((bf16[4,224,192]{1,2,0:T(8,128)(2,1)}), bf16[4,224,192]{1,2,0:T(8,128)(2,1)S(1)}, u32[]{:S(2)}, u32[]{:S(2)}) async-start(bf16[4,224,192]{1,2,0:T(8,128)(2,1)} %copy.100), calls=%async_computation.2 | async-start | bytes 786432 | tf_op jit(solution)/shard_map/all_to_all | solution.py:967
  445.6 23.2 %all-to-all-start.6 = ((bf16[4,224,192]{1,2,0:T(8,128)(2,1)}), bf16[4,224,192]{1,2,0:T(8,128)(2,1)S(1)}, u32[]{:S(2)}, u32[]{:S(2)}) async-start(bf16[4,224,192]{1,2,0:T(8,128)(2,1)} %copy.105), calls=%async_computation.6 | async-start | bytes 786432 | tf_op jit(solution)/shard_map/all_to_all | solution.py:967
  468.7 23.0 %all-to-all-start.3 = ((bf16[4,224,192]{1,2,0:T(8,128)(2,1)}), bf16[4,224,192]{1,2,0:T(8,128)(2,1)S(1)}, u32[]{:S(2)}, u32[]{:S(2)}) async-start(bf16[4,224,192]{1,2,0:T(8,128)(2,1)} %copy.103), calls=%async_computation.3 | async-start | bytes 786432 | tf_op jit(solution)/shard_map/all_to_all | solution.py:967
  491.7 22.7 %all-to-all-start.7 = ((bf16[4,224,192]{1,2,0:T(8,128)(2,1)}), bf16[4,224,192]{1,2,0:T(8,128)(2,1)S(1)}, u32[]{:S(2)}, u32[]{:S(2)}) async-start(bf16[4,224,192]{1,2,0:T(8,128)(2,1)} %copy.107), calls=%async_computation.7 | async-start | bytes 786432 | tf_op jit(solution)/shard_map/all_to_all | solution.py:967
  514.4 23.1 %all-to-all-start.4 = ((bf16[4,224,576]{2,1,0:T(8,128)(2,1)}), bf16[4,224,576]{2,1,0:T(8,128)(2,1)S(1)}, u32[]{:S(2)}, u32[]{:S(2)}) async-start(bf16[4,224,576]{2,1,0:T(8,128)(2,1)} %get-tuple-element.56), calls=%async_computation.4 | async-start | bytes 2293760 | tf_op jit(solution)/shard_map/all_to_all | solution.py:967
  518.0 353.6 %reduce-scatter.2.cloned.1.call-start = ((), (), s32[]{:S(2)}) async-start(), calls=%async_computation.15 | async-start | bytes 17694720 | tf_op jit(solution)/shard_map/reduce_scatter | solution.py:1006
  537.5 18.5 %copy-start = (bf16[4,224,576]{2,1,0:T(8,128)(2,1)}, bf16[4,224,576]{2,1,0:T(8,128)(2,1)S(1)}, u32[]{:S(2)}) copy-start(bf16[4,224,576]{2,1,0:T(8,128)(2,1)S(1)} %all-to-all-done.4.dqkv_ref.refs_8_) | copy-start | bytes 3096580
  575.4 5.0 copy-start.3
  575.4 5.0 copy-start.6
  580.4 1.0 copy-start.4
  580.4 1.1 copy-start.7
  581.5 10.9 %copy-start.8 = (f32[8,768]{1,0:T(8,128)S(1)}, f32[8,768]{1,0:T(8,128)}, u32[]{:S(2)}) copy-start(f32[8,768]{1,0:T(8,128)} %get-tuple-element.81) | copy-start | bytes 73732
  581.6 10.9 %copy-start.9 = (f32[8,768]{1,0:T(8,128)S(1)}, f32[8,768]{1,0:T(8,128)}, u32[]{:S(2)}) copy-start(f32[8,768]{1,0:T(8,128)} %get-tuple-element.82) | copy-start | bytes 73732
  581.6 11.1 %copy-start.10 = (f32[4,1,768]{2,1,0:T(1,128)S(1)}, f32[4,1,768]{2,1,0:T(1,128)}, u32[]{:S(2)}) copy-start(f32[4,1,768]{2,1,0:T(1,128)} %get-tuple-element.83) | copy-start | bytes 36868
  581.6 11.1 %copy-start.11 = (f32[4,1,768]{2,1,0:T(1,128)S(1)}, f32[4,1,768]{2,1,0:T(1,128)}, u32[]{:S(2)}) copy-start(f32[4,1,768]{2,1,0:T(1,128)} %get-tuple-element.84) | copy-start | bytes 36868
  581.6 11.6 %copy-start.17 = (f32[2,192]{1,0:T(2,128)S(1)}, f32[2,192]{1,0:T(2,128)}, u32[]{:S(2)}) copy-start(f32[2,192]{1,0:T(2,128)} %get-tuple-element.79) | copy-start | bytes 4612
  581.6 11.6 %copy-start.18 = (f32[2,192]{1,0:T(2,128)S(1)}, f32[2,192]{1,0:T(2,128)}, u32[]{:S(2)}) copy-start(f32[2,192]{1,0:T(2,128)} %get-tuple-element.80) | copy-start | bytes 4612
  581.7 27.8 %collective-permute-start.5 = (bf16[2,2,112,768]{3,2,1,0:T(8,128)(2,1)S(1)}, bf16[2,2,112,768]{3,2,1,0:T(8,128)(2,1)S(1)}, u32[]{:S(2)}, u32[]{:S(2)}) collective-permute-start(bf16[2,2,112,768]{3,2,1,0:T(8,128)(2,1)S(1)} %get-tuple-element.177), channel_id=1, source_target_pairs={{16,0},{21,1},{26,2},{31,3},{0,4},{5,5},{10,6},{15,7},{28,8},{17,9... | collective-permute-start | bytes 2064392 | tf_op jit(solution)/shard_map/ppermute | solution.py:1053
  585.9 33.4 %collective-permute-start.4 = (bf16[2,2,112,768]{3,2,1,0:T(8,128)(2,1)S(1)}, bf16[2,2,112,768]{3,2,1,0:T(8,128)(2,1)S(1)}, u32[]{:S(2)}, u32[]{:S(2)}) collective-permute-start(bf16[2,2,112,768]{3,2,1,0:T(8,128)(2,1)S(1)} %get-tuple-element.178), channel_id=1, source_target_pairs={{0,0},{5,1},{10,2},{15,3},{16,4},{21,5},{26,6},{31,7},{12,8},{1,9}... | collective-permute-start | bytes 2064392 | tf_op jit(solution)/shard_map/ppermute | solution.py:1053
  594.6 32.9 %all-to-all-start.13 = ((f32[32,1,720]{2,1,0:T(1,128)}), f32[32,1,720]{2,1,0:T(1,128)S(1)}, u32[]{:S(2)}, u32[]{:S(2)}) async-start(f32[32,1,720]{2,1,0:T(1,128)} %copy.120), calls=%async_computation.14 | async-start | bytes 196608 | tf_op jit(solution)/shard_map/all_to_all | solution.py:1039
  627.5 134.4 %copy-start.5 = (f32[32,1,720]{2,1,0:T(1,128)}, f32[32,1,720]{2,1,0:T(1,128)S(1)}, u32[]{:S(2)}) copy-start(f32[32,1,720]{2,1,0:T(1,128)S(1)} %all-to-all-done.13) | copy-start | bytes 276484
  627.5 134.4 %slice-start = ((s8[4816896]{0:T(1024)(128)(4,1)}), s8[4194304]{0:T(1024)(128)(4,1)S(1)}, s32[]{:S(2)}) async-start(s8[4816896]{0:T(1024)(128)(4,1)} %bitcast.195), calls=%async_computation.18 | async-start | bytes 8388608
  650.8 111.1 %slice-start.1 = ((s8[4816896]{0:T(1024)(128)(4,1)}), s8[622592]{0:T(1024)(128)(4,1)S(1)}, s32[]{:S(2)}) async-start(s8[4816896]{0:T(1024)(128)(4,1)} %bitcast.195), calls=%async_computation.19 | async-start | bytes 1245184
  871.6 82.2 %all-to-all-start.12 = ((bf16[8,96,2304]{2,1,0:T(8,128)(2,1)}), bf16[8,96,2304]{2,1,0:T(8,128)(2,1)S(1)}, u32[]{:S(2)}, u32[]{:S(2)}) async-start(bf16[8,96,2304]{2,1,0:T(8,128)(2,1)} %bitcast.197), calls=%async_computation.13 | async-start | bytes 7077888 | tf_op jit(solution)/shard_map/all_to_all | solution.py:1007
  877.2 31.1 %all-gather.7.cloned.1.call-start = ((), (), s32[]{:S(2)}) async-start(), calls=%async_computation.17 | async-start | bytes 3440640 | tf_op jit(solution)/shard_map/all_gather | solution.py:1055
Sparse Core Ops, SparseCore 0:
  16.7 199.7 all-gather.4
  570.5 120.7 reduce-scatter.1
  880.1 28.1 all-gather.6

commit v2 on v1

--- a/solution.py
+++ b/solution.py
@@ -403,7 +403,7 @@
     )
 
 def cost(flops, moved):
-    return pl.CostEstimate(flops=int(flops), bytes_accessed=int(moved), transcendentals=0)
+    return pl.CostEstimate(flops=int(flops) // 100, bytes_accessed=int(moved) // 100, transcendentals=0)
 
 
 def params(**more):
@@ -767,7 +767,9 @@
     total = dz_ref[...]
     for h in range(dqkv_ref.shape[0]):
         total = total + dot(dqkv_ref[h], w_ref[h, :, : dqkv_ref.shape[2]], 1, 1)
-    o_ref[...] = total.astype(BF16)
+    share = o_ref.shape[2]
+    for h in range(o_ref.shape[0]):
+        o_ref[h] = total[:, h * share : (h + 1) * share].astype(BF16)
 
 
 def input_grad(dqkv, weights, dz):
@@ -775,22 +777,23 @@
     model = dz.shape[1]
     return pl.pallas_call(
         input_kernel,
-        out_shape=jax.ShapeDtypeStruct((rows, model), BF16),
+        out_shape=jax.ShapeDtypeStruct((groups, rows, model // groups), BF16),
         grid=(1,),
         in_specs=[
             whole(dqkv),
             pl.BlockSpec((groups, model, model), lambda i: (0, 0, 0)),
             whole(dz),
         ],
-        out_specs=pl.BlockSpec((rows, model), lambda i: (0, 0)),
+        out_specs=pl.BlockSpec((groups, rows, model // groups), lambda i: (0, 0, 0)),
         compiler_params=params(),
         cost_estimate=cost(2 * groups * rows * columns * model, 2 * groups * columns * model),
         name="input_grad",
     )(dqkv, weights, dz)
 
 
-def weight_kernel(cuts, micros, *refs):
+def weight_kernel(cuts, micros, vector_ref, *refs):
     out_ref = refs[-1]
+    out_ref[0, :, cuts[-1] :] = vector_ref[0]
     qkv_end, out_end, up_end, down_end = cuts
 
     def product(lefts, rights):
@@ -807,33 +810,582 @@
     out_ref[0, :, up_end:down_end] = product(b2, act)
 
 
-def weight_grads(cuts, lefts, rights):
+def weight_grads(cuts, lefts, rights, vectors):
     micros = len(lefts[0])
     groups = rights[0][0].shape[0]
     model = lefts[0][0].shape[1]
     flat_left = [a for family in lefts for a in family]
     flat_right = [a for family in rights for a in family]
     rows = flat_left[0].shape[0]
+    columns = cuts[-1] + vectors.shape[2]
     return pl.pallas_call(
         functools.partial(weight_kernel, cuts, micros),
-        out_shape=jax.ShapeDtypeStruct((groups, model, cuts[-1]), BF16),
+        out_shape=jax.ShapeDtypeStruct((groups, model, columns), BF16),
         grid=(groups,),
-        in_specs=[whole(a) for a in flat_left]
+        in_specs=[pl.BlockSpec((1, *vectors.shape[1:]), lambda h: (h, 0, 0))]
+        + [whole(a) for a in flat_left]
         + [pl.BlockSpec((1, *a.shape[1:]), lambda h: (h, 0, 0)) for a in flat_right],
-        out_specs=pl.BlockSpec((1, model, cuts[-1]), lambda h: (h, 0, 0)),
+        out_specs=pl.BlockSpec((1, model, columns), lambda h: (h, 0, 0)),
         compiler_params=params(),
         cost_estimate=cost(2 * micros * groups * rows * model * cuts[-1], 2 * groups * model * cuts[-1]),
         name="weight_grads",
-    )(*flat_left, *flat_right)
-
-
-def by_step(step, groups, slots):
-    pairs = []
-    for home in range(slots):
+    )(vectors, *flat_left, *flat_right)
+
+
+MESH = pl.DeviceIdType.MESH
+SIDE = 2
+
+
+def remote(source, target, send_sem, recv_sem, device):
+    return pltpu.make_async_remote_copy(
+        src_ref=source,
+        dst_ref=target,
+        send_sem=send_sem,
+        recv_sem=recv_sem,
+        device_id=device,
+        device_id_type=MESH,
+    )
+
+
+def signal(device):
+    pl.semaphore_signal(
+        pltpu.get_barrier_semaphore(), inc=1, device_id=device, device_id_type=MESH
+    )
+
+
+def greet(devices):
+    for device in devices:
+        signal(device)
+    pl.semaphore_wait(pltpu.get_barrier_semaphore(), len(devices))
+
+
+def cross_kernel(groups, x_ref, o_ref, send_sem, recv_sem, own_sem):
+    me = lax.axis_index("head")
+    peers = [lax.rem(me + i, groups) for i in range(1, groups)]
+    greet([{"head": peer} for peer in peers])
+    copies = []
+    for i, peer in enumerate(peers):
+        copy = remote(x_ref.at[peer], o_ref.at[me], send_sem.at[i], recv_sem.at[i], {"head": peer})
+        copy.start()
+        copies.append(copy)
+    own = pltpu.make_async_copy(x_ref.at[me], o_ref.at[me], own_sem)
+    own.start()
+    own.wait()
+    for copy in copies:
+        copy.wait()
+
+
+def across_heads(x, number):
+    groups = x.shape[0]
+    return pl.pallas_call(
+        functools.partial(cross_kernel, groups),
+        out_shape=jax.ShapeDtypeStruct(x.shape, x.dtype),
+        in_specs=[pl.BlockSpec(memory_space=pltpu.VMEM)],
+        out_specs=pl.BlockSpec(memory_space=pl.ANY),
+        scratch_shapes=[
+            pltpu.SemaphoreType.DMA((groups - 1,)),
+            pltpu.SemaphoreType.DMA((groups - 1,)),
+            pltpu.SemaphoreType.DMA,
+        ],
+        compiler_params=params(collective_id=number, has_side_effects=True),
+        cost_estimate=cost(0, 40 * x.size),
+        name="across_heads",
+    )(x)
+
+
+SIDES = 2
+LINE = 4
+
+
+class Place:
+    def __init__(self):
+        self.here, self.head = lax.axis_index("seq"), lax.axis_index("head")
+        self.z, self.x = self.here // SIDES, lax.rem(self.here, SIDES)
+        self.y, self.c = self.head // 2, lax.rem(self.head, 2)
+        self.up, self.down = {"seq": self.here + SIDES}, {"seq": self.here - SIDES}
+        self.across = {"seq": self.z * SIDES + (1 - self.x)}
+        self.over = {"head": (1 - self.y) * 2 + self.c}
+        self.beside = {"head": self.y * 2 + (1 - self.c)}
+        self.not_last, self.not_first = self.z < LINE - 1, self.z > 0
+        half = (LINE - 1 - self.z) // 2
+        self.order = [self.z, self.z + 1 - 2 * lax.rem(self.z, 2), 1 + half, (LINE - 1) * half]
+
+    def greet_neighbours(self):
+        pl.when(self.not_last)(lambda: signal(self.up))
+        pl.when(self.not_first)(lambda: signal(self.down))
+        for device in (self.across, self.over, self.beside):
+            signal(device)
+        return 3 + self.not_last.astype(jnp.int32) + self.not_first.astype(jnp.int32)
+
+
+def arrived(block, send_sem, recv_sem, device):
+    remote(block, block, send_sem, recv_sem, device).wait_recv()
+
+
+def gather_kernel(
+    slots, groups, pack_ref, piece_ref, all_ref, rows_ref,
+    z_s, z_r, x_s, x_r, y_s, y_r, c_s, c_r, piece_s, piece_r, own_sem,
+):
+    me = Place()
+    here, head, x, y, c = me.here, me.head, me.x, me.y, me.c
+    group = lax.rem(head - here + slots, groups)
+    homes = [group * SIDE + p for p in range(SIDE)]
+    targets = [
+        lax.rem(head - me.z + groups, groups) + groups * lax.rem(here + step, 2) for step in range(2)
+    ]
+    expected = me.greet_neighbours()
+    for home in homes:
+        pl.when(home != here)(lambda home=home: signal({"seq": home}))
+    for target in targets:
+        expected = expected + (target != here).astype(jnp.int32)
+    pl.semaphore_wait(pltpu.get_barrier_semaphore(), expected)
+
+    def at(i, side, row, core=c):
+        return all_ref.at[row * 2 + core, i * SIDES + side]
+
+    def half(i, side, row, part):
+        return all_ref.at[row * 2 + c, i * SIDES + side, part]
+
+    def source(k):
+        return pack_ref if k == 0 else at(me.order[k], x, y)
+
+    def upward(k):
+        i = me.order[k]
+        return remote(source(k), at(i, x, y), z_s.at[i], z_r.at[i], me.up)
+
+    def downward(k):
+        i = me.order[k]
+        return remote(source(k), at(i, x, y), z_s.at[LINE + i], z_r.at[i], me.down)
+
+    def goes_up(k):
+        return (me.order[k] <= me.z) & me.not_last
+
+    def goes_down(k):
+        return (me.order[k] >= me.z) & me.not_first
+
+    def over_x(k, kind):
+        i = me.order[k]
+        n = kind * LINE + i
+        if kind < 2:
+            return remote(source(k).at[kind], half(i, x, y, kind), x_s.at[n], x_r.at[n], me.across)
+        block = half(i, x, 1 - y, 1)
+        return remote(block, block, x_s.at[n], x_r.at[n], me.across)
+
+    def over_y(k, kind):
+        i = me.order[k]
+        n = kind * LINE + i
+        if kind < 2:
+            return remote(source(k).at[1 - kind], half(i, x, y, 1 - kind), y_s.at[n], y_r.at[n], me.over)
+        block = half(i, 1 - x, y, 0)
+        return remote(block, block, y_s.at[n], y_r.at[n], me.over)
+
+    def to_core(k, kind):
+        i = me.order[k]
+        n = kind * LINE + i
+        if kind == 0:
+            return remote(source(k), at(i, x, y), c_s.at[n], c_r.at[n], me.beside)
+        block = at(i, *((1 - x, y), (x, 1 - y), (1 - x, 1 - y))[kind - 1])
+        return remote(block, block, c_s.at[n], c_r.at[n], me.beside)
+
+    def second(k):
+        i = me.order[k]
+        arrived(half(i, 1 - x, y, 0), x_s.at[i], x_r.at[i], me.across)
+        over_y(k, 2).start()
+        arrived(half(i, x, 1 - y, 1), y_s.at[i], y_r.at[i], me.over)
+        over_x(k, 2).start()
+
+    def piece(step):
+        return remote(
+            piece_ref.at[step], rows_ref.at[:, x], piece_s.at[step], piece_r.at[x], {"seq": targets[step]}
+        )
+
+    def piece_here(step):
+        return pltpu.make_async_copy(piece_ref.at[step], rows_ref.at[:, x], own_sem.at[1])
+
+    own = pltpu.make_async_copy(pack_ref, at(me.z, x, y), own_sem.at[0])
+    own.start()
+    for k in range(LINE):
+        i = me.order[k]
+        if k:
+            arrived(at(i, x, y), z_s.at[i], z_r.at[i], me.up)
+        pl.when(goes_up(k))(lambda k=k: upward(k).start())
+        pl.when(goes_down(k))(lambda k=k: downward(k).start())
+        over_x(k, 0).start()
+        over_y(k, 0).start()
+        if k:
+            second(k - 1)
+        over_x(k, 1).start()
+        over_y(k, 1).start()
+        to_core(k, 0).start()
+        if k == 2:
+            for step, target in enumerate(targets):
+                pl.when(target != here)(lambda step=step: piece(step).start())
+                pl.when(target == here)(lambda step=step: piece_here(step).start())
+    second(LINE - 1)
+    for k in range(LINE):
+        i = me.order[k]
+        n = LINE + i
+        arrived(half(i, 1 - x, y, 1), x_s.at[n], x_r.at[n], me.across)
+        to_core(k, 1).start()
+        arrived(half(i, x, 1 - y, 0), y_s.at[n], y_r.at[n], me.over)
+        to_core(k, 2).start()
+        n = 2 * LINE + i
+        arrived(half(i, 1 - x, 1 - y, 1), x_s.at[n], x_r.at[n], me.across)
+        arrived(half(i, 1 - x, 1 - y, 0), y_s.at[n], y_r.at[n], me.over)
+        to_core(k, 3).start()
+    for kind, (side, row) in enumerate(((x, y), (1 - x, y), (x, 1 - y), (1 - x, 1 - y))):
+        for k in range(LINE):
+            i = me.order[k]
+            n = kind * LINE + i
+            arrived(at(i, side, row, 1 - c), c_s.at[n], c_r.at[n], me.beside)
+    for p, home in enumerate(homes):
+        block = rows_ref.at[:, p]
+        pl.when(home != here)(
+            lambda block=block, p=p, home=home: arrived(
+                block, piece_s.at[p], piece_r.at[p], {"seq": home}
+            )
+        )
+    for step, target in enumerate(targets):
+        pl.when(target != here)(lambda step=step: piece(step).wait_send())
+        pl.when(target == here)(lambda step=step: piece_here(step).wait())
+    own.wait()
+    for k in range(LINE):
+        pl.when(goes_up(k))(lambda k=k: upward(k).wait_send())
+        pl.when(goes_down(k))(lambda k=k: downward(k).wait_send())
+        for kind in range(3):
+            over_x(k, kind).wait_send()
+            over_y(k, kind).wait_send()
+        for kind in range(4):
+            to_core(k, kind).wait_send()
+
+
+def gather_all(packed, pieces, slots, groups, number):
+    dma = pltpu.SemaphoreType.DMA
+    return pl.pallas_call(
+        functools.partial(gather_kernel, slots, groups),
+        out_shape=(
+            jax.ShapeDtypeStruct((groups, slots, *packed.shape), packed.dtype),
+            jax.ShapeDtypeStruct((pieces.shape[1], SIDE, *pieces.shape[2:]), pieces.dtype),
+        ),
+        in_specs=[pl.BlockSpec(memory_space=pltpu.VMEM)] * 2,
+        out_specs=(pl.BlockSpec(memory_space=pl.ANY),) * 2,
+        scratch_shapes=[dma((2 * LINE,)), dma((LINE,))]
+        + [dma((3 * LINE,))] * 4
+        + [dma((4 * LINE,))] * 2
+        + [dma((2,))] * 3,
+        compiler_params=params(collective_id=number, has_side_effects=True),
+        cost_estimate=cost(0, 3000000 * 40),
+        name="gather_all",
+    )(packed, pieces)
+
+
+def add_into(target, terms, shape):
+    rows = shape[-2]
+    tile = 16
+    steps = rows // tile
+    outer = 1
+    for n in shape[:-2]:
+        outer *= n
+
+    def body(i, carry):
+        at = pl.ds(pl.multiple_of(lax.rem(i, steps) * tile, tile), tile)
+        rest = i // steps
+        index = []
+        for n in reversed(shape[:-2]):
+            index.insert(0, lax.rem(rest, n))
+            rest = rest // n
+        index = (*index, at)
+        total = terms[0][index].astype(F32)
+        for term in terms[1:]:
+            total = total + term[index].astype(F32)
+        target[index] = total.astype(target.dtype)
+        return carry
+
+    lax.fori_loop(0, outer * steps, body, 0)
+
+
+def finish_kernel(
+    slots, groups, micros, part_ref, y_ref, dx_ref, sum_ref, tokens_ref, grads_ref,
+    held, first_a, first_b, second_a, second_b, line,
+    c_s, c_r, x_s, x_r, y_s, y_r, z_s, z_r, home_s, home_r, over_s, over_r, near_s, near_r, pass_s, pass_r,
+    grad_s, grad_r, own_sem,
+):
+    me = Place()
+    here, head, x, y, z, c = me.here, me.head, me.x, me.y, me.z, me.c
+    order = me.order[::-1]
+    group = lax.rem(head - here + slots, groups)
+    homes = [group * SIDE + p for p in range(SIDE)]
+    mine = lax.rem(head - z + groups, groups)
+    senders = [lax.rem(slot + z, groups) for slot in range(slots)]
+
+    def is_me(slot, other):
+        return (slot == here) & (other == head)
+
+    expected = me.greet_neighbours()
+    for slot in range(slots):
+        pl.when(jnp.logical_not(is_me(slot, senders[slot])))(
+            lambda slot=slot: signal({"seq": slot, "head": senders[slot]})
+        )
+    for home in homes:
         for h in range(groups):
-            slot = (h - home // 2) % groups + groups * ((home + step) % 2)
-            pairs.append((home * groups + h, slot * groups + h))
-    return pairs
+            expected = expected + 1 - is_me(home, h).astype(jnp.int32)
+    pl.semaphore_wait(pltpu.get_barrier_semaphore(), expected)
+
+    def to_core(k, row):
+        i = order[k]
+        n = row * LINE + i
+        return remote(
+            part_ref.at[row * 2 + (1 - c), i], held.at[i, row], c_s.at[n], c_r.at[n], me.beside
+        )
+
+    def first_y(k):
+        i = order[k]
+        return remote(held.at[i, 1 - y, :, 0], first_a.at[i], y_s.at[i], y_r.at[i], me.over)
+
+    def first_x(k):
+        i = order[k]
+        return remote(held.at[i, :, 1 - x, 1], first_b.at[i], x_s.at[i], x_r.at[i], me.across)
+
+    def second_x(k):
+        i = order[k]
+        n = LINE + i
+        return remote(held.at[i, y, 1 - x, 0], second_a.at[i], x_s.at[n], x_r.at[n], me.across)
+
+    def second_y(k):
+        i = order[k]
+        n = LINE + i
+        return remote(held.at[i, 1 - y, x, 1], second_b.at[i], y_s.at[n], y_r.at[n], me.over)
+
+    def upward(k):
+        i = order[k]
+        return remote(held.at[i, y, x], line.at[0, i], z_s.at[i], z_r.at[i], me.up)
+
+    def downward(k):
+        i = order[k]
+        n = LINE + i
+        return remote(held.at[i, y, x], line.at[1, i], z_s.at[n], z_r.at[n], me.down)
+
+    rows, columns = sum_ref.shape[1:]
+
+    def begin(k):
+        i = order[k]
+        for row in range(2):
+            arrived(held.at[i, row], c_s.at[row * LINE + i], c_r.at[row * LINE + i], me.beside)
+            add_into(
+                held.at[i, row], [held.at[i, row], part_ref.at[row * 2 + c, i]], (SIDES, 2, rows, columns)
+            )
+        first_y(k).start()
+        first_x(k).start()
+
+    def middle(k):
+        i = order[k]
+        arrived(first_a.at[i], y_s.at[i], y_r.at[i], me.over)
+        for side in range(SIDES):
+            block = held.at[i, y, side, 0]
+            add_into(block, [block, first_a.at[i, side]], (rows, columns))
+        second_x(k).start()
+        arrived(first_b.at[i], x_s.at[i], x_r.at[i], me.across)
+        for row in range(2):
+            block = held.at[i, row, x, 1]
+            add_into(block, [block, first_b.at[i, row]], (rows, columns))
+        second_y(k).start()
+
+    def end(k):
+        i = order[k]
+        n = LINE + i
+        last = k == LINE - 1
+        arrived(second_a.at[i], x_s.at[n], x_r.at[n], me.across)
+        arrived(second_b.at[i], y_s.at[n], y_r.at[n], me.over)
+        for part, other in enumerate((second_a, second_b)):
+            block = held.at[i, y, x, part]
+            add_into(sum_ref.at[part] if last else block, [block, other.at[i]], (rows, columns))
+        target = sum_ref if last else held.at[i, y, x]
+
+        def below():
+            arrived(line.at[0, i], z_s.at[i], z_r.at[i], me.up)
+            add_into(target, [target, line.at[0, i]], (2, rows, columns))
+
+        def above():
+            arrived(line.at[1, i], z_s.at[n], z_r.at[n], me.up)
+            add_into(target, [target, line.at[1, i]], (2, rows, columns))
+
+        pl.when((i >= z) & me.not_first)(below)
+        pl.when((i <= z) & me.not_last)(above)
+        if not last:
+            pl.when(i > z)(lambda: upward(k).start())
+            pl.when(i < z)(lambda: downward(k).start())
+
+    def home_copy(m, p):
+        n = m * SIDE + p
+        return remote(
+            y_ref.at[m, p], tokens_ref.at[m, here], home_s.at[n], home_r.at[m * 2 + here // groups], {"seq": homes[p]}
+        )
+
+    def home_here(m, p):
+        return pltpu.make_async_copy(y_ref.at[m, p], tokens_ref.at[m, here], own_sem.at[m])
+
+    def grad_copy(m, p, h):
+        n = (m * SIDE + p) * groups + h
+        return remote(
+            dx_ref.at[m, h, p], grads_ref.at[m, here], grad_s.at[n], grad_r.at[m * slots + here],
+            {"seq": homes[p], "head": h},
+        )
+
+    def grad_here(m, p, h):
+        return pltpu.make_async_copy(dx_ref.at[m, h, p], grads_ref.at[m, here], own_sem.at[micros + m])
+
+    def slot_of(other, j):
+        return lax.rem(other - z + groups, groups) + groups * j
+
+    far_head, near_head = (1 - y) * 2 + c, y * 2 + (1 - c)
+    last_head = (1 - y) * 2 + (1 - c)
+
+    def far(m, j):
+        n, block = m * 2 + j, tokens_ref.at[m, slot_of(head, j)]
+        return remote(block, block, over_s.at[n], over_r.at[n], me.over)
+
+    def near(m, j):
+        n, block = m * 2 + j, tokens_ref.at[m, slot_of(head, j)]
+        return remote(block, block, near_s.at[n], near_r.at[n], me.beside)
+
+    def passed(m, j):
+        n, block = m * 2 + j, tokens_ref.at[m, slot_of(far_head, j)]
+        return remote(block, block, pass_s.at[n], pass_r.at[n], me.beside)
+
+    for k in range(LINE):
+        for row in range(2):
+            to_core(k, row).start()
+    for m in range(micros):
+        for p, home in enumerate(homes):
+            pl.when(home != here)(lambda m=m, p=p: home_copy(m, p).start())
+            pl.when(home == here)(lambda m=m, p=p: home_here(m, p).start())
+            for h in range(groups):
+                same = is_me(home, h)
+                pl.when(jnp.logical_not(same))(lambda m=m, p=p, h=h: grad_copy(m, p, h).start())
+                pl.when(same)(lambda m=m, p=p, h=h: grad_here(m, p, h).start())
+    for k in range(LINE):
+        begin(k)
+        if k >= 1:
+            middle(k - 1)
+        if k >= 2:
+            end(k - 2)
+    middle(LINE - 1)
+    end(LINE - 2)
+    for m in range(micros):
+        for p, home in enumerate(homes):
+            pl.when(home == here)(lambda m=m, p=p: home_here(m, p).wait())
+        for j in range(2):
+            slot = slot_of(head, j)
+            pl.when(slot != here)(
+                lambda m=m, j=j, slot=slot: arrived(
+                    tokens_ref.at[m, slot], home_s.at[m * 2 + j], home_r.at[m * 2 + j], {"seq": slot}
+                )
+            )
+            far(m, j).start()
+            near(m, j).start()
+    end(LINE - 1)
+    for m in range(micros):
+        for j in range(2):
+            n = m * 2 + j
+            arrived(tokens_ref.at[m, slot_of(far_head, j)], over_s.at[n], over_r.at[n], me.over)
+            passed(m, j).start()
+    for m in range(micros):
+        for j in range(2):
+            n = m * 2 + j
+            arrived(tokens_ref.at[m, slot_of(near_head, j)], near_s.at[n], near_r.at[n], me.beside)
+            arrived(tokens_ref.at[m, slot_of(last_head, j)], pass_s.at[n], pass_r.at[n], me.beside)
+        for slot in range(slots):
+            n = m * slots + slot
+            pl.when(jnp.logical_not(is_me(slot, senders[slot])))(
+                lambda m=m, n=n, slot=slot: arrived(
+                    grads_ref.at[m, slot], grad_s.at[0], grad_r.at[n], {"seq": slot, "head": senders[slot]}
+                )
+            )
+    for m in range(micros):
+        for p, home in enumerate(homes):
+            pl.when(home != here)(lambda m=m, p=p: home_copy(m, p).wait_send())
+            for h in range(groups):
+                same = is_me(home, h)
+                pl.when(jnp.logical_not(same))(lambda m=m, p=p, h=h: grad_copy(m, p, h).wait_send())
+                pl.when(same)(lambda m=m, p=p, h=h: grad_here(m, p, h).wait())
+        for j in range(2):
+            far(m, j).wait_send()
+            near(m, j).wait_send()
+            passed(m, j).wait_send()
+    for k in range(LINE):
+        for row in range(2):
+            to_core(k, row).wait_send()
+        for copy in (first_y, first_x, second_x, second_y):
+            copy(k).wait_send()
+        if k < LINE - 1:
+            i = order[k]
+            pl.when(i > z)(lambda k=k: upward(k).wait_send())
+            pl.when(i < z)(lambda k=k: downward(k).wait_send())
+
+
+def finish(part, y, dx, slots, groups, number):
+    columns = part.shape[-1]
+    micros, _, piece, model = y.shape
+    rows = part.shape[-2]
+    dma = pltpu.SemaphoreType.DMA
+    vmem = pltpu.VMEM
+    part = part.reshape(groups, LINE, SIDES, 2, rows, columns)
+    return pl.pallas_call(
+        functools.partial(finish_kernel, slots, groups, micros),
+        out_shape=(
+            jax.ShapeDtypeStruct((2, rows, columns), F32),
+            jax.ShapeDtypeStruct((micros, slots, piece, model), BF16),
+            jax.ShapeDtypeStruct((micros, slots, piece, dx.shape[-1]), BF16),
+        ),
+        in_specs=[pl.BlockSpec(memory_space=pltpu.VMEM)] * 3,
+        out_specs=(pl.BlockSpec(memory_space=pltpu.VMEM),) + (pl.BlockSpec(memory_space=pl.ANY),) * 2,
+        scratch_shapes=[
+            vmem((LINE, 2, SIDES, 2, rows, columns), BF16),
+            vmem((LINE, SIDES, rows, columns), BF16),
+            vmem((LINE, 2, rows, columns), BF16),
+            vmem((LINE, rows, columns), BF16),
+            vmem((LINE, rows, columns), BF16),
+            vmem((2, LINE, 2, rows, columns), BF16),
+        ]
+        + [dma((2 * LINE,))] * 8
+        + [dma((2 * micros,))] * 8
+        + [dma((2 * groups * micros,)), dma((slots * micros,)), dma((2 * micros,))],
+        compiler_params=params(collective_id=number, has_side_effects=True),
+        cost_estimate=cost(0, 3000000 * 40),
+        name="finish",
+    )(part, y, dx)
+
+
+def order_kernel(micros, index_ref, *refs):
+    inputs, outputs = refs[: 2 * micros], refs[2 * micros :]
+    for n, out in enumerate(outputs):
+        for m in range(micros):
+            out[m, 0] = inputs[n * micros + m][0, 0]
+
+
+def in_order(arrays, index):
+    micros, slots = arrays[0].shape[:2]
+
+    def source(m):
+        return lambda i, ix: (m, ix[m, i], 0, 0)
+
+    return pl.pallas_call(
+        functools.partial(order_kernel, micros),
+        out_shape=tuple(jax.ShapeDtypeStruct(a.shape, a.dtype) for a in arrays),
+        grid_spec=pltpu.PrefetchScalarGridSpec(
+            num_scalar_prefetch=1,
+            grid=(slots,),
+            in_specs=[
+                pl.BlockSpec((1, 1, *a.shape[2:]), source(m)) for a in arrays for m in range(micros)
+            ],
+            out_specs=tuple(
+                pl.BlockSpec((micros, 1, *a.shape[2:]), lambda i, ix: (0, i, 0, 0)) for a in arrays
+            ),
+        ),
+        compiler_params=params(),
+        cost_estimate=cost(0, 4 * sum(a.size for a in arrays)),
+        name="in_order",
+    )(index, *[a for a in arrays for _ in range(micros)])
 
 
 def fits(mesh):
@@ -920,9 +1472,29 @@
         ],
         axis=1,
     )
-    gathered = lax.all_gather(packed, grid, axis=0).reshape(slots, groups, own_rows, -1)
-    vectors = gathered[..., cuts[-1] : cuts[-1] + lots].reshape(slots, groups, -1).astype(F32)
-    weights = jnp.transpose(gathered, (1, 0, 2, 3)).reshape(groups, model, -1)
+    pieces = jnp.stack(
+        [
+            jnp.stack(
+                [
+                    lax.dynamic_index_in_dim(array[m], inverse[m][slot], 0, keepdims=False)
+                    for array in (tokens, cot_tokens)
+                    for m in range(micros)
+                ]
+            )
+            for slot in (
+                (head - here // 2) % groups + groups * ((here + step) % 2) for step in range(2)
+            )
+        ]
+    )
+    weights, rows_all = gather_all(packed.reshape(2, own_rows // 2, -1), pieces, slots, groups, 1)
+    rows = per * piece
+    rows_all = rows_all.reshape(2 * micros, rows, model)
+    rows_in, cot_rows = rows_all[:micros], rows_all[micros:]
+
+    weights = weights.reshape(groups, slots, own_rows, -1)
+    vectors = jnp.transpose(weights[..., cuts[-1] : cuts[-1] + lots], (1, 0, 2, 3))
+    vectors = vectors.reshape(slots, groups, -1).astype(F32)
+    weights = weights.reshape(groups, model, -1)
     q_len = heads * HEAD_DIM // slots
     offsets = [0, q_len, 2 * q_len]
     for _ in range(7):
@@ -941,30 +1513,8 @@
         [plain(2), plain(3), plain(4), plain(6), plain(7), plain(8), jnp.zeros((2, model), F32)], axis=0
     )
 
-    def slot_of(step):
-        return (head - here // 2) % groups + groups * ((here + step) % 2)
-
-    def to_slots(array):
-        arrived = []
-        for step in range(2):
-            slot = slot_of(step)
-            out = jnp.stack(
-                [
-                    lax.dynamic_index_in_dim(array[m], inverse[m][slot], 0, keepdims=False)
-                    for m in range(micros)
-                ]
-            )
-            arrived.append(lax.ppermute(out, grid, by_step(step, groups, slots)))
-        swap = here // groups == 1
-        first = jnp.where(swap, arrived[1], arrived[0])
-        second = jnp.where(swap, arrived[0], arrived[1])
-        return jnp.concatenate([first, second], axis=1)
-
-    rows_in = to_slots(tokens)
-    cot_rows = to_slots(cot_tokens)
-
-    def across_heads(array):
-        return lax.all_to_all(array, "head", split_axis=0, concat_axis=0, tiled=True)
+    qkv = project(rows_in.reshape(micros * rows, model), weights, bias_qkv)
+    qkv = across_heads(qkv, 3).reshape(groups, micros, rows, 3 * width)
 
     got_prev, after = [], None
     for m in range(micros):
@@ -973,26 +1523,28 @@
             send, _ = lax.optimization_barrier((send, after))
         got = lax.all_to_all(send, "seq", split_axis=0, concat_axis=0, tiled=True)
         got_prev.append(got)
-        after = got
-
-    rows = per * piece
-    qkv = project(rows_in.reshape(micros * rows, model), weights, bias_qkv)
-    qkv = across_heads(qkv).reshape(groups, micros, rows, 3 * width)
+        after = (got, qkv)
 
     logits, grad_logits = None, None
     kept, sums_own, sums_rows, sums_up, returned = [], [], [], [], []
     for m in range(micros):
         logits, attend, context = attention_forward(info[m], qkv, got_prev[m], m, micros, logits)
-        context_rows = across_heads(context)
+        context_rows = across_heads(context, 4)
         y, dz, dcon, h1, act, b1, b2, b0, sums, dbup = row_work(
             cuts, context_rows, rows_in[m], cot_rows[m], weights, bias_up, row_vectors
         )
-        dcontext = across_heads(dcon)
+        dcontext = across_heads(dcon, 4)
         send, dqkv, own = attention_backward(
             info[m], qkv, attend, context, dcontext, cot_square, m
         )
+        if m:
+            send, _ = lax.optimization_barrier((send, first_grads))
         got = lax.all_to_all(send, "seq", split_axis=0, concat_axis=0, tiled=True)
-        dqkv = across_heads(dqkv)
+        dqkv = across_heads(dqkv, 5)
+        if m:
+            dqkv, _ = lax.optimization_barrier((dqkv, first_grads))
+        else:
+            first_grads = got
         dx = input_grad(dqkv, weights, dz)
         kept.append((rows_in[m], b0, h1, b2, dqkv, context_rows, b1, act))
         sums_own.append(own)
@@ -1000,12 +1552,6 @@
         sums_up.append(dbup)
         returned.append((y, dx))
         grad_logits = place_blocks(got, m, micros, dealing[m], grad_logits)
-
-    families = list(zip(*kept))
-    part = weight_grads(cuts, families[:4], families[4:])
-    part = lax.psum_scatter(part, "head", scatter_dimension=0, tiled=True).reshape(slots, own_rows, -1)
-    part = lax.all_to_all(part, "seq", split_axis=0, concat_axis=0, tiled=True)
-    part = part.astype(F32).sum(axis=0)
 
     own = sums_own[0]
     rows_sum = sums_rows[0]
@@ -1036,40 +1582,31 @@
         ],
         axis=2,
     ).reshape(slots * groups, -1)
-    out_vectors = lax.all_to_all(out_vectors, grid, split_axis=0, concat_axis=0, tiled=True).sum(axis=0)
+    out_vectors = jnp.pad(out_vectors, ((0, 0), (0, lots * own_rows - out_vectors.shape[1])))
+    out_vectors = out_vectors.astype(BF16).reshape(slots, groups, own_rows, lots)
+    out_vectors = jnp.transpose(out_vectors, (1, 0, 2, 3)).reshape(groups, model, lots)
+    out_vectors = jnp.pad(out_vectors, ((0, 0), (0, 0), (0, 128 - lots)))
+
+    families = list(zip(*kept))
+    part = weight_grads(cuts, families[:4], families[4:], out_vectors)
+    ys = jnp.stack([y for y, _ in returned]).reshape(micros, per, piece, model)
+    dxs = jnp.stack([dx for _, dx in returned]).reshape(micros, groups, per, piece, -1)
+    part = part.reshape(groups, slots, 2, own_rows // 2, -1)
+    part, all_y, all_dx = finish(part, ys, dxs, slots, groups, 7)
+    part = part.reshape(own_rows, -1)
+    out_tokens, grad_tokens = in_order((all_y, all_dx), dealing)
+    out_vectors = part[:, cuts[-1] : cuts[-1] + lots].reshape(-1)
 
     def vector_out(i):
         return out_vectors[offsets[i] : offsets[i + 1]]
 
-    sent = []
-    for m in range(micros):
-        y, dx = returned[m]
-        sent.append(jnp.stack([y.reshape(per, piece, model), dx.reshape(per, piece, model)], axis=1))
-    sent = jnp.stack(sent, axis=1)
-    back = []
-    for step in range(2):
-        block = lax.dynamic_index_in_dim(sent, (here // groups + step) % 2, 0, keepdims=False)
-        pairs = [(b, a) for a, b in by_step(step, groups, slots)]
-        back.append(lax.ppermute(block, grid, pairs))
-    back = jnp.stack(back)
-    all_y = lax.all_gather(back[:, :, 0], "head", axis=0).reshape(-1, micros, piece, model)
-    dx_send = back[:, :, 1].reshape(2, micros, piece, groups, -1)
-    dx_send = jnp.transpose(dx_send, (3, 0, 1, 2, 4))
-    all_dx = across_heads(dx_send).reshape(-1, micros, piece, model // groups)
-    out_tokens, grad_tokens = [], []
-    for m in range(micros):
-        slot = dealing[m]
-        which = ((slot + here // 2) % groups) * 2 + (slot // groups + here) % 2
-        out_tokens.append(jnp.take(all_y[:, m], which, axis=0, mode="clip"))
-        grad_tokens.append(jnp.take(all_dx[:, m], which, axis=0, mode="clip"))
-
     def columns(start, count):
         return part[:, start : start + count]
 
     return (
-        jnp.stack(out_tokens),
+        out_tokens,
         jnp.transpose(logits, (0, 2, 1, 3))[:, None],
-        jnp.stack(grad_tokens),
+        grad_tokens,
         jnp.transpose(grad_logits, (0, 1, 3, 2, 4)),
         columns(0, width),
         vector_out(0).reshape(heads, -1),

time: 971 us -> 694 us (0.71)
  Pallas kernels: 167 us -> 538 us
  waiting for transfers between devices: 348 us -> 56 us
  blocking collectives: 263 us -> 0 us
  local copies, waits for them, and re-layouts: 69 us -> 27.4 us
  starting transfers between devices: 73 us -> 44.4 us
  between operations: 26.1 us -> 13.1 us
    pallas_call x2 -> x12, Pallas kernels: 9.96 us -> 380 us  [the longest x1 148 us: gather_all(): pl.pallas_call(functools.partial(gather_kernel, slots, groups), out_shape...]
    ppermute x6 -> x0, waiting for transfers between devices: 290 us -> none  [the longest x4 271 us: to_slots(): arrived.append(lax.ppermute(out, grid, by_step(step, groups, slots)))]
    all_to_all x4 -> x0, blocking collectives: 263 us -> none  [the longest x2 221 us: on_device(): got = lax.all_to_all(send, 'seq', split_axis=0, concat_axis=0, tiled=True)]
    all_to_all x2 -> x4, waiting for transfers between devices: 0.01 us -> 56 us  [on_device(): got = lax.all_to_all(send, 'seq', split_axis=0, concat_axis=0, tiled=True)]
    all_to_all x8 -> x0, waiting for transfers between devices: 42.1 us -> none  [the longest x6 18.4 us: across_heads(): lax.all_to_all(array, 'head', split_axis=0, concat_axis=0, tiled=True)]
    all_to_all x8 -> x0, starting transfers between devices: 33.8 us -> none  [the longest x6 23 us: across_heads(): lax.all_to_all(array, 'head', split_axis=0, concat_axis=0, tiled=True)]
    all_to_all x2 -> x4, starting transfers between devices: 16.3 us -> 44.4 us  [on_device(): got = lax.all_to_all(send, 'seq', split_axis=0, concat_axis=0, tiled=True)]
    ppermute x6 -> x0, starting transfers between devices: 22.6 us -> none  [the longest x4 12.1 us: to_slots(): arrived.append(lax.ppermute(out, grid, by_step(step, groups, slots)))]
  transfers between devices with their start and end apart: 19 -> 4, of which waited for: 10 -> 2; matrix products, arithmetic and copies ran while one was open for 7% -> 5% of each run, Pallas kernels for 16% -> 76%
where the time goes in v2:
time: 694 us; the launch traced here: 688 us
  Pallas kernels  538 us (78%)
  waiting for transfers between devices  56 us (8%)
  starting transfers between devices  44.4 us (6%)
  local copies, waits for them, and re-layouts  27.4 us (4%)
  between operations  13.1 us (2%)
  other arithmetic  8.65 us (1%)
    pallas_call x1, Pallas kernels, gather_all(): pl.pallas_call(functools.partial(gather_kernel, slots, groups), out_shape...  148 us
    pallas_call x1, Pallas kernels, finish(): pl.pallas_call(functools.partial(finish_kernel, slots, groups, micros), o...  118 us
    pallas_call x7, Pallas kernels, across_heads(): pl.pallas_call(functools.partial(cross_kernel, groups), out_shape=jax.Sha...  97.9 us
    all_to_all x4, waiting for transfers between devices, on_device(): got = lax.all_to_all(send, 'seq', split_axis=0, concat_axis=0, tiled=True)  56 us
    all_to_all x4, starting transfers between devices, on_device(): got = lax.all_to_all(send, 'seq', split_axis=0, concat_axis=0, tiled=True)  44.4 us
    pallas_call x2, Pallas kernels, attention_backward(): pl.pallas_call(functools.partial(backward_kernel, heads), out_shape=(jax....  36.6 us
    pallas_call x2, Pallas kernels, attention_forward(): pl.pallas_call(functools.partial(forward_kernel, heads), out_shape=(jax.S...  36.1 us
    pallas_call x2, Pallas kernels, row_work(): pl.pallas_call(functools.partial(rows_kernel, cuts), out_shape=(shape((ro...  33.1 us
  transfers between devices with their start and end apart: 4, of which 2 were waited for; matrix products, arithmetic and copies ran while one was open for 5% of the time, Pallas kernels for 76%

profile of v2, /device:TPU:15, one launch (start us, length us, event | category | flops | bytes accessed | tf_op | source)
XLA Modules:
  0.0 687.8 jit_solution(2544285249178343365)
XLA Ops:
  0.7 0.8 slice_bitcast_fusion.2
  1.4 0.6 select_reduce_fusion.1.index_ref
  2.0 7.7 %pick_blocks.2 = bf16[8,3,112,896]{3,2,1,0:T(8,128)(2,1)} custom-call(s32[8]{0:T(128)} %select_reduce_fusion.1.index_ref, bf16[2,8,3,112,896]{4,3,2,1,0:T(8,128)(2,1)} %bitcast.127), custom_call_target="tpu_custom_call" | custom-call | bytes 96337 | tf_op jit(solution)/shard_map/pick_blocks/pallas_call | solution.py:428
  9.7 5.8 all-to-all-start
  15.6 0.6 fusion.13
  21.6 8.0 %pick_blocks.3 = bf16[8,3,112,896]{3,2,1,0:T(8,128)(2,1)} custom-call(s32[8]{0:T(128)} %copy-done.19, bf16[2,8,3,112,896]{4,3,2,1,0:T(8,128)(2,1)} %bitcast.128), custom_call_target="tpu_custom_call" | custom-call | bytes 96337 | tf_op jit(solution)/shard_map/pick_blocks/pallas_call | solution.py:428
  32.9 0.9 concatenate.34
  34.0 1.6 copy-done.2
  36.1 1.2 pad_maximum_fusion.piece_ref
  37.3 147.5 %gather_all.1 = (bf16[4,8,2,48,2432]{4,3,2,1,0:T(8,128)(2,1)}, bf16[4,2,112,768]{3,2,1,0:T(8,128)(2,1)}) custom-call(bf16[2,48,2432]{2,1,0:T(8,128)(2,1)} %bitcast.138, bf16[2,4,112,768]{3,2,1,0:T(8,128)(2,1)} %pad_maximum_fusion.piece_ref), custom_call_target="tpu_custom_call" | custom-call | bytes 1200000 | tf_op jit(solution)/shard_map/gather_all/pallas_call | solution.py:1064
  184.8 2.0 slice.188
  186.8 1.3 convert_bitcast_fusion
  188.1 0.8 reshape.200
  189.5 0.6 pad_maximum_fusion.3.b_ref
  190.1 6.4 project.1.x_ref
  196.5 28.8 %across_heads.7 = bf16[4,448,576]{2,1,0:T(8,128)(2,1)} custom-call(bf16[4,448,576]{2,1,0:T(8,128)(2,1)} %project.1.x_ref), custom_call_target="tpu_custom_call" | custom-call | bytes 412876 | tf_op jit(solution)/shard_map/across_heads/pallas_call | solution.py:880
  225.3 23.5 %all-to-all-start.1 = ((bf16[8,3,112,896]{3,2,1,0:T(8,128)(2,1)}), bf16[8,3,112,896]{3,2,1,0:T(8,128)(2,1)}, u32[]{:S(2)}, u32[]{:S(2)}) async-start(bf16[8,3,112,896]{3,2,1,0:T(8,128)(2,1)} %pick_blocks.3), calls=%async_computation.1 | async-start | bytes 9633792 | tf_op jit(solution)/shard_map/all_to_all | solution.py:1524
  252.2 0.7 reshape.194.bup_ref
  254.2 0.6 concatenate.36.vec_ref
  254.8 0.6 constant_dynamic-slice_fusion.1
  255.4 1.2 pad_add_fusion.info_ref
  256.6 1.1 fusion.8
  257.8 18.1 %attention_forward.2 = (bf16[2,3,896,896]{3,2,1,0:T(8,128)(2,1)}, bf16[8,3,112,896]{3,2,1,0:T(8,128)(2,1)}, bf16[4,224,192]{2,1,0:T(8,128)(2,1)}) custom-call(s32[2]{0:T(128)} %pad_add_fusion.info_ref, bf16[4,2,224,576]{3,2,1,0:T(8,128)(2,1)} %bitcast.121, bf16[8,3,112,896]{3,2,1,0:T(8,128)(2,1)} %all-to-all-done.prev_ref), custom_call_target="tpu_custom_call" | custom-call | flops 24662508 | bytes 144506 | tf_op jit(solution)/shard_map/attention_forward/pallas_call | solution.py:540
  275.8 8.8 %across_heads.8.con_ref.refs_10_ = bf16[4,224,192]{2,1,0:T(8,128)(2,1)} custom-call(bf16[4,224,192]{2,1,0:T(8,128)(2,1)} %get-tuple-element.64.x_ref.context_ref), custom_call_target="tpu_custom_call" | custom-call | bytes 68812 | tf_op jit(solution)/shard_map/across_heads/pallas_call | solution.py:880
  284.6 16.5 %row_work.2 = (bf16[224,768]{1,0:T(8,128)(2,1)}, f32[224,768]{1,0:T(8,128)}, bf16[4,224,192]{2,1,0:T(8,128)(2,1)}, bf16[224,768]{1,0:T(8,128)(2,1)}, bf16[4,224,...) custom-call(bf16[4,224,192]{2,1,0:T(8,128)(2,1)} %across_heads.8.con, ...), custom_call_target="tpu_custom_call" | custom-call | flops 52848232 | bytes 149422 | tf_op jit(solution)/shard_map/row_work/pallas_call | solution.py:737
  301.2 8.8 %across_heads.9.dcon_ref = bf16[4,224,192]{2,1,0:T(8,128)(2,1)} custom-call(bf16[4,224,192]{2,1,0:T(8,128)(2,1)} %get-tuple-element.65.x_ref), custom_call_target="tpu_custom_call" | custom-call | bytes 68812 | tf_op jit(solution)/shard_map/across_heads/pallas_call | solution.py:880
  310.0 18.3 %attention_backward.2 = (bf16[8,3,112,896]{3,2,1,0:T(8,128)(2,1)}, bf16[4,224,576]{2,1,0:T(8,128)(2,1)}, f32[2,192]{1,0:T(2,128)}) custom-call(s32[2]{0:T(128)} %pad_add_fusion.info_ref, bf16[4,2,224,576]{3,2,1,0:T(8,128)(2,1)} %bitcast.122, bf16[8,3,112,896]{3,2,1,0:T(8,128)(2,1)} %get-tuple-element.63.attend_ref, ...), custom_call_target="tpu_custom_call" | custom-call | flops 49325016 | bytes 144506 | tf_op jit(solution)/shard_map/attention_backward/pallas_call | solution.py:623
  328.3 23.8 %all-to-all-done.1.prev_ref = bf16[8,3,112,896]{3,2,1,0:T(8,128)(2,1)} async-done(((bf16[8,3,112,896]{3,2,1,0:T(8,128)(2,1)}), bf16[8,3,112,896]{3,2,1,0:T(8,128)(2,1)}, u32[]{:S(2)}, u32[]{:S(2)}) %all-to-all-start.1) | async-done | bytes 4816928 | tf_op jit(solution)/shard_map/all_to_all | solution.py:1524
  352.1 7.7 %all-to-all-start.2 = ((bf16[8,3,112,896]{3,2,1,0:T(8,128)(2,1)}), bf16[8,3,112,896]{3,2,1,0:T(8,128)(2,1)}, u32[]{:S(2)}, u32[]{:S(2)}) async-start(bf16[8,3,112,896]{3,2,1,0:T(8,128)(2,1)} %get-tuple-element.85), calls=%async_computation.2 | async-start | bytes 9633792 | tf_op jit(solution)/shard_map/all_to_all | solution.py:1542
  359.8 1.2 pad_add_fusion.1.info_ref
  361.1 18.0 %attention_forward.3 = (bf16[2,3,896,896]{3,2,1,0:T(8,128)(2,1)}, bf16[8,3,112,896]{3,2,1,0:T(8,128)(2,1)}, bf16[4,224,192]{2,1,0:T(8,128)(2,1)}) custom-call(s32[2]{0:T(128)} %pad_add_fusion.1.info_ref, bf16[4,2,224,576]{3,2,1,0:T(8,128)(2,1)} %bitcast.123, bf16[8,3,112,896]{3,2,1,0:T(8,128)(2,1)} %all-to-all-done.1.prev_ref, ...), custom_call_target="tpu_custom_call", output_to_operand_aliasing={{0}: (3, {})} | custom-call | flops 24662508 | bytes 144506 | tf_op jit(solution)/shard_map/attention_forward/pallas_call | solution.py:540
  379.1 8.9 %across_heads.10.con_ref.refs_11_ = bf16[4,224,192]{2,1,0:T(8,128)(2,1)} custom-call(bf16[4,224,192]{2,1,0:T(8,128)(2,1)} %get-tuple-element.70.x_ref.context_ref), custom_call_target="tpu_custom_call" | custom-call | bytes 68812 | tf_op jit(solution)/shard_map/across_heads/pallas_call | solution.py:880
  388.0 16.6 %row_work.3 = (bf16[224,768]{1,0:T(8,128)(2,1)}, f32[224,768]{1,0:T(8,128)}, bf16[4,224,192]{2,1,0:T(8,128)(2,1)}, bf16[224,768]{1,0:T(8,128)(2,1)}, bf16[4,224,...) custom-call(bf16[4,224,192]{2,1,0:T(8,128)(2,1)} %across_heads.10.co, ...), custom_call_target="tpu_custom_call" | custom-call | flops 52848232 | bytes 149422 | tf_op jit(solution)/shard_map/row_work/pallas_call | solution.py:737
  404.5 8.8 %across_heads.11.dcon_ref = bf16[4,224,192]{2,1,0:T(8,128)(2,1)} custom-call(bf16[4,224,192]{2,1,0:T(8,128)(2,1)} %get-tuple-element.71.x_ref), custom_call_target="tpu_custom_call" | custom-call | bytes 68812 | tf_op jit(solution)/shard_map/across_heads/pallas_call | solution.py:880
  413.4 18.3 %attention_backward.3 = (bf16[8,3,112,896]{3,2,1,0:T(8,128)(2,1)}, bf16[4,224,576]{2,1,0:T(8,128)(2,1)}, f32[2,192]{1,0:T(2,128)}) custom-call(s32[2]{0:T(128)} %pad_add_fusion.1.info_ref, bf16[4,2,224,576]{3,2,1,0:T(8,128)(2,1)} %bitcast.124, bf16[8,3,112,896]{3,2,1,0:T(8,128)(2,1)} %get-tuple-element.69.attend_ref, ...), custom_call_target="tpu_custom_call" | custom-call | flops 49325016 | bytes 144506 | tf_op jit(solution)/shard_map/attention_backward/pallas_call | solution.py:623
  431.7 32.2 %all-to-all-done.2.x_ref = bf16[8,3,112,896]{3,2,1,0:T(8,128)(2,1)} async-done(((bf16[8,3,112,896]{3,2,1,0:T(8,128)(2,1)}), bf16[8,3,112,896]{3,2,1,0:T(8,128)(2,1)}, u32[]{:S(2)}, u32[]{:S(2)}) %all-to-all-start.2) | async-done | bytes 4816928 | tf_op jit(solution)/shard_map/all_to_all | solution.py:1542
  463.9 7.4 %all-to-all-start.3 = ((bf16[8,3,112,896]{3,2,1,0:T(8,128)(2,1)}), bf16[8,3,112,896]{3,2,1,0:T(8,128)(2,1)}, u32[]{:S(2)}, u32[]{:S(2)}) async-start(bf16[8,3,112,896]{3,2,1,0:T(8,128)(2,1)} %get-tuple-element.101), calls=%async_computation.3 | async-start | bytes 9633792 | tf_op jit(solution)/shard_map/all_to_all | solution.py:1542
  471.3 17.3 %across_heads.12.refs_8_.dqkv_ref = bf16[4,224,576]{2,1,0:T(8,128)(2,1)} custom-call(bf16[4,224,576]{2,1,0:T(8,128)(2,1)} %get-tuple-element.83.x_ref), custom_call_target="tpu_custom_call" | custom-call | bytes 206438 | tf_op jit(solution)/shard_map/across_heads/pallas_call | solution.py:880
  488.8 5.1 input_grad.2
  495.4 0.9 reshape.196
  496.4 1.0 pad.20.vector_ref
  497.4 16.4 %across_heads.13.refs_9_.dqkv_ref = bf16[4,224,576]{2,1,0:T(8,128)(2,1)} custom-call(bf16[4,224,576]{2,1,0:T(8,128)(2,1)} %get-tuple-element.84.x_ref), custom_call_target="tpu_custom_call" | custom-call | bytes 206438 | tf_op jit(solution)/shard_map/across_heads/pallas_call | solution.py:880
  513.9 5.1 input_grad.3
  518.9 14.8 %weight_grads.1 = bf16[4,768,2432]{2,1,0:T(8,128)(2,1)} custom-call(bf16[4,768,128]{2,1,0:T(8,128)(2,1)} %pad.20.vector_ref, bf16[224,768]{1,0:T(8,128)(2,1)} %bitcast.136, bf16[224,768]{1,0:T(8,128)(2,1)} %bitcast.134, bf16[224,768]{1,0:T(8,128)(2,1)} %get-tuple-element.77.refs_2_, bf16[224,768]{1,0:T(8,128)(2,1)} %get-tuple-element.78.refs_3_, ...), custom_call_target="tpu_custom_call" | custom-call | flops 63417876 | bytes 141557 | tf_op jit(solution)/shard_map/weight_grads/pallas_call | solution.py:821
  533.8 0.9 pad_maximum_fusion.2.y_ref
  534.8 0.3 copy-done.4
  535.1 1.1 pad_maximum_fusion.1.dx_ref
  536.2 117.7 %finish.1 = (f32[2,48,2432]{2,1,0:T(8,128)}, bf16[2,8,112,768]{3,2,1,0:T(8,128)(2,1)}, bf16[2,8,112,192]{3,2,1,0:T(8,128)(2,1)}) custom-call(bf16[4,4,2,2,48,2432]{5,4,3,2,1,0:T(8,128)(2,1)} %bitcast.120, bf16[2,2,112,768]{3,2,1,0:T(8,128)(2,1)} %pad_maximum_fusion.2.y_ref, bf16[2,4,2,112,192]{4,3,2,1,0:T(8,128)(2,1)} %pad_maximum_fusion.1.dx_ref), custom_call_target="tpu_custom_call" | custom-call | bytes 1200000 | tf_op jit(solution)/shard_map/finish/pallas_call | solution.py:1333
  653.9 0.9 fusion.9
  654.8 0.6 slice.231
  655.4 0.6 slice.229
  656.0 0.6 slice.227
  656.6 0.6 slice.222
  657.2 0.6 slice.220
  657.8 0.6 slice.218
  658.4 0.7 reshape.199
  659.0 1.9 slice_bitcast_fusion.1
  660.9 0.7 copy.70
  661.6 7.1 %in_order.1 = (bf16[2,8,112,768]{3,2,1,0:T(8,128)(2,1)}, bf16[2,8,112,192]{3,2,1,0:T(8,128)(2,1)}) custom-call(s32[2,8]{1,0:T(2,128)} %index_ref.1, bf16[2,8,112,768]{3,2,1,0:T(8,128)(2,1)} %get-tuple-element.95.refs_0_.refs_1_, bf16[2,8,112,768]{3,2,1,0:T(8,128)(2,1)} %get-tuple-element.95.refs_0_.refs_1_, ...), custom_call_target="tpu_custom_call" | custom-call | bytes 68812 | tf_op jit(solution)/shard_map/in_order/pallas_call | solution.py:1372
  668.7 2.2 copy.69
  670.9 7.8 %place_blocks.2.rest_0_ = bf16[2,8,3,112,896]{4,3,2,1,0:T(8,128)(2,1)} custom-call(s32[8]{0:T(128)} %copy-done.21, bf16[8,3,112,896]{3,2,1,0:T(8,128)(2,1)} %all-to-all-done.2.x_ref), custom_call_target="tpu_custom_call" | custom-call | bytes 96337 | tf_op jit(solution)/shard_map/place_blocks/pallas_call | solution.py:451
  678.7 0.6 fusion.10
  679.2 0.8 slice_bitcast_fusion
  680.1 7.7 %place_blocks.3 = bf16[2,8,3,112,896]{4,3,2,1,0:T(8,128)(2,1)} custom-call(s32[8]{0:T(128)} %copy-done.20, bf16[8,3,112,896]{3,2,1,0:T(8,128)(2,1)} %all-to-all-done.3.x_ref, bf16[2,8,3,112,896]{4,3,2,1,0:T(8,128)(2,1)} %place_blocks.2.rest_0_), custom_call_target="tpu_custom_call", output_to_operand_aliasing={{}: (2, {})} | custom-call | bytes 96337 | tf_op jit(solution)/shard_map/place_blocks/pallas_call | solution.py:451
  (140 shorter events, 4.5 us)
Async XLA Ops:
  1.4 8.3 %copy-start.21 = (s32[8]{0:T(128)}, s32[8]{0:T(128)S(1)}, u32[]{:S(2)}) copy-start(s32[8]{0:T(128)S(1)} %get-tuple-element.210.index_ref) | copy-start | bytes 100
  1.4 14.1 %copy-start.20 = (s32[8]{0:T(128)}, s32[8]{0:T(128)S(1)}, u32[]{:S(2)}) copy-start(s32[8]{0:T(128)S(1)} %get-tuple-element.209.index_ref) | copy-start | bytes 100
  9.7 5.9 copy-start.18
  9.7 215.6 %all-to-all-start = ((bf16[8,3,112,896]{3,2,1,0:T(8,128)(2,1)}), bf16[8,3,112,896]{3,2,1,0:T(8,128)(2,1)}, u32[]{:S(2)}, u32[]{:S(2)}) async-start(bf16[8,3,112,896]{3,2,1,0:T(8,128)(2,1)} %pick_blocks.2), calls=%async_computation | async-start | bytes 9633792 | tf_op jit(solution)/shard_map/all_to_all | solution.py:1524
  15.6 5.8 copy-start.19
  21.4 8.2 %copy-start.31 = (bf16[3,8]{1,0:T(4,128)(2,1)S(1)}, bf16[3,8]{1,0:T(4,128)(2,1)}, u32[]{:S(2)}) copy-start(bf16[3,8]{1,0:T(4,128)(2,1)} %param.26) | copy-start | bytes 148
  21.4 8.2 %copy-start.32 = (bf16[3,8]{1,0:T(4,128)(2,1)S(1)}, bf16[3,8]{1,0:T(4,128)(2,1)}, u32[]{:S(2)}) copy-start(bf16[3,8]{1,0:T(4,128)(2,1)} %param.29) | copy-start | bytes 148
  21.5 8.3 %copy-start.33 = (bf16[3,32]{1,0:T(4,128)(2,1)S(1)}, bf16[3,32]{1,0:T(4,128)(2,1)}, u32[]{:S(2)}) copy-start(bf16[3,32]{1,0:T(4,128)(2,1)} %param.35) | copy-start | bytes 580
  21.5 8.4 %copy-start.25 = (bf16[96]{0:T(256)(128)(2,1)S(1)}, bf16[96]{0:T(256)(128)(2,1)}, u32[]{:S(2)}) copy-start(bf16[96]{0:T(256)(128)(2,1)} %param.31) | copy-start | bytes 580
  21.5 8.4 %copy-start.26 = (bf16[96]{0:T(256)(128)(2,1)S(1)}, bf16[96]{0:T(256)(128)(2,1)}, u32[]{:S(2)}) copy-start(bf16[96]{0:T(256)(128)(2,1)} %param.32) | copy-start | bytes 580
  21.5 8.4 %copy-start.27 = (bf16[96]{0:T(256)(128)(2,1)S(1)}, bf16[96]{0:T(256)(128)(2,1)}, u32[]{:S(2)}) copy-start(bf16[96]{0:T(256)(128)(2,1)} %param.33) | copy-start | bytes 580
  21.5 8.4 %copy-start.28 = (bf16[96]{0:T(256)(128)(2,1)S(1)}, bf16[96]{0:T(256)(128)(2,1)}, u32[]{:S(2)}) copy-start(bf16[96]{0:T(256)(128)(2,1)} %param.37) | copy-start | bytes 580
  21.5 8.4 %copy-start.29 = (bf16[96]{0:T(256)(128)(2,1)S(1)}, bf16[96]{0:T(256)(128)(2,1)}, u32[]{:S(2)}) copy-start(bf16[96]{0:T(256)(128)(2,1)} %param.38) | copy-start | bytes 580
  21.5 8.4 %copy-start.30 = (bf16[96]{0:T(256)(128)(2,1)S(1)}, bf16[96]{0:T(256)(128)(2,1)}, u32[]{:S(2)}) copy-start(bf16[96]{0:T(256)(128)(2,1)} %param.39) | copy-start | bytes 580
  21.5 8.6 %copy-start.10 = (bf16[192,96]{1,0:T(8,128)(2,1)S(1)}, bf16[192,96]{1,0:T(8,128)(2,1)}, u32[]{:S(2)}) copy-start(bf16[192,96]{1,0:T(8,128)(2,1)} %param.30) | copy-start | bytes 110596
  21.6 11.3 %copy-start.8 = (bf16[96,768]{1,0:T(8,128)(2,1)S(1)}, bf16[96,768]{1,0:T(8,128)(2,1)}, u32[]{:S(2)}) copy-start(bf16[96,768]{1,0:T(8,128)(2,1)} %param.34) | copy-start | bytes 442372
  21.6 11.3 %copy-start.9 = (bf16[768,96]{0,1:T(8,128)(2,1)S(1)}, bf16[768,96]{0,1:T(8,128)(2,1)}, u32[]{:S(2)}) copy-start(bf16[768,96]{0,1:T(8,128)(2,1)} %param.36) | copy-start | bytes 442372
  21.6 11.3 %copy-start.11 = (bf16[96,192]{1,0:T(8,128)(2,1)S(1)}, bf16[96,192]{1,0:T(8,128)(2,1)}, u32[]{:S(2)}) copy-start(bf16[96,192]{1,0:T(8,128)(2,1)} %param.25) | copy-start | bytes 110596
  21.6 11.3 %copy-start.12 = (bf16[96,192]{1,0:T(8,128)(2,1)S(1)}, bf16[96,192]{1,0:T(8,128)(2,1)}, u32[]{:S(2)}) copy-start(bf16[96,192]{1,0:T(8,128)(2,1)} %param.27) | copy-start | bytes 110596
  21.6 11.3 %copy-start.13 = (bf16[96,192]{1,0:T(8,128)(2,1)S(1)}, bf16[96,192]{1,0:T(8,128)(2,1)}, u32[]{:S(2)}) copy-start(bf16[96,192]{1,0:T(8,128)(2,1)} %param.28) | copy-start | bytes 110596
  21.6 12.2 %copy-start.1 = (bf16[2,8,112,768]{3,2,1,0:T(8,128)(2,1)S(1)}, bf16[2,8,112,768]{3,2,1,0:T(8,128)(2,1)}, u32[]{:S(2)}) copy-start(bf16[2,8,112,768]{3,2,1,0:T(8,128)(2,1)} %param.21) | copy-start | bytes 8257540
  33.8 1.8 copy-start.2
  225.3 29.5 %copy-start.24 = (s32[2,8]{1,0:T(2,128)S(1)}, s32[2,8]{1,0:T(2,128)}, u32[]{:S(2)}) copy-start(s32[2,8]{1,0:T(2,128)} %param.23) | copy-start | bytes 196
  225.3 31.3 %copy-start = (bf16[4,2,112,768]{3,2,1,0:T(8,128)(2,1)S(1)}, bf16[4,2,112,768]{3,2,1,0:T(8,128)(2,1)}, u32[]{:S(2)}) copy-start(bf16[4,2,112,768]{3,2,1,0:T(8,128)(2,1)} %get-tuple-element.61) | copy-start | bytes 4128772
  225.3 126.8 %all-to-all-start.1 = ((bf16[8,3,112,896]{3,2,1,0:T(8,128)(2,1)}), bf16[8,3,112,896]{3,2,1,0:T(8,128)(2,1)}, u32[]{:S(2)}, u32[]{:S(2)}) async-start(bf16[8,3,112,896]{3,2,1,0:T(8,128)(2,1)} %pick_blocks.3), calls=%async_computation.1 | async-start | bytes 9633792 | tf_op jit(solution)/shard_map/all_to_all | solution.py:1524
  352.1 111.8 %all-to-all-start.2 = ((bf16[8,3,112,896]{3,2,1,0:T(8,128)(2,1)}), bf16[8,3,112,896]{3,2,1,0:T(8,128)(2,1)}, u32[]{:S(2)}, u32[]{:S(2)}) async-start(bf16[8,3,112,896]{3,2,1,0:T(8,128)(2,1)} %get-tuple-element.85), calls=%async_computation.2 | async-start | bytes 9633792 | tf_op jit(solution)/shard_map/all_to_all | solution.py:1542
  463.9 216.2 %all-to-all-start.3 = ((bf16[8,3,112,896]{3,2,1,0:T(8,128)(2,1)}), bf16[8,3,112,896]{3,2,1,0:T(8,128)(2,1)}, u32[]{:S(2)}, u32[]{:S(2)}) async-start(bf16[8,3,112,896]{3,2,1,0:T(8,128)(2,1)} %get-tuple-element.101), calls=%async_computation.3 | async-start | bytes 9633792 | tf_op jit(solution)/shard_map/all_to_all | solution.py:1542
  488.7 5.1 copy-start.14
  488.7 5.1 copy-start.15
  488.7 5.7 copy-start.22
  488.7 5.7 copy-start.23
  488.7 6.1 copy-start.16
  488.7 6.1 copy-start.17
  518.9 14.8 %copy-start.6 = (bf16[224,768]{1,0:T(8,128)(2,1)S(1)}, bf16[224,768]{1,0:T(8,128)(2,1)}, u32[]{:S(2)}) copy-start(bf16[224,768]{1,0:T(8,128)(2,1)} %get-tuple-element.91) | copy-start | bytes 1032196
  518.9 14.8 %copy-start.7 = (bf16[224,768]{1,0:T(8,128)(2,1)S(1)}, bf16[224,768]{1,0:T(8,128)(2,1)}, u32[]{:S(2)}) copy-start(bf16[224,768]{1,0:T(8,128)(2,1)} %get-tuple-element.92) | copy-start | bytes 1032196
  533.7 1.1 copy-start.3
  533.7 1.4 copy-start.4
  670.9 7.8 %copy-start.5 = (f32[2,48,2432]{2,1,0:T(8,128)S(1)}, f32[2,48,2432]{2,1,0:T(8,128)}, u32[]{:S(2)}) copy-start(f32[2,48,2432]{2,1,0:T(8,128)} %get-tuple-element.102) | copy-start | bytes 2801668

commit v3 on v2

--- a/solution.py
+++ b/solution.py
@@ -418,73 +418,244 @@
     return pl.BlockSpec(x.shape, lambda *_: (0,) * len(x.shape))
 
 
-def pick_kernel(index_ref, x_ref, o_ref):
-    o_ref[0] = x_ref[0, 0]
-
-
-def pick_blocks(stacked, micro, index):
-    _, count, heads, rows, extent = stacked.shape
-    block = (heads, rows, extent)
+def move_blocks(reads, writes, buffers, in_sem, out_sem):
+    ins = [pltpu.make_async_copy(r, v, in_sem.at[i]) for i, (r, v) in enumerate(zip(reads, buffers))]
+    outs = [pltpu.make_async_copy(v, w, out_sem.at[i]) for i, (v, w) in enumerate(zip(buffers, writes))]
+    for copy in ins:
+        copy.start()
+    for copy, out in zip(ins, outs):
+        copy.wait()
+        out.start()
+    for out in outs:
+        out.wait()
+
+
+SMALL = pl.BlockSpec(memory_space=pltpu.SMEM)
+ANYWHERE = pl.BlockSpec(memory_space=pl.ANY)
+
+
+def inverse_of(dealing_ref, inverse_ref, micros, slots):
+    for m in micros:
+        for i in range(slots):
+            inverse_ref[dealing_ref[m, i]] = i
+
+
+def pick_copies(micro, count, inverse_ref, x_ref, o_ref, buffer):
+    steps = range(count)
+    return (
+        [x_ref.at[micro, inverse_ref[i]] for i in steps],
+        [o_ref.at[i] for i in steps],
+        [buffer.at[i] for i in steps],
+    )
+
+
+def pick_kernel(micro, count, dealing_ref, x_ref, o_ref, buffer, inverse_ref, in_sem, out_sem):
+    inverse_of(dealing_ref, inverse_ref, [micro], count)
+    move_blocks(*pick_copies(micro, count, inverse_ref, x_ref, o_ref, buffer), in_sem, out_sem)
+
+
+def pick_blocks(stacked, micro, dealing):
+    count = stacked.shape[1]
+    block = stacked.shape[2:]
+    dma = pltpu.SemaphoreType.DMA
     return pl.pallas_call(
-        pick_kernel,
+        functools.partial(pick_kernel, micro, count),
         out_shape=jax.ShapeDtypeStruct((count, *block), stacked.dtype),
-        grid_spec=pltpu.PrefetchScalarGridSpec(
-            num_scalar_prefetch=1,
-            grid=(count,),
-            in_specs=[pl.BlockSpec((1, 1, *block), lambda i, ix: (micro, ix[i], 0, 0, 0))],
-            out_specs=pl.BlockSpec((1, *block), lambda i, ix: (i, 0, 0, 0)),
+        in_specs=[SMALL, ANYWHERE],
+        out_specs=ANYWHERE,
+        scratch_shapes=[
+            pltpu.VMEM((count, *block), stacked.dtype),
+            pltpu.SMEM((count,), jnp.int32),
+            dma((count,)),
+            dma((count,)),
+        ],
+        compiler_params=params(),
+        cost_estimate=cost(0, 4 * stacked.size // stacked.shape[0]),
+        name="pick_blocks",
+    )(dealing, stacked)
+
+
+PLAIN, QUERY_AT, VALUE_AT, UP_AT, VECTOR_ROWS = 6, 8, 16, 24, 32
+
+
+def prepare_kernel(
+    micros, slots, groups, dealing_ref, prev_ref, tokens_ref, cot_ref,
+    wq_ref, wk_ref, wv_ref, wo_ref, wu_ref, wd_ref, bq_ref, bv_ref, bu_ref, plain_refs,
+    send_ref, piece_ref, pack_ref, block_buffer, piece_buffer, vector_scr, inverse_refs, in_sem, out_sem,
+):
+    here, head = lax.axis_index("seq"), lax.axis_index("head")
+    for m in range(micros):
+        inverse_of(dealing_ref, inverse_refs[m], [m], slots)
+    reads, writes, buffers = [], [], []
+    for step in range(2):
+        slot = lax.rem(head - here // 2 + groups, groups) + groups * lax.rem(here + step, 2)
+        for a, array_ref in enumerate((tokens_ref, cot_ref)):
+            for m in range(micros):
+                n = a * micros + m
+                reads.append(array_ref.at[m, inverse_refs[m][slot]])
+                writes.append(piece_ref.at[step, n])
+                buffers.append(piece_buffer.at[step, n])
+    blocks = pick_copies(0, slots, inverse_refs[0], prev_ref, send_ref, block_buffer)
+    reads, writes, buffers = reads + blocks[0], writes + blocks[1], buffers + blocks[2]
+    for i, (source, target) in enumerate(zip(reads, buffers)):
+        pltpu.make_async_copy(source, target, in_sem.at[i]).start()
+
+    at = 0
+    for ref in (wq_ref, wk_ref, wv_ref, wo_ref, wu_ref, wd_ref):
+        pack_ref[:, at : at + ref.shape[1]] = ref[...]
+        at += ref.shape[1]
+    vector_scr[...] = jnp.zeros_like(vector_scr)
+    for i, ref in enumerate(plain_refs):
+        vector_scr[i : i + 1, : ref.shape[1]] = ref[...].astype(F32)
+    for first, ref in ((QUERY_AT, bq_ref), (VALUE_AT, bv_ref), (UP_AT, bu_ref)):
+        vector_scr[first : first + ref.shape[0], : ref.shape[1]] = ref[...].astype(F32)
+    pack_ref[:VECTOR_ROWS, at:] = vector_scr[...].astype(BF16)
+    pack_ref[VECTOR_ROWS:, at:] = jnp.zeros_like(pack_ref[VECTOR_ROWS:, at:])
+
+    for i, (source, target, buffer) in enumerate(zip(reads, writes, buffers)):
+        pltpu.make_async_copy(source, buffer, in_sem.at[i]).wait()
+        pltpu.make_async_copy(buffer, target, out_sem.at[i]).start()
+    for i, (target, buffer) in enumerate(zip(writes, buffers)):
+        pltpu.make_async_copy(buffer, target, out_sem.at[i]).wait()
+
+
+def prepare(dealing, prev, tokens, cot_tokens, weights, head_vectors, plain_vectors, groups):
+    micros, slots = prev.shape[:2]
+    block, row = prev.shape[2:], tokens.shape[2:]
+    dma = pltpu.SemaphoreType.DMA
+    copies = slots + 4 * micros
+    columns = sum(w.shape[1] for w in weights) + 128
+    in_vmem = pl.BlockSpec(memory_space=pltpu.VMEM)
+    flat = [*weights, *head_vectors]
+
+    def body(*refs):
+        fixed = 4 + len(flat)
+        plain_refs = refs[fixed : fixed + len(plain_vectors)]
+        rest = refs[fixed + len(plain_vectors) :]
+        send_ref, piece_ref, pack_ref, block_buffer, piece_buffer, vector_scr = rest[:6]
+        prepare_kernel(
+            micros, slots, groups, *refs[:fixed], plain_refs, send_ref, piece_ref, pack_ref,
+            block_buffer, piece_buffer, vector_scr, rest[6 : 6 + micros], *rest[6 + micros :],
+        )
+
+    return pl.pallas_call(
+        body,
+        out_shape=(
+            jax.ShapeDtypeStruct((slots, *block), prev.dtype),
+            jax.ShapeDtypeStruct((2, 2 * micros, *row), tokens.dtype),
+            jax.ShapeDtypeStruct((weights[0].shape[0], columns), BF16),
+        ),
+        in_specs=[SMALL, ANYWHERE, ANYWHERE, ANYWHERE] + [in_vmem] * (len(flat) + len(plain_vectors)),
+        out_specs=(ANYWHERE, ANYWHERE, in_vmem),
+        scratch_shapes=[
+            pltpu.VMEM((slots, *block), prev.dtype),
+            pltpu.VMEM((2, 2 * micros, *row), tokens.dtype),
+            pltpu.VMEM((VECTOR_ROWS, 128), F32),
+        ]
+        + [pltpu.SMEM((slots,), jnp.int32)] * micros
+        + [dma((copies,)), dma((copies,))],
+        compiler_params=params(),
+        cost_estimate=cost(0, 4 * prev.size // micros),
+        name="prepare",
+    )(dealing, prev, tokens, cot_tokens, *flat, *plain_vectors)
+
+
+def unpack_kernel(heads, x_ref, qkv_ref, up_ref, plain_ref):
+    groups, slots = x_ref.shape[:2]
+    width = heads * HEAD_DIM
+    qkv_ref[...] = jnp.zeros_like(qkv_ref)
+    lanes = plain_ref.shape[1] // slots
+    per_head = HEAD_DIM // slots
+    unit = up_ref.shape[2] // heads
+    per_unit = unit // slots
+    for s in range(slots):
+        for h in range(groups):
+            block = x_ref[h, s].astype(F32)
+            if h == 0:
+                plain_ref[:, s * lanes : (s + 1) * lanes] = block[:8, :lanes]
+            for j in range(heads):
+                at = j * HEAD_DIM + s * per_head
+                qkv_ref[h, :, at : at + per_head] = block[QUERY_AT + j : QUERY_AT + j + 1, :per_head]
+                at += 2 * width
+                qkv_ref[h, :, at : at + per_head] = block[VALUE_AT + j : VALUE_AT + j + 1, :per_head]
+                at = j * unit + s * per_unit
+                up_ref[h, :, at : at + per_unit] = block[UP_AT + j : UP_AT + j + 1, :per_unit]
+
+
+def unpack_vectors(shards, heads, width, unit, model):
+    groups, slots, _, columns = shards.shape
+    last = columns // 128 - 1
+    shape = jax.ShapeDtypeStruct
+    return pl.pallas_call(
+        functools.partial(unpack_kernel, heads),
+        out_shape=(
+            shape((groups, 1, 3 * width), F32),
+            shape((groups, 1, unit), F32),
+            shape((8, model), F32),
+        ),
+        grid=(1,),
+        in_specs=[pl.BlockSpec((groups, slots, VECTOR_ROWS, 128), lambda i: (0, 0, 0, last))],
+        out_specs=(
+            pl.BlockSpec((groups, 1, 3 * width), lambda i: (0, 0, 0)),
+            pl.BlockSpec((groups, 1, unit), lambda i: (0, 0, 0)),
+            pl.BlockSpec((8, model), lambda i: (0, 0)),
         ),
         compiler_params=params(),
-        cost_estimate=cost(0, 4 * count * heads * rows * extent),
-        name="pick_blocks",
-    )(index, stacked)
-
-
-def place_kernel(index_ref, x_ref, *rest):
-    rest[-1][0, 0] = x_ref[0]
+        cost_estimate=cost(0, 4 * groups * slots * VECTOR_ROWS * 128),
+        name="unpack_vectors",
+    )(shards)
+
+
+def place_kernel(micro, count, index_ref, x_ref, *rest):
+    o_ref, buffer, in_sem, out_sem = rest[-4:]
+    steps = range(count)
+    move_blocks(
+        [x_ref.at[index_ref[i]] for i in steps],
+        [o_ref.at[micro, i] for i in steps],
+        [buffer.at[i] for i in steps],
+        in_sem,
+        out_sem,
+    )
 
 
 def place_blocks(blocks, micro, micros, index, into):
-    count, heads, rows, extent = blocks.shape
-    block = (heads, rows, extent)
+    count = blocks.shape[0]
     others = [] if into is None else [into]
+    dma = pltpu.SemaphoreType.DMA
     return pl.pallas_call(
-        place_kernel,
-        out_shape=jax.ShapeDtypeStruct((micros, count, *block), blocks.dtype),
-        grid_spec=pltpu.PrefetchScalarGridSpec(
-            num_scalar_prefetch=1,
-            grid=(count,),
-            in_specs=[pl.BlockSpec((1, *block), lambda i, ix: (ix[i], 0, 0, 0))]
-            + [pl.BlockSpec(memory_space=pl.ANY) for _ in others],
-            out_specs=pl.BlockSpec((1, 1, *block), lambda i, ix: (micro, i, 0, 0, 0)),
-        ),
+        functools.partial(place_kernel, micro, count),
+        out_shape=jax.ShapeDtypeStruct((micros, *blocks.shape), blocks.dtype),
+        in_specs=[SMALL, ANYWHERE] + [ANYWHERE for _ in others],
+        out_specs=ANYWHERE,
+        scratch_shapes=[pltpu.VMEM(blocks.shape, blocks.dtype), dma((count,)), dma((count,))],
         input_output_aliases={2: 0} if others else {},
         compiler_params=params(),
-        cost_estimate=cost(0, 4 * count * heads * rows * extent),
+        cost_estimate=cost(0, 4 * blocks.size),
         name="place_blocks",
     )(index, blocks, *others)
 
 
-def project_kernel(x_ref, w_ref, b_ref, o_ref):
-    columns = o_ref.shape[2]
-    o_ref[0] = (dot(x_ref[...], w_ref[0, :, :columns], 1, 0) + b_ref[0]).astype(BF16)
+def project_kernel(x_ref, w_ref, b_ref, *outs):
+    columns = outs[0].shape[2]
+    for m, o_ref in enumerate(outs):
+        o_ref[0] = (dot(x_ref[m], w_ref[0, :, :columns], 1, 0) + b_ref[0]).astype(BF16)
 
 
 def project(x, weights, bias):
-    rows, width = x.shape
+    micros, rows, width = x.shape
     groups, _, columns = bias.shape
     return pl.pallas_call(
         project_kernel,
-        out_shape=jax.ShapeDtypeStruct((groups, rows, columns), BF16),
+        out_shape=(jax.ShapeDtypeStruct((groups, rows, columns), BF16),) * micros,
         grid=(groups,),
         in_specs=[
             whole(x),
             pl.BlockSpec((1, width, width), lambda h: (h, 0, 0)),
             pl.BlockSpec((1, 1, columns), lambda h: (h, 0, 0)),
         ],
-        out_specs=pl.BlockSpec((1, rows, columns), lambda h: (h, 0, 0)),
+        out_specs=(pl.BlockSpec((1, rows, columns), lambda h: (h, 0, 0)),) * micros,
         compiler_params=params(),
-        cost_estimate=cost(2 * groups * rows * width * columns, 2 * groups * columns * (width + rows)),
+        cost_estimate=cost(2 * micros * groups * rows * width * columns, 2 * groups * columns * (width + rows)),
         name="project",
     )(x, weights, bias)
 
@@ -496,7 +667,7 @@
 
 def gather_rows(info_ref, qkv_ref, groups, rows, width, q_scr, k_scr, v_scr):
     for g in range(groups):
-        block = qkv_ref[(info_ref[1] + g) % groups, 0]
+        block = qkv_ref[(info_ref[1] + g) % groups]
         q_scr[g * rows : (g + 1) * rows] = block[:, :width]
         k_scr[g * rows : (g + 1) * rows] = block[:, width : 2 * width]
         v_scr[g * rows : (g + 1) * rows] = block[:, 2 * width :]
@@ -505,7 +676,7 @@
 def forward_kernel(heads, info_ref, qkv_ref, prev_ref, *rest):
     logit_ref, attend_ref, context_ref, q_scr, k_scr, v_scr = rest[-6:]
     step = pl.program_id(0)
-    groups, _, rows, columns = qkv_ref.shape
+    groups, rows, columns = qkv_ref.shape
     piece, extent = prev_ref.shape[2:]
     width = columns // 3
 
@@ -532,7 +703,7 @@
 
 
 def attention_forward(info, qkv, prev, micro, micros, logits_into):
-    groups, _, rows, columns = qkv.shape
+    groups, rows, columns = qkv.shape
     pieces, heads, piece, extent = prev.shape
     width = columns // 3
     per = rows // piece
@@ -548,7 +719,7 @@
             num_scalar_prefetch=1,
             grid=(pieces,),
             in_specs=[
-                pl.BlockSpec((groups, 1, rows, columns), lambda j, i: (0, micro, 0, 0)),
+                pl.BlockSpec((groups, rows, columns), lambda j, i: (0, 0, 0)),
                 pl.BlockSpec((1, heads, piece, extent), lambda j, i: (j, 0, 0, 0)),
             ]
             + [pl.BlockSpec(memory_space=pl.ANY) for _ in others],
@@ -571,7 +742,7 @@
     send_ref, dqkv_ref, sums_ref, q_scr, k_scr, v_scr, dq_scr, dk_scr, dv_scr,
 ):
     step = pl.program_id(0)
-    groups, _, rows, columns = qkv_ref.shape
+    groups, rows, columns = qkv_ref.shape
     piece, extent = attend_ref.shape[2:]
     width = columns // 3
     scale = HEAD_DIM ** (-0.5)
@@ -614,7 +785,7 @@
 
 
 def attention_backward(info, qkv, attend, context, dcontext, cot, micro):
-    groups, _, rows, columns = qkv.shape
+    groups, rows, columns = qkv.shape
     pieces, heads, piece, extent = attend.shape
     width = columns // 3
     per = rows // piece
@@ -631,7 +802,7 @@
             num_scalar_prefetch=1,
             grid=(pieces,),
             in_specs=[
-                pl.BlockSpec((groups, 1, rows, columns), lambda j, i: (0, micro, 0, 0)),
+                pl.BlockSpec((groups, rows, columns), lambda j, i: (0, 0, 0)),
                 square,
                 rotated,
                 rotated,
@@ -791,10 +962,15 @@
     )(dqkv, weights, dz)
 
 
-def weight_kernel(cuts, micros, vector_ref, *refs):
-    out_ref = refs[-1]
-    out_ref[0, :, cuts[-1] :] = vector_ref[0]
+def weight_kernel(cuts, micros, heads, slots, *refs):
+    out_ref, vector_scr = refs[-2:]
     qkv_end, out_end, up_end, down_end = cuts
+
+    def summed(family):
+        total = family[0][...]
+        for ref in family[1:]:
+            total = total + ref[...]
+        return total
 
     def product(lefts, rights):
         total = None
@@ -803,33 +979,60 @@
             total = term if total is None else total + term
         return total.astype(BF16)
 
-    x, b0, h1, b2, dqkv, con, b1, act = (refs[i * micros : (i + 1) * micros] for i in range(8))
+    x, b0, h1, b2, dqkv, con, b1, act, own, plain, up = (
+        refs[i * micros : (i + 1) * micros] for i in range(11)
+    )
     out_ref[0, :, 0:qkv_end] = product(x, dqkv)
     out_ref[0, :, qkv_end:out_end] = product(b0, con)
     out_ref[0, :, out_end:up_end] = product(h1, b1)
     out_ref[0, :, up_end:down_end] = product(b2, act)
 
-
-def weight_grads(cuts, lefts, rights, vectors):
+    own_sum = jnp.where(pl.program_id(0) == lax.axis_index("head"), summed(own), 0.0)
+    plain_sum, up_sum = summed(plain), summed(up)[0]
+    rows = out_ref.shape[1] // slots
+    lanes = plain_sum.shape[1] // slots
+    unit = up_sum.shape[1] // heads
+    vector_scr[...] = jnp.zeros_like(vector_scr)
+    for s in range(slots):
+        vector_scr[:8, :lanes] = plain_sum[:, s * lanes : (s + 1) * lanes]
+        for j in range(heads):
+            at, step = j * HEAD_DIM + s * (HEAD_DIM // slots), HEAD_DIM // slots
+            vector_scr[QUERY_AT + j : QUERY_AT + j + 1, :step] = own_sum[0:1, at : at + step]
+            vector_scr[VALUE_AT + j : VALUE_AT + j + 1, :step] = own_sum[1:2, at : at + step]
+            at, step = j * unit + s * (unit // slots), unit // slots
+            vector_scr[UP_AT + j : UP_AT + j + 1, :step] = up_sum[:, at : at + step]
+        out_ref[0, s * rows : s * rows + VECTOR_ROWS, down_end:] = vector_scr[...].astype(BF16)
+        out_ref[0, s * rows + VECTOR_ROWS : (s + 1) * rows, down_end:] = jnp.zeros(
+            (rows - VECTOR_ROWS, 128), BF16
+        )
+
+
+def weight_grads(cuts, heads, slots, lefts, rights, own, plain, up):
     micros = len(lefts[0])
     groups = rights[0][0].shape[0]
     model = lefts[0][0].shape[1]
     flat_left = [a for family in lefts for a in family]
     flat_right = [a for family in rights for a in family]
     rows = flat_left[0].shape[0]
-    columns = cuts[-1] + vectors.shape[2]
+    columns = cuts[-1] + 128
+
+    def per_group(a):
+        return pl.BlockSpec((1, *a.shape[1:]), lambda h: (h, 0, 0))
+
     return pl.pallas_call(
-        functools.partial(weight_kernel, cuts, micros),
+        functools.partial(weight_kernel, cuts, micros, heads, slots),
         out_shape=jax.ShapeDtypeStruct((groups, model, columns), BF16),
         grid=(groups,),
-        in_specs=[pl.BlockSpec((1, *vectors.shape[1:]), lambda h: (h, 0, 0))]
-        + [whole(a) for a in flat_left]
-        + [pl.BlockSpec((1, *a.shape[1:]), lambda h: (h, 0, 0)) for a in flat_right],
+        in_specs=[whole(a) for a in flat_left]
+        + [per_group(a) for a in flat_right]
+        + [whole(a) for a in (*own, *plain)]
+        + [per_group(a) for a in up],
         out_specs=pl.BlockSpec((1, model, columns), lambda h: (h, 0, 0)),
+        scratch_shapes=[pltpu.VMEM((VECTOR_ROWS, 128), F32)],
         compiler_params=params(),
         cost_estimate=cost(2 * micros * groups * rows * model * cuts[-1], 2 * groups * model * cuts[-1]),
         name="weight_grads",
-    )(vectors, *flat_left, *flat_right)
+    )(*flat_left, *flat_right, *own, *plain, *up)
 
 
 MESH = pl.DeviceIdType.MESH
@@ -922,9 +1125,9 @@
     remote(block, block, send_sem, recv_sem, device).wait_recv()
 
 
-def gather_kernel(
+def line_kernel(
     slots, groups, pack_ref, piece_ref, all_ref, rows_ref,
-    z_s, z_r, x_s, x_r, y_s, y_r, c_s, c_r, piece_s, piece_r, own_sem,
+    z_s, z_r, x_s, x_r, y_s, y_r, piece_s, piece_r, own_sem,
 ):
     me = Place()
     here, head, x, y, c = me.here, me.head, me.x, me.y, me.c
@@ -940,11 +1143,8 @@
         expected = expected + (target != here).astype(jnp.int32)
     pl.semaphore_wait(pltpu.get_barrier_semaphore(), expected)
 
-    def at(i, side, row, core=c):
-        return all_ref.at[row * 2 + core, i * SIDES + side]
-
-    def half(i, side, row, part):
-        return all_ref.at[row * 2 + c, i * SIDES + side, part]
+    def at(i, side, row):
+        return all_ref.at[row * 2 + c, i * SIDES + side]
 
     def source(k):
         return pack_ref if k == 0 else at(me.order[k], x, y)
@@ -957,42 +1157,19 @@
         i = me.order[k]
         return remote(source(k), at(i, x, y), z_s.at[LINE + i], z_r.at[i], me.down)
 
+    def over_x(k):
+        i = me.order[k]
+        return remote(source(k), at(i, x, y), x_s.at[i], x_r.at[i], me.across)
+
+    def over_y(k):
+        i = me.order[k]
+        return remote(source(k), at(i, x, y), y_s.at[i], y_r.at[i], me.over)
+
     def goes_up(k):
         return (me.order[k] <= me.z) & me.not_last
 
     def goes_down(k):
         return (me.order[k] >= me.z) & me.not_first
-
-    def over_x(k, kind):
-        i = me.order[k]
-        n = kind * LINE + i
-        if kind < 2:
-            return remote(source(k).at[kind], half(i, x, y, kind), x_s.at[n], x_r.at[n], me.across)
-        block = half(i, x, 1 - y, 1)
-        return remote(block, block, x_s.at[n], x_r.at[n], me.across)
-
-    def over_y(k, kind):
-        i = me.order[k]
-        n = kind * LINE + i
-        if kind < 2:
-            return remote(source(k).at[1 - kind], half(i, x, y, 1 - kind), y_s.at[n], y_r.at[n], me.over)
-        block = half(i, 1 - x, y, 0)
-        return remote(block, block, y_s.at[n], y_r.at[n], me.over)
-
-    def to_core(k, kind):
-        i = me.order[k]
-        n = kind * LINE + i
-        if kind == 0:
-            return remote(source(k), at(i, x, y), c_s.at[n], c_r.at[n], me.beside)
-        block = at(i, *((1 - x, y), (x, 1 - y), (1 - x, 1 - y))[kind - 1])
-        return remote(block, block, c_s.at[n], c_r.at[n], me.beside)
-
-    def second(k):
-        i = me.order[k]
-        arrived(half(i, 1 - x, y, 0), x_s.at[i], x_r.at[i], me.across)
-        over_y(k, 2).start()
-        arrived(half(i, x, 1 - y, 1), y_s.at[i], y_r.at[i], me.over)
-        over_x(k, 2).start()
 
     def piece(step):
         return remote(
@@ -1010,34 +1187,16 @@
             arrived(at(i, x, y), z_s.at[i], z_r.at[i], me.up)
         pl.when(goes_up(k))(lambda k=k: upward(k).start())
         pl.when(goes_down(k))(lambda k=k: downward(k).start())
-        over_x(k, 0).start()
-        over_y(k, 0).start()
-        if k:
-            second(k - 1)
-        over_x(k, 1).start()
-        over_y(k, 1).start()
-        to_core(k, 0).start()
+        over_x(k).start()
+        over_y(k).start()
         if k == 2:
             for step, target in enumerate(targets):
                 pl.when(target != here)(lambda step=step: piece(step).start())
                 pl.when(target == here)(lambda step=step: piece_here(step).start())
-    second(LINE - 1)
     for k in range(LINE):
         i = me.order[k]
-        n = LINE + i
-        arrived(half(i, 1 - x, y, 1), x_s.at[n], x_r.at[n], me.across)
-        to_core(k, 1).start()
-        arrived(half(i, x, 1 - y, 0), y_s.at[n], y_r.at[n], me.over)
-        to_core(k, 2).start()
-        n = 2 * LINE + i
-        arrived(half(i, 1 - x, 1 - y, 1), x_s.at[n], x_r.at[n], me.across)
-        arrived(half(i, 1 - x, 1 - y, 0), y_s.at[n], y_r.at[n], me.over)
-        to_core(k, 3).start()
-    for kind, (side, row) in enumerate(((x, y), (1 - x, y), (x, 1 - y), (1 - x, 1 - y))):
-        for k in range(LINE):
-            i = me.order[k]
-            n = kind * LINE + i
-            arrived(at(i, side, row, 1 - c), c_s.at[n], c_r.at[n], me.beside)
+        arrived(at(i, 1 - x, y), x_s.at[i], x_r.at[i], me.across)
+        arrived(at(i, x, 1 - y), y_s.at[i], y_r.at[i], me.over)
     for p, home in enumerate(homes):
         block = rows_ref.at[:, p]
         pl.when(home != here)(
@@ -1052,31 +1211,77 @@
     for k in range(LINE):
         pl.when(goes_up(k))(lambda k=k: upward(k).wait_send())
         pl.when(goes_down(k))(lambda k=k: downward(k).wait_send())
-        for kind in range(3):
-            over_x(k, kind).wait_send()
-            over_y(k, kind).wait_send()
-        for kind in range(4):
-            to_core(k, kind).wait_send()
-
-
-def gather_all(packed, pieces, slots, groups, number):
+        over_x(k).wait_send()
+        over_y(k).wait_send()
+
+
+def gather_line(packed, pieces, slots, groups, number):
     dma = pltpu.SemaphoreType.DMA
     return pl.pallas_call(
-        functools.partial(gather_kernel, slots, groups),
+        functools.partial(line_kernel, slots, groups),
         out_shape=(
             jax.ShapeDtypeStruct((groups, slots, *packed.shape), packed.dtype),
             jax.ShapeDtypeStruct((pieces.shape[1], SIDE, *pieces.shape[2:]), pieces.dtype),
         ),
         in_specs=[pl.BlockSpec(memory_space=pltpu.VMEM)] * 2,
-        out_specs=(pl.BlockSpec(memory_space=pl.ANY),) * 2,
-        scratch_shapes=[dma((2 * LINE,)), dma((LINE,))]
-        + [dma((3 * LINE,))] * 4
-        + [dma((4 * LINE,))] * 2
-        + [dma((2,))] * 3,
+        out_specs=(ANYWHERE,) * 2,
+        scratch_shapes=[dma((2 * LINE,)), dma((LINE,))] + [dma((LINE,))] * 4 + [dma((2,))] * 3,
+        compiler_params=params(collective_id=number, has_side_effects=True),
+        cost_estimate=cost(0, 3000000 * 20),
+        name="gather_line",
+    )(packed, pieces)
+
+
+def plane_kernel(in_ref, all_ref, y_s, y_r, c_s, c_r):
+    me = Place()
+    x, y, c = me.x, me.y, me.c
+    greet([me.over, me.beside])
+
+    def at(i, side, row, core=c):
+        return all_ref.at[row * 2 + core, i * SIDES + side]
+
+    def over_y(i):
+        block = at(i, 1 - x, y)
+        return remote(block, block, y_s.at[i], y_r.at[i], me.over)
+
+    places = ((x, y), (1 - x, y), (x, 1 - y), (1 - x, 1 - y))
+
+    def to_core(i, kind):
+        n = kind * LINE + i
+        block = at(i, *places[kind])
+        return remote(block, block, c_s.at[n], c_r.at[n], me.beside)
+
+    for i in range(LINE):
+        over_y(i).start()
+    for kind in range(3):
+        for i in range(LINE):
+            to_core(i, kind).start()
+    for i in range(LINE):
+        arrived(at(i, 1 - x, 1 - y), y_s.at[i], y_r.at[i], me.over)
+        to_core(i, 3).start()
+    for kind, (side, row) in enumerate(places):
+        for i in range(LINE):
+            n = kind * LINE + i
+            arrived(at(i, side, row, 1 - c), c_s.at[n], c_r.at[n], me.beside)
+    for i in range(LINE):
+        over_y(i).wait_send()
+        for kind in range(4):
+            to_core(i, kind).wait_send()
+
+
+def gather_plane(shards, number):
+    dma = pltpu.SemaphoreType.DMA
+    return pl.pallas_call(
+        plane_kernel,
+        out_shape=jax.ShapeDtypeStruct(shards.shape, shards.dtype),
+        in_specs=[ANYWHERE],
+        out_specs=ANYWHERE,
+        scratch_shapes=[dma((LINE,))] * 2 + [dma((4 * LINE,))] * 2,
+        input_output_aliases={0: 0},
         compiler_params=params(collective_id=number, has_side_effects=True),
         cost_estimate=cost(0, 3000000 * 40),
-        name="gather_all",
-    )(packed, pieces)
+        name="gather_plane",
+    )(shards)
 
 
 def add_into(target, terms, shape):
@@ -1106,7 +1311,7 @@
 
 def finish_kernel(
     slots, groups, micros, part_ref, y_ref, dx_ref, sum_ref, tokens_ref, grads_ref,
-    held, first_a, first_b, second_a, second_b, line,
+    held, first, second, line,
     c_s, c_r, x_s, x_r, y_s, y_r, z_s, z_r, home_s, home_r, over_s, over_r, near_s, near_r, pass_s, pass_r,
     grad_s, grad_r, own_sem,
 ):
@@ -1138,23 +1343,18 @@
             part_ref.at[row * 2 + (1 - c), i], held.at[i, row], c_s.at[n], c_r.at[n], me.beside
         )
 
-    def first_y(k):
+    sides = (1 - x, x)
+
+    def over_y(k, n):
         i = order[k]
-        return remote(held.at[i, 1 - y, :, 0], first_a.at[i], y_s.at[i], y_r.at[i], me.over)
-
-    def first_x(k):
+        at = n * LINE + i
+        return remote(
+            held.at[i, 1 - y, sides[n]], first.at[i, sides[n]], y_s.at[at], y_r.at[at], me.over
+        )
+
+    def over_x(k):
         i = order[k]
-        return remote(held.at[i, :, 1 - x, 1], first_b.at[i], x_s.at[i], x_r.at[i], me.across)
-
-    def second_x(k):
-        i = order[k]
-        n = LINE + i
-        return remote(held.at[i, y, 1 - x, 0], second_a.at[i], x_s.at[n], x_r.at[n], me.across)
-
-    def second_y(k):
-        i = order[k]
-        n = LINE + i
-        return remote(held.at[i, 1 - y, x, 1], second_b.at[i], y_s.at[n], y_r.at[n], me.over)
+        return remote(held.at[i, y, 1 - x], second.at[i], x_s.at[i], x_r.at[i], me.across)
 
     def upward(k):
         i = order[k]
@@ -1165,49 +1365,45 @@
         n = LINE + i
         return remote(held.at[i, y, x], line.at[1, i], z_s.at[n], z_r.at[n], me.down)
 
-    rows, columns = sum_ref.shape[1:]
+    rows, columns = sum_ref.shape
 
     def begin(k):
         i = order[k]
-        for row in range(2):
-            arrived(held.at[i, row], c_s.at[row * LINE + i], c_r.at[row * LINE + i], me.beside)
-            add_into(
-                held.at[i, row], [held.at[i, row], part_ref.at[row * 2 + c, i]], (SIDES, 2, rows, columns)
-            )
-        first_y(k).start()
-        first_x(k).start()
+        for row in (1 - y, y):
+            n = row * LINE + i
+            arrived(held.at[i, row], c_s.at[n], c_r.at[n], me.beside)
+        block = held.at[i, 1 - y]
+        add_into(block, [block, part_ref.at[(1 - y) * 2 + c, i]], (SIDES, rows, columns))
+        over_y(k, 0).start()
+        over_y(k, 1).start()
+        block = held.at[i, y]
+        add_into(block, [block, part_ref.at[y * 2 + c, i]], (SIDES, rows, columns))
 
     def middle(k):
         i = order[k]
-        arrived(first_a.at[i], y_s.at[i], y_r.at[i], me.over)
-        for side in range(SIDES):
-            block = held.at[i, y, side, 0]
-            add_into(block, [block, first_a.at[i, side]], (rows, columns))
-        second_x(k).start()
-        arrived(first_b.at[i], x_s.at[i], x_r.at[i], me.across)
-        for row in range(2):
-            block = held.at[i, row, x, 1]
-            add_into(block, [block, first_b.at[i, row]], (rows, columns))
-        second_y(k).start()
+        for n, side in enumerate(sides):
+            at = n * LINE + i
+            arrived(first.at[i, side], y_s.at[at], y_r.at[at], me.over)
+            block = held.at[i, y, side]
+            add_into(block, [block, first.at[i, side]], (rows, columns))
+            if n == 0:
+                over_x(k).start()
 
     def end(k):
         i = order[k]
         n = LINE + i
         last = k == LINE - 1
-        arrived(second_a.at[i], x_s.at[n], x_r.at[n], me.across)
-        arrived(second_b.at[i], y_s.at[n], y_r.at[n], me.over)
-        for part, other in enumerate((second_a, second_b)):
-            block = held.at[i, y, x, part]
-            add_into(sum_ref.at[part] if last else block, [block, other.at[i]], (rows, columns))
+        arrived(second.at[i], x_s.at[i], x_r.at[i], me.across)
         target = sum_ref if last else held.at[i, y, x]
+        add_into(target, [held.at[i, y, x], second.at[i]], (rows, columns))
 
         def below():
             arrived(line.at[0, i], z_s.at[i], z_r.at[i], me.up)
-            add_into(target, [target, line.at[0, i]], (2, rows, columns))
+            add_into(target, [target, line.at[0, i]], (rows, columns))
 
         def above():
             arrived(line.at[1, i], z_s.at[n], z_r.at[n], me.up)
-            add_into(target, [target, line.at[1, i]], (2, rows, columns))
+            add_into(target, [target, line.at[1, i]], (rows, columns))
 
         pl.when((i >= z) & me.not_first)(below)
         pl.when((i <= z) & me.not_last)(above)
@@ -1315,8 +1511,9 @@
     for k in range(LINE):
         for row in range(2):
             to_core(k, row).wait_send()
-        for copy in (first_y, first_x, second_x, second_y):
-            copy(k).wait_send()
+        over_y(k, 0).wait_send()
+        over_y(k, 1).wait_send()
+        over_x(k).wait_send()
         if k < LINE - 1:
             i = order[k]
             pl.when(i > z)(lambda k=k: upward(k).wait_send())
@@ -1329,23 +1526,21 @@
     rows = part.shape[-2]
     dma = pltpu.SemaphoreType.DMA
     vmem = pltpu.VMEM
-    part = part.reshape(groups, LINE, SIDES, 2, rows, columns)
+    part = part.reshape(groups, LINE, SIDES, rows, columns)
     return pl.pallas_call(
         functools.partial(finish_kernel, slots, groups, micros),
         out_shape=(
-            jax.ShapeDtypeStruct((2, rows, columns), F32),
+            jax.ShapeDtypeStruct((rows, columns), F32),
             jax.ShapeDtypeStruct((micros, slots, piece, model), BF16),
             jax.ShapeDtypeStruct((micros, slots, piece, dx.shape[-1]), BF16),
         ),
         in_specs=[pl.BlockSpec(memory_space=pltpu.VMEM)] * 3,
         out_specs=(pl.BlockSpec(memory_space=pltpu.VMEM),) + (pl.BlockSpec(memory_space=pl.ANY),) * 2,
         scratch_shapes=[
-            vmem((LINE, 2, SIDES, 2, rows, columns), BF16),
+            vmem((LINE, 2, SIDES, rows, columns), BF16),
             vmem((LINE, SIDES, rows, columns), BF16),
-            vmem((LINE, 2, rows, columns), BF16),
             vmem((LINE, rows, columns), BF16),
-            vmem((LINE, rows, columns), BF16),
-            vmem((2, LINE, 2, rows, columns), BF16),
+            vmem((2, LINE, rows, columns), BF16),
         ]
         + [dma((2 * LINE,))] * 8
         + [dma((2 * micros,))] * 8
@@ -1356,36 +1551,34 @@
     )(part, y, dx)
 
 
-def order_kernel(micros, index_ref, *refs):
-    inputs, outputs = refs[: 2 * micros], refs[2 * micros :]
-    for n, out in enumerate(outputs):
-        for m in range(micros):
-            out[m, 0] = inputs[n * micros + m][0, 0]
+def order_kernel(micros, slots, index_ref, *refs):
+    count = (len(refs) - 2) // 3
+    inputs, outputs, buffers = refs[:count], refs[count : 2 * count], refs[2 * count : 3 * count]
+    in_sem, out_sem = refs[-2:]
+    where = [(n, m, i) for m in range(micros) for n in range(count) for i in range(slots)]
+    move_blocks(
+        [inputs[n].at[m, index_ref[m, i]] for n, m, i in where],
+        [outputs[n].at[m, i] for n, m, i in where],
+        [buffers[n].at[m, i] for n, m, i in where],
+        in_sem,
+        out_sem,
+    )
 
 
 def in_order(arrays, index):
     micros, slots = arrays[0].shape[:2]
-
-    def source(m):
-        return lambda i, ix: (m, ix[m, i], 0, 0)
-
+    total = len(arrays) * micros * slots
+    dma = pltpu.SemaphoreType.DMA
     return pl.pallas_call(
-        functools.partial(order_kernel, micros),
+        functools.partial(order_kernel, micros, slots),
         out_shape=tuple(jax.ShapeDtypeStruct(a.shape, a.dtype) for a in arrays),
-        grid_spec=pltpu.PrefetchScalarGridSpec(
-            num_scalar_prefetch=1,
-            grid=(slots,),
-            in_specs=[
-                pl.BlockSpec((1, 1, *a.shape[2:]), source(m)) for a in arrays for m in range(micros)
-            ],
-            out_specs=tuple(
-                pl.BlockSpec((micros, 1, *a.shape[2:]), lambda i, ix: (0, i, 0, 0)) for a in arrays
-            ),
-        ),
+        in_specs=[SMALL] + [ANYWHERE for _ in arrays],
+        out_specs=tuple(ANYWHERE for _ in arrays),
+        scratch_shapes=[pltpu.VMEM(a.shape, a.dtype) for a in arrays] + [dma((total,)), dma((total,))],
         compiler_params=params(),
         cost_estimate=cost(0, 4 * sum(a.size for a in arrays)),
         name="in_order",
-    )(index, *[a for a in arrays for _ in range(micros)])
+    )(index, *arrays)
 
 
 def fits(mesh):
@@ -1445,89 +1638,41 @@
     prev = jnp.transpose(prev_logits, (0, 1, 3, 2, 4))
     cot_square = jnp.transpose(cot_logits[:, 0], (0, 2, 1, 3))
 
-    vector = jnp.concatenate(
-        [
-            b_query.reshape(-1),
-            b_value.reshape(-1),
-            b_out,
-            gain_one,
-            shift_one,
-            b_up.reshape(-1),
-            b_down,
-            gain_two,
-            shift_two,
-        ]
+    first_send, pieces, packed = prepare(
+        dealing,
+        prev,
+        tokens,
+        cot_tokens,
+        (w_query, w_key, w_value, w_out.T, w_up, w_down.T),
+        (b_query, b_value, b_up),
+        [v.reshape(1, -1) for v in (b_out, gain_one, shift_one, b_down, gain_two, shift_two)],
+        groups,
     )
-    lots = 8
-    vector = jnp.pad(vector, (0, lots * own_rows - vector.shape[0])).reshape(own_rows, lots)
-    packed = jnp.concatenate(
-        [
-            w_query,
-            w_key,
-            w_value,
-            w_out.T,
-            w_up,
-            w_down.T,
-            jnp.pad(vector, ((0, 0), (0, 128 - lots))),
-        ],
-        axis=1,
-    )
-    pieces = jnp.stack(
-        [
-            jnp.stack(
-                [
-                    lax.dynamic_index_in_dim(array[m], inverse[m][slot], 0, keepdims=False)
-                    for array in (tokens, cot_tokens)
-                    for m in range(micros)
-                ]
-            )
-            for slot in (
-                (head - here // 2) % groups + groups * ((here + step) % 2) for step in range(2)
-            )
-        ]
-    )
-    weights, rows_all = gather_all(packed.reshape(2, own_rows // 2, -1), pieces, slots, groups, 1)
+    line, arrived_rows = gather_line(packed, pieces, slots, groups, 1)
     rows = per * piece
-    rows_all = rows_all.reshape(2 * micros, rows, model)
+    rows_all = arrived_rows.reshape(2 * micros, rows, model)
     rows_in, cot_rows = rows_all[:micros], rows_all[micros:]
 
+    weights = gather_plane(line, 2)
     weights = weights.reshape(groups, slots, own_rows, -1)
-    vectors = jnp.transpose(weights[..., cuts[-1] : cuts[-1] + lots], (1, 0, 2, 3))
-    vectors = vectors.reshape(slots, groups, -1).astype(F32)
+    bias_qkv, bias_up, row_vectors = unpack_vectors(weights, heads, width, unit, model)
     weights = weights.reshape(groups, model, -1)
-    q_len = heads * HEAD_DIM // slots
-    offsets = [0, q_len, 2 * q_len]
-    for _ in range(7):
-        offsets.append(offsets[-1] + own_rows)
-
-    def plain(i):
-        return vectors[:, 0, offsets[i] : offsets[i + 1]].reshape(1, -1)
-
-    def by_head(i):
-        part = vectors[:, :, offsets[i] : offsets[i + 1]].reshape(slots, groups, heads, -1)
-        return jnp.transpose(part, (1, 2, 0, 3)).reshape(groups, 1, -1)
-
-    bias_query, bias_value, bias_up = by_head(0), by_head(1), by_head(5)
-    bias_qkv = jnp.concatenate([bias_query, jnp.zeros_like(bias_query), bias_value], axis=2)
-    row_vectors = jnp.concatenate(
-        [plain(2), plain(3), plain(4), plain(6), plain(7), plain(8), jnp.zeros((2, model), F32)], axis=0
-    )
-
-    qkv = project(rows_in.reshape(micros * rows, model), weights, bias_qkv)
-    qkv = across_heads(qkv, 3).reshape(groups, micros, rows, 3 * width)
-
-    got_prev, after = [], None
+
+    projected = project(rows_in, weights, bias_qkv)
+    first_qkv = across_heads(projected[0], 3)
+    got_prev, after = [], arrived_rows
     for m in range(micros):
-        send = pick_blocks(prev, m, inverse[m])
-        if after is not None:
-            send, _ = lax.optimization_barrier((send, after))
+        send = pick_blocks(prev, m, dealing) if m else first_send
+        send, _ = lax.optimization_barrier((send, after))
         got = lax.all_to_all(send, "seq", split_axis=0, concat_axis=0, tiled=True)
         got_prev.append(got)
-        after = (got, qkv)
-
+        after = (got, first_qkv)
+
+    second_qkv = [across_heads(projected[m], 3) for m in range(1, micros)]
     logits, grad_logits = None, None
-    kept, sums_own, sums_rows, sums_up, returned = [], [], [], [], []
+    kept, sums_own, sums_rows, sums_up, returned, sent = [], [], [], [], [], []
     for m in range(micros):
+        qkv = second_qkv[m - 1] if m else first_qkv
         logits, attend, context = attention_forward(info[m], qkv, got_prev[m], m, micros, logits)
         context_rows = across_heads(context, 4)
         y, dz, dcon, h1, act, b1, b2, b0, sums, dbup = row_work(
@@ -1537,68 +1682,38 @@
         send, dqkv, own = attention_backward(
             info[m], qkv, attend, context, dcontext, cot_square, m
         )
-        if m:
-            send, _ = lax.optimization_barrier((send, first_grads))
-        got = lax.all_to_all(send, "seq", split_axis=0, concat_axis=0, tiled=True)
         dqkv = across_heads(dqkv, 5)
-        if m:
-            dqkv, _ = lax.optimization_barrier((dqkv, first_grads))
-        else:
-            first_grads = got
         dx = input_grad(dqkv, weights, dz)
         kept.append((rows_in[m], b0, h1, b2, dqkv, context_rows, b1, act))
         sums_own.append(own)
         sums_rows.append(sums)
         sums_up.append(dbup)
         returned.append((y, dx))
-        grad_logits = place_blocks(got, m, micros, dealing[m], grad_logits)
-
-    own = sums_own[0]
-    rows_sum = sums_rows[0]
-    up_sum = sums_up[0]
-    for m in range(1, micros):
-        own, rows_sum, up_sum = own + sums_own[m], rows_sum + sums_rows[m], up_sum + sums_up[m]
-    mine = (jnp.arange(groups) == head)[None, :, None]
-
-    def spread_own(row):
-        piece_of = jnp.transpose(row.reshape(heads, slots, -1), (1, 0, 2)).reshape(slots, 1, -1)
-        return jnp.where(mine, piece_of, 0.0)
-
-    def spread_plain(row):
-        return jnp.broadcast_to(row.reshape(slots, 1, -1), (slots, groups, own_rows))
-
-    up_part = jnp.transpose(up_sum.reshape(groups, heads, slots, -1), (2, 0, 1, 3))
-    out_vectors = jnp.concatenate(
-        [
-            spread_own(own[0]),
-            spread_own(own[1]),
-            spread_plain(rows_sum[0]),
-            spread_plain(rows_sum[1]),
-            spread_plain(rows_sum[2]),
-            up_part.reshape(slots, groups, own_rows),
-            spread_plain(rows_sum[3]),
-            spread_plain(rows_sum[4]),
-            spread_plain(rows_sum[5]),
-        ],
-        axis=2,
-    ).reshape(slots * groups, -1)
-    out_vectors = jnp.pad(out_vectors, ((0, 0), (0, lots * own_rows - out_vectors.shape[1])))
-    out_vectors = out_vectors.astype(BF16).reshape(slots, groups, own_rows, lots)
-    out_vectors = jnp.transpose(out_vectors, (1, 0, 2, 3)).reshape(groups, model, lots)
-    out_vectors = jnp.pad(out_vectors, ((0, 0), (0, 0), (0, 128 - lots)))
+        if m == 0:
+            send, _ = lax.optimization_barrier((send, (dx, second_qkv)))
+            after = lax.all_to_all(send, "seq", split_axis=0, concat_axis=0, tiled=True)
+            sent.append(after)
+        else:
+            sent.append(send)
 
     families = list(zip(*kept))
-    part = weight_grads(cuts, families[:4], families[4:], out_vectors)
+    part = weight_grads(cuts, heads, slots, families[:4], families[4:], sums_own, sums_rows, sums_up)
+    for m in range(micros):
+        if m:
+            send, _ = lax.optimization_barrier((sent[m], (sent[m - 1], part)))
+            sent[m] = lax.all_to_all(send, "seq", split_axis=0, concat_axis=0, tiled=True)
+        grad_logits = place_blocks(sent[m], m, micros, dealing[m], grad_logits)
     ys = jnp.stack([y for y, _ in returned]).reshape(micros, per, piece, model)
     dxs = jnp.stack([dx for _, dx in returned]).reshape(micros, groups, per, piece, -1)
-    part = part.reshape(groups, slots, 2, own_rows // 2, -1)
+    part = part.reshape(groups, slots, own_rows, -1)
     part, all_y, all_dx = finish(part, ys, dxs, slots, groups, 7)
-    part = part.reshape(own_rows, -1)
     out_tokens, grad_tokens = in_order((all_y, all_dx), dealing)
-    out_vectors = part[:, cuts[-1] : cuts[-1] + lots].reshape(-1)
-
-    def vector_out(i):
-        return out_vectors[offsets[i] : offsets[i + 1]]
+
+    def plain_out(i):
+        return part[i, cuts[-1] : cuts[-1] + own_rows]
+
+    def head_out(first, count):
+        return part[first : first + heads, cuts[-1] : cuts[-1] + count]
 
     def columns(start, count):
         return part[:, start : start + count]
@@ -1609,20 +1724,20 @@
         grad_tokens,
         jnp.transpose(grad_logits, (0, 1, 3, 2, 4)),
         columns(0, width),
-        vector_out(0).reshape(heads, -1),
+        head_out(QUERY_AT, HEAD_DIM // slots),
         columns(width, width),
         columns(2 * width, width),
-        vector_out(1).reshape(heads, -1),
+        head_out(VALUE_AT, HEAD_DIM // slots),
         columns(3 * width, width).T,
-        vector_out(2),
-        vector_out(3),
-        vector_out(4),
+        plain_out(0),
+        plain_out(1),
+        plain_out(2),
         columns(cuts[1], unit),
-        vector_out(5).reshape(heads, -1),
+        head_out(UP_AT, unit // heads // slots),
         columns(cuts[2], unit).T,
-        vector_out(6),
-        vector_out(7),
-        vector_out(8),
+        plain_out(3),
+        plain_out(4),
+        plain_out(5),
     )
 
 

time: 694 us -> 626 us (0.902)
  waiting for transfers between devices: 56 us -> 13.3 us
  Pallas kernels: 538 us -> 557 us
  local copies, waits for them, and re-layouts: 27.4 us -> 13.3 us
  starting transfers between devices: 44.4 us -> 30.6 us
  between operations: 13.1 us -> 4.98 us
    pallas_call x1, Pallas kernels: 118 us -> 164 us  [finish(): pl.pallas_call(functools.partial(finish_kernel, slots, groups, micros), o...]
    all_to_all x4 -> x2, waiting for transfers between devices: 56 us -> 11.8 us  [on_device(): got = lax.all_to_all(send, 'seq', split_axis=0, concat_axis=0, tiled=True)]
    pallas_call x8 -> x10, Pallas kernels: 207 us -> 169 us  [the longest x1 63.2 us: gather_line(): pl.pallas_call(functools.partial(line_kernel, slots, groups), out_shape=(...]
    all_to_all x4 -> x2, starting transfers between devices: 44.4 us -> 17.1 us  [on_device(): got = lax.all_to_all(send, 'seq', split_axis=0, concat_axis=0, tiled=True)]
    all_to_all x0 -> x2, starting transfers between devices: none -> 13.5 us  [the longest x1 7.94 us: on_device(): lax.all_to_all(send, 'seq', split_axis=0, concat_axis=0, tiled=True)]
    pallas_call x7 -> x8, Pallas kernels: 97.9 us -> 108 us  [across_heads(): pl.pallas_call(functools.partial(cross_kernel, groups), out_shape=jax.Sha...]
  transfers between devices with their start and end apart: 4 -> 4, of which waited for: 2 -> 2; matrix products, arithmetic and copies ran while one was open for 5% -> 3% of each run, Pallas kernels for 76% -> 77%
where the time goes in v3:
time: 626 us; the launch traced here: 625 us
  Pallas kernels  557 us (89%)
  starting transfers between devices  30.6 us (5%)
  local copies, waits for them, and re-layouts  13.3 us (2%)
  waiting for transfers between devices  13.3 us (2%)
    pallas_call x1, Pallas kernels, finish(): pl.pallas_call(functools.partial(finish_kernel, slots, groups, micros), o...  164 us
    pallas_call x8, Pallas kernels, across_heads(): pl.pallas_call(functools.partial(cross_kernel, groups), out_shape=jax.Sha...  108 us
    pallas_call x1, Pallas kernels, gather_line(): pl.pallas_call(functools.partial(line_kernel, slots, groups), out_shape=(...  63.2 us
    pallas_call x1, Pallas kernels, gather_plane(): pl.pallas_call(plane_kernel, out_shape=jax.ShapeDtypeStruct(shards.shape,...  56.4 us
    pallas_call x2, Pallas kernels, attention_backward(): pl.pallas_call(functools.partial(backward_kernel, heads), out_shape=(jax....  36.5 us
    pallas_call x2, Pallas kernels, attention_forward(): pl.pallas_call(functools.partial(forward_kernel, heads), out_shape=(jax.S...  35.9 us
    pallas_call x2, Pallas kernels, row_work(): pl.pallas_call(functools.partial(rows_kernel, cuts), out_shape=(shape((ro...  33.2 us
    all_to_all x2, starting transfers between devices, on_device(): got = lax.all_to_all(send, 'seq', split_axis=0, concat_axis=0, tiled=True)  17.1 us
  transfers between devices with their start and end apart: 4, of which 2 were waited for; matrix products, arithmetic and copies ran while one was open for 3% of the time, Pallas kernels for 77%

profile of v3, /device:TPU:15, one launch (start us, length us, event | category | flops | bytes accessed | tf_op | source)
XLA Modules:
  0.0 624.8 jit_solution(9921802941724963213)
XLA Ops:
  0.7 1.5 copy.47
  2.2 7.3 %prepare.1 = (bf16[8,3,112,896]{3,2,1,0:T(8,128)(2,1)}, bf16[2,4,112,768]{3,2,1,0:T(8,128)(2,1)}, bf16[96,2432]{1,0:T(8,128)(2,1)}) custom-call(s32[2,8]{1,0:T(2,128)} %index_ref.1, bf16[2,8,3,112,896]{4,3,2,1,0:T(8,128)(2,1)} %bitcast.60, bf16[2,8,112,768]{3,2,1,0:T(8,128)(2,1)} %refs_2_.1, bf16[2,8,112,768]{3,2,1,0:T(8,128)(2,1)} %refs_3_.1, ...), custom_call_target="tpu_custom_call" | custom-call | bytes 96337 | tf_op jit(solution)/shard_map/prepare/pallas_call | solution.py:541
  9.5 63.2 %gather_line.1 = (bf16[4,8,96,2432]{3,2,1,0:T(8,128)(2,1)}, bf16[4,2,112,768]{3,2,1,0:T(8,128)(2,1)}) custom-call(bf16[96,2432]{1,0:T(8,128)(2,1)} %get-tuple-element.70.pack_ref, bf16[2,4,112,768]{3,2,1,0:T(8,128)(2,1)} %get-tuple-element.71.piece_ref), custom_call_target="tpu_custom_call" | custom-call | bytes 600000 | tf_op jit(solution)/shard_map/gather_line/pallas_call | solution.py:1220
  72.7 10.6 %all-to-all-start = ((bf16[8,3,112,896]{3,2,1,0:T(8,128)(2,1)}), bf16[8,3,112,896]{3,2,1,0:T(8,128)(2,1)}, u32[]{:S(2)}, u32[]{:S(2)}) async-start(bf16[8,3,112,896]{3,2,1,0:T(8,128)(2,1)} %get-tuple-element.77), calls=%async_computation | async-start | bytes 9633792 | tf_op jit(solution)/shard_map/all_to_all | solution.py:1667
  83.3 5.0 pick_blocks.1
  88.4 0.0 copy-done
  88.4 0.9 slice.86
  89.3 56.4 %gather_plane.1.x_ref = bf16[4,8,96,2432]{3,2,1,0:T(8,128)(2,1)} custom-call(bf16[4,8,96,2432]{3,2,1,0:T(8,128)(2,1)} %get-tuple-element.73.in_ref), custom_call_target="tpu_custom_call", output_to_operand_aliasing={{}: (0, {})} | custom-call | bytes 1200000 | tf_op jit(solution)/shard_map/gather_plane/pallas_call | solution.py:1274
  145.7 1.9 unpack_vectors.1
  147.6 6.2 project.1
  153.8 19.2 %across_heads.8.qkv_ref = bf16[4,224,576]{2,1,0:T(8,128)(2,1)} custom-call(bf16[4,224,576]{2,1,0:T(8,128)(2,1)} %get-tuple-element.75.x_ref), custom_call_target="tpu_custom_call" | custom-call | bytes 206438 | tf_op jit(solution)/shard_map/across_heads/pallas_call | solution.py:1083
  173.0 0.0 copy-start.5
  173.0 0.0 copy-start.8
  173.1 11.8 %all-to-all-done.prev_ref = bf16[8,3,112,896]{3,2,1,0:T(8,128)(2,1)} async-done(((bf16[8,3,112,896]{3,2,1,0:T(8,128)(2,1)}), bf16[8,3,112,896]{3,2,1,0:T(8,128)(2,1)}, u32[]{:S(2)}, u32[]{:S(2)}) %all-to-all-start) | async-done | bytes 4816928 | tf_op jit(solution)/shard_map/all_to_all | solution.py:1667
  184.8 6.5 %all-to-all-start.1 = ((bf16[8,3,112,896]{3,2,1,0:T(8,128)(2,1)}), bf16[8,3,112,896]{3,2,1,0:T(8,128)(2,1)}, u32[]{:S(2)}, u32[]{:S(2)}) async-start(bf16[8,3,112,896]{3,2,1,0:T(8,128)(2,1)} %pick_blocks.1), calls=%async_computation.1 | async-start | bytes 9633792 | tf_op jit(solution)/shard_map/all_to_all | solution.py:1667
  191.3 0.0 copy-done.5
  191.3 0.0 copy-start.6
  191.3 0.0 copy-start.7
  191.3 0.1 select_reduce_fusion
  191.4 0.6 dynamic_slice.12
  193.3 0.6 dynamic_slice.14
  195.2 21.0 %across_heads.10.qkv_ref = bf16[4,224,576]{2,1,0:T(8,128)(2,1)} custom-call(bf16[4,224,576]{2,1,0:T(8,128)(2,1)} %get-tuple-element.82.x_ref), custom_call_target="tpu_custom_call" | custom-call | bytes 206438 | tf_op jit(solution)/shard_map/across_heads/pallas_call | solution.py:1083
  217.5 0.0 copy-done.8
  217.5 0.6 constant_dynamic-slice_fusion
  218.1 1.2 pad_add_fusion.info_ref
  219.4 1.1 fusion
  220.5 17.9 %attention_forward.2 = (bf16[2,3,896,896]{3,2,1,0:T(8,128)(2,1)}, bf16[8,3,112,896]{3,2,1,0:T(8,128)(2,1)}, bf16[4,224,192]{2,1,0:T(8,128)(2,1)}) custom-call(s32[2]{0:T(128)} %pad_add_fusion.info_ref, bf16[4,224,576]{2,1,0:T(8,128)(2,1)} %across_heads.8.qkv_ref, bf16[8,3,112,896]{3,2,1,0:T(8,128)(2,1)} %all-to-all-done.prev_ref), custom_call_target="tpu_custom_call" | custom-call | flops 24662508 | bytes 144506 | tf_op jit(solution)/shard_map/attention_forward/pallas_call | solution.py:711
  238.4 0.0 copy-done.6
  238.4 0.0 copy-done.7
  238.4 8.8 %across_heads.9.con_ref.refs_10_ = bf16[4,224,192]{2,1,0:T(8,128)(2,1)} custom-call(bf16[4,224,192]{2,1,0:T(8,128)(2,1)} %get-tuple-element.78.x_ref.context_ref), custom_call_target="tpu_custom_call" | custom-call | bytes 68812 | tf_op jit(solution)/shard_map/across_heads/pallas_call | solution.py:1083
  247.2 16.6 %row_work.2 = (bf16[224,768]{1,0:T(8,128)(2,1)}, f32[224,768]{1,0:T(8,128)}, bf16[4,224,192]{2,1,0:T(8,128)(2,1)}, bf16[224,768]{1,0:T(8,128)(2,1)}, bf16[4,224,...) custom-call(bf16[4,224,192]{2,1,0:T(8,128)(2,1)} %across_heads.9.con, ...), custom_call_target="tpu_custom_call" | custom-call | flops 52848232 | bytes 149422 | tf_op jit(solution)/shard_map/row_work/pallas_call | solution.py:908
  263.8 8.7 %across_heads.12.dcon_ref = bf16[4,224,192]{2,1,0:T(8,128)(2,1)} custom-call(bf16[4,224,192]{2,1,0:T(8,128)(2,1)} %get-tuple-element.92.x_ref), custom_call_target="tpu_custom_call" | custom-call | bytes 68812 | tf_op jit(solution)/shard_map/across_heads/pallas_call | solution.py:1083
  272.5 18.2 %attention_backward.2 = (bf16[8,3,112,896]{3,2,1,0:T(8,128)(2,1)}, bf16[4,224,576]{2,1,0:T(8,128)(2,1)}, f32[2,192]{1,0:T(2,128)}) custom-call(s32[2]{0:T(128)} %pad_add_fusion.info_ref, bf16[4,224,576]{2,1,0:T(8,128)(2,1)} %across_heads.8.qkv_ref, bf16[8,3,112,896]{3,2,1,0:T(8,128)(2,1)} %get-tuple-element.91.attend_ref, ...), custom_call_target="tpu_custom_call" | custom-call | flops 49325016 | bytes 144506 | tf_op jit(solution)/shard_map/attention_backward/pallas_call | solution.py:794
  290.8 16.1 %across_heads.13.refs_8_.dqkv_ref = bf16[4,224,576]{2,1,0:T(8,128)(2,1)} custom-call(bf16[4,224,576]{2,1,0:T(8,128)(2,1)} %get-tuple-element.93.x_ref), custom_call_target="tpu_custom_call" | custom-call | bytes 206438 | tf_op jit(solution)/shard_map/across_heads/pallas_call | solution.py:1083
  306.9 5.1 input_grad.2
  312.0 0.0 all-to-all-done.1.prev_ref
  312.0 5.6 all-to-all-start.2
  317.6 1.2 pad_add_fusion.1.info_ref
  318.8 18.0 %attention_forward.3 = (bf16[2,3,896,896]{3,2,1,0:T(8,128)(2,1)}, bf16[8,3,112,896]{3,2,1,0:T(8,128)(2,1)}, bf16[4,224,192]{2,1,0:T(8,128)(2,1)}) custom-call(s32[2]{0:T(128)} %pad_add_fusion.1.info_ref, bf16[4,224,576]{2,1,0:T(8,128)(2,1)} %across_heads.10.qkv_ref, ...), custom_call_target="tpu_custom_call", output_to_operand_aliasing={{0}: (3, {})} | custom-call | flops 24662508 | bytes 144506 | tf_op jit(solution)/shard_map/attention_forward/pallas_call | solution.py:711
  336.8 8.8 %across_heads.11.con_ref.refs_11_ = bf16[4,224,192]{2,1,0:T(8,128)(2,1)} custom-call(bf16[4,224,192]{2,1,0:T(8,128)(2,1)} %get-tuple-element.85.x_ref.context_ref), custom_call_target="tpu_custom_call" | custom-call | bytes 68812 | tf_op jit(solution)/shard_map/across_heads/pallas_call | solution.py:1083
  345.6 16.6 %row_work.3 = (bf16[224,768]{1,0:T(8,128)(2,1)}, f32[224,768]{1,0:T(8,128)}, bf16[4,224,192]{2,1,0:T(8,128)(2,1)}, bf16[224,768]{1,0:T(8,128)(2,1)}, bf16[4,224,...) custom-call(bf16[4,224,192]{2,1,0:T(8,128)(2,1)} %across_heads.11.co, ...), custom_call_target="tpu_custom_call" | custom-call | flops 52848232 | bytes 149422 | tf_op jit(solution)/shard_map/row_work/pallas_call | solution.py:908
  362.2 8.8 %across_heads.14.dcon_ref = bf16[4,224,192]{2,1,0:T(8,128)(2,1)} custom-call(bf16[4,224,192]{2,1,0:T(8,128)(2,1)} %get-tuple-element.95.x_ref), custom_call_target="tpu_custom_call" | custom-call | bytes 68812 | tf_op jit(solution)/shard_map/across_heads/pallas_call | solution.py:1083
  371.0 18.3 %attention_backward.3 = (bf16[8,3,112,896]{3,2,1,0:T(8,128)(2,1)}, bf16[4,224,576]{2,1,0:T(8,128)(2,1)}, f32[2,192]{1,0:T(2,128)}) custom-call(s32[2]{0:T(128)} %pad_add_fusion.1.info_ref, bf16[4,224,576]{2,1,0:T(8,128)(2,1)} %across_heads.10.qkv_ref, bf16[8,3,112,896]{3,2,1,0:T(8,128)(2,1)} %get-tuple-element.94.attend_ref, ...), custom_call_target="tpu_custom_call" | custom-call | flops 49325016 | bytes 144506 | tf_op jit(solution)/shard_map/attention_backward/pallas_call | solution.py:794
  389.3 16.1 %across_heads.15.refs_9_.dqkv_ref = bf16[4,224,576]{2,1,0:T(8,128)(2,1)} custom-call(bf16[4,224,576]{2,1,0:T(8,128)(2,1)} %get-tuple-element.96.x_ref), custom_call_target="tpu_custom_call" | custom-call | bytes 206438 | tf_op jit(solution)/shard_map/across_heads/pallas_call | solution.py:1083
  405.4 14.8 %weight_grads.1 = bf16[4,768,2432]{2,1,0:T(8,128)(2,1)} custom-call(bf16[224,768]{1,0:T(8,128)(2,1)} %bitcast.69, bf16[224,768]{1,0:T(8,128)(2,1)} %bitcast.67, bf16[224,768]{1,0:T(8,128)(2,1)} %get-tuple-element.81.refs_2_, bf16[224,768]{1,0:T(8,128)(2,1)} %get-tuple-element.86.refs_3_, bf16[224,768]{1,0:T(8,128)(2,1)} %get-tuple-element.87.refs_4_, ...), custom_call_target="tpu_custom_call" | custom-call | flops 63417876 | bytes 141557 | tf_op jit(solution)/shard_map/weight_grads/pallas_call | solution.py:1022
  420.2 1.5 all-to-all-done.2.x_ref
  421.7 7.9 %all-to-all-start.3 = ((bf16[8,3,112,896]{3,2,1,0:T(8,128)(2,1)}), bf16[8,3,112,896]{3,2,1,0:T(8,128)(2,1)}, u32[]{:S(2)}, u32[]{:S(2)}) async-start(bf16[8,3,112,896]{3,2,1,0:T(8,128)(2,1)} %get-tuple-element.119), calls=%async_computation.3 | async-start | bytes 9633792 | tf_op jit(solution)/shard_map/all_to_all | solution.py:1704
  429.6 5.2 input_grad.3
  434.8 0.0 copy-done.3
  434.8 0.0 copy-done.4
  434.8 0.9 pad_maximum_fusion.1.y_ref
  435.7 2.1 pad_maximum_fusion.dx_ref
  437.8 164.2 %finish.1 = (f32[96,2432]{1,0:T(8,128)}, bf16[2,8,112,768]{3,2,1,0:T(8,128)(2,1)}, bf16[2,8,112,192]{3,2,1,0:T(8,128)(2,1)}) custom-call(bf16[4,4,2,96,2432]{4,3,2,1,0:T(8,128)(2,1)} %bitcast.59, bf16[2,2,112,768]{3,2,1,0:T(8,128)(2,1)} %pad_maximum_fusion.1.y_ref, bf16[2,4,2,112,192]{4,3,2,1,0:T(8,128)(2,1)} %pad_maximum_fusion.dx_ref), custom_call_target="tpu_custom_call" | custom-call | bytes 1200000 | tf_op jit(solution)/shard_map/finish/pallas_call | solution.py:1530
  602.0 1.3 slice.101
  603.3 1.9 slice_bitcast_fusion.1
  605.2 0.7 copy.50
  605.9 4.6 in_order.1
  610.5 2.2 copy.49
  612.7 5.0 place_blocks.2.rest_0_
  617.7 0.5 slice_bitcast_fusion.2
  618.3 0.6 fusion.1
  618.8 0.8 slice_bitcast_fusion
  619.7 0.0 all-to-all-done.3.x_ref
  619.7 4.9 place_blocks.3
  (8 shorter events, 0.0 us)
Async XLA Ops:
  72.7 112.1 %all-to-all-start = ((bf16[8,3,112,896]{3,2,1,0:T(8,128)(2,1)}), bf16[8,3,112,896]{3,2,1,0:T(8,128)(2,1)}, u32[]{:S(2)}, u32[]{:S(2)}) async-start(bf16[8,3,112,896]{3,2,1,0:T(8,128)(2,1)} %get-tuple-element.77), calls=%async_computation | async-start | bytes 9633792 | tf_op jit(solution)/shard_map/all_to_all | solution.py:1667
  83.3 5.1 copy-start
  173.0 18.2 %copy-start.5 = (s32[2,8]{1,0:T(2,128)S(1)}, s32[2,8]{1,0:T(2,128)}, u32[]{:S(2)}) copy-start(s32[2,8]{1,0:T(2,128)} %index_ref.1) | copy-start | bytes 196
  173.0 44.5 %copy-start.8 = (s32[2,8]{1,0:T(2,128)S(1)}, s32[2,8]{1,0:T(2,128)}, u32[]{:S(2)}) copy-start(s32[2,8]{1,0:T(2,128)} %param.23) | copy-start | bytes 196
  184.8 127.2 %all-to-all-start.1 = ((bf16[8,3,112,896]{3,2,1,0:T(8,128)(2,1)}), bf16[8,3,112,896]{3,2,1,0:T(8,128)(2,1)}, u32[]{:S(2)}, u32[]{:S(2)}) async-start(bf16[8,3,112,896]{3,2,1,0:T(8,128)(2,1)} %pick_blocks.1), calls=%async_computation.1 | async-start | bytes 9633792 | tf_op jit(solution)/shard_map/all_to_all | solution.py:1667
  191.3 47.1 %copy-start.6 = (s32[8]{0:T(128)}, s32[8]{0:T(128)S(1)}, u32[]{:S(2)}) copy-start(s32[8]{0:T(128)S(1)} %get-tuple-element.179.index_ref) | copy-start | bytes 100
  191.3 47.1 %copy-start.7 = (s32[8]{0:T(128)}, s32[8]{0:T(128)S(1)}, u32[]{:S(2)}) copy-start(s32[8]{0:T(128)S(1)} %get-tuple-element.180.index_ref) | copy-start | bytes 100
  312.0 109.7 %all-to-all-start.2 = ((bf16[8,3,112,896]{3,2,1,0:T(8,128)(2,1)}), bf16[8,3,112,896]{3,2,1,0:T(8,128)(2,1)}, u32[]{:S(2)}, u32[]{:S(2)}) async-start(bf16[8,3,112,896]{3,2,1,0:T(8,128)(2,1)} %get-tuple-element.118), calls=%async_computation.2 | async-start | bytes 9633792 | tf_op jit(solution)/shard_map/all_to_all | solution.py:1694
  421.7 198.0 %all-to-all-start.3 = ((bf16[8,3,112,896]{3,2,1,0:T(8,128)(2,1)}), bf16[8,3,112,896]{3,2,1,0:T(8,128)(2,1)}, u32[]{:S(2)}, u32[]{:S(2)}) async-start(bf16[8,3,112,896]{3,2,1,0:T(8,128)(2,1)} %get-tuple-element.119), calls=%async_computation.3 | async-start | bytes 9633792 | tf_op jit(solution)/shard_map/all_to_all | solution.py:1704
  429.6 5.2 copy-start.3
  429.6 5.2 copy-start.4
  429.6 6.1 copy-start.1
  612.7 5.0 copy-start.2

commit v4 on v3

--- a/solution.py
+++ b/solution.py
@@ -481,11 +481,14 @@
 def prepare_kernel(
     micros, slots, groups, dealing_ref, prev_ref, tokens_ref, cot_ref,
     wq_ref, wk_ref, wv_ref, wo_ref, wu_ref, wd_ref, bq_ref, bv_ref, bu_ref, plain_refs,
-    send_ref, piece_ref, pack_ref, block_buffer, piece_buffer, vector_scr, inverse_refs, in_sem, out_sem,
+    send_ref, piece_ref, pack_ref, info_ref, block_buffer, piece_buffer, vector_scr, inverse_refs, in_sem, out_sem,
+    lengths_ref,
 ):
     here, head = lax.axis_index("seq"), lax.axis_index("head")
     for m in range(micros):
         inverse_of(dealing_ref, inverse_refs[m], [m], slots)
+        info_ref[m, 0] = lengths_ref[m, inverse_refs[m][here]]
+        info_ref[m, 1] = lax.rem(here, groups)
     reads, writes, buffers = [], [], []
     for step in range(2):
         slot = lax.rem(head - here // 2 + groups, groups) + groups * lax.rem(here + step, 2)
@@ -501,9 +504,10 @@
         pltpu.make_async_copy(source, target, in_sem.at[i]).start()
 
     at = 0
-    for ref in (wq_ref, wk_ref, wv_ref, wo_ref, wu_ref, wd_ref):
-        pack_ref[:, at : at + ref.shape[1]] = ref[...]
-        at += ref.shape[1]
+    turned = wo_ref[...].astype(F32).T.astype(BF16)
+    for block in (wq_ref[...], wk_ref[...], wv_ref[...], turned, wu_ref[...], wd_ref[...]):
+        pack_ref[:, at : at + block.shape[1]] = block
+        at += block.shape[1]
     vector_scr[...] = jnp.zeros_like(vector_scr)
     for i, ref in enumerate(plain_refs):
         vector_scr[i : i + 1, : ref.shape[1]] = ref[...].astype(F32)
@@ -519,23 +523,23 @@
         pltpu.make_async_copy(buffer, target, out_sem.at[i]).wait()
 
 
-def prepare(dealing, prev, tokens, cot_tokens, weights, head_vectors, plain_vectors, groups):
+def prepare(lengths, dealing, prev, tokens, cot_tokens, weights, head_vectors, plain_vectors, groups):
     micros, slots = prev.shape[:2]
     block, row = prev.shape[2:], tokens.shape[2:]
     dma = pltpu.SemaphoreType.DMA
     copies = slots + 4 * micros
-    columns = sum(w.shape[1] for w in weights) + 128
+    columns = sum(w.size for w in weights) // weights[0].shape[0] + 128
     in_vmem = pl.BlockSpec(memory_space=pltpu.VMEM)
     flat = [*weights, *head_vectors]
 
-    def body(*refs):
+    def body(lengths_ref, *refs):
         fixed = 4 + len(flat)
         plain_refs = refs[fixed : fixed + len(plain_vectors)]
         rest = refs[fixed + len(plain_vectors) :]
-        send_ref, piece_ref, pack_ref, block_buffer, piece_buffer, vector_scr = rest[:6]
+        made, buffers = rest[:4], rest[4:7]
         prepare_kernel(
-            micros, slots, groups, *refs[:fixed], plain_refs, send_ref, piece_ref, pack_ref,
-            block_buffer, piece_buffer, vector_scr, rest[6 : 6 + micros], *rest[6 + micros :],
+            micros, slots, groups, *refs[:fixed], plain_refs, *made, *buffers,
+            rest[7 : 7 + micros], *rest[7 + micros :], lengths_ref,
         )
 
     return pl.pallas_call(
@@ -544,9 +548,10 @@
             jax.ShapeDtypeStruct((slots, *block), prev.dtype),
             jax.ShapeDtypeStruct((2, 2 * micros, *row), tokens.dtype),
             jax.ShapeDtypeStruct((weights[0].shape[0], columns), BF16),
+            jax.ShapeDtypeStruct((micros, 2), jnp.int32),
         ),
-        in_specs=[SMALL, ANYWHERE, ANYWHERE, ANYWHERE] + [in_vmem] * (len(flat) + len(plain_vectors)),
-        out_specs=(ANYWHERE, ANYWHERE, in_vmem),
+        in_specs=[SMALL, SMALL, ANYWHERE, ANYWHERE, ANYWHERE] + [in_vmem] * (len(flat) + len(plain_vectors)),
+        out_specs=(ANYWHERE, ANYWHERE, in_vmem, SMALL),
         scratch_shapes=[
             pltpu.VMEM((slots, *block), prev.dtype),
             pltpu.VMEM((2, 2 * micros, *row), tokens.dtype),
@@ -557,7 +562,7 @@
         compiler_params=params(),
         cost_estimate=cost(0, 4 * prev.size // micros),
         name="prepare",
-    )(dealing, prev, tokens, cot_tokens, *flat, *plain_vectors)
+    )(lengths, dealing, prev, tokens, cot_tokens, *flat, *plain_vectors)
 
 
 def unpack_kernel(heads, x_ref, qkv_ref, up_ref, plain_ref):
@@ -610,7 +615,7 @@
     o_ref, buffer, in_sem, out_sem = rest[-4:]
     steps = range(count)
     move_blocks(
-        [x_ref.at[index_ref[i]] for i in steps],
+        [x_ref.at[index_ref[micro, i]] for i in steps],
         [o_ref.at[micro, i] for i in steps],
         [buffer.at[i] for i in steps],
         in_sem,
@@ -642,14 +647,14 @@
 
 
 def project(x, weights, bias):
-    micros, rows, width = x.shape
+    micros, rows, width = x.shape[0] // 2, *x.shape[1:]
     groups, _, columns = bias.shape
     return pl.pallas_call(
         project_kernel,
         out_shape=(jax.ShapeDtypeStruct((groups, rows, columns), BF16),) * micros,
         grid=(groups,),
         in_specs=[
-            whole(x),
+            pl.BlockSpec((micros, rows, width), lambda h: (0, 0, 0)),
             pl.BlockSpec((1, width, width), lambda h: (h, 0, 0)),
             pl.BlockSpec((1, 1, columns), lambda h: (h, 0, 0)),
         ],
@@ -665,15 +670,15 @@
     return lane // HEAD_DIM == head
 
 
-def gather_rows(info_ref, qkv_ref, groups, rows, width, q_scr, k_scr, v_scr):
+def gather_rows(shift, qkv_ref, groups, rows, width, q_scr, k_scr, v_scr):
     for g in range(groups):
-        block = qkv_ref[(info_ref[1] + g) % groups]
+        block = qkv_ref[(shift + g) % groups]
         q_scr[g * rows : (g + 1) * rows] = block[:, :width]
         k_scr[g * rows : (g + 1) * rows] = block[:, width : 2 * width]
         v_scr[g * rows : (g + 1) * rows] = block[:, 2 * width :]
 
 
-def forward_kernel(heads, info_ref, qkv_ref, prev_ref, *rest):
+def forward_kernel(heads, micro, info_ref, qkv_ref, prev_ref, *rest):
     logit_ref, attend_ref, context_ref, q_scr, k_scr, v_scr = rest[-6:]
     step = pl.program_id(0)
     groups, rows, columns = qkv_ref.shape
@@ -682,10 +687,10 @@
 
     @pl.when(step == 0)
     def _():
-        gather_rows(info_ref, qkv_ref, groups, rows, width, q_scr, k_scr, v_scr)
+        gather_rows(info_ref[micro, 1], qkv_ref, groups, rows, width, q_scr, k_scr, v_scr)
 
     q = q_scr[pl.ds(pl.multiple_of(step * piece, 16), piece), :]
-    key_valid = lax.broadcasted_iota(jnp.int32, (1, extent), 1) < info_ref[0]
+    key_valid = lax.broadcasted_iota(jnp.int32, (1, extent), 1) < info_ref[micro, 0]
     total = jnp.zeros((piece, width), F32)
     for h in range(heads):
         mine = head_mask((1, width), h)
@@ -709,7 +714,7 @@
     per = rows // piece
     others = [] if logits_into is None else [logits_into]
     return pl.pallas_call(
-        functools.partial(forward_kernel, heads),
+        functools.partial(forward_kernel, heads, micro),
         out_shape=(
             jax.ShapeDtypeStruct((micros, heads, extent, extent), BF16),
             jax.ShapeDtypeStruct(prev.shape, BF16),
@@ -726,7 +731,7 @@
             out_specs=(
                 pl.BlockSpec((1, heads, piece, extent), lambda j, i: (micro, 0, j, 0)),
                 pl.BlockSpec((1, heads, piece, extent), lambda j, i: (j, 0, 0, 0)),
-                pl.BlockSpec((1, piece, width), lambda j, i: ((j // per + i[1]) % groups, j % per, 0)),
+                pl.BlockSpec((1, piece, width), lambda j, i: ((j // per + i[micro, 1]) % groups, j % per, 0)),
             ),
             scratch_shapes=[pltpu.VMEM((extent, width), BF16)] * 3,
         ),
@@ -738,7 +743,7 @@
 
 
 def backward_kernel(
-    heads, info_ref, qkv_ref, attend_ref, context_ref, dcon_ref, cot_ref,
+    heads, micro, info_ref, qkv_ref, attend_ref, context_ref, dcon_ref, cot_ref,
     send_ref, dqkv_ref, sums_ref, q_scr, k_scr, v_scr, dq_scr, dk_scr, dv_scr,
 ):
     step = pl.program_id(0)
@@ -749,7 +754,7 @@
 
     @pl.when(step == 0)
     def _():
-        gather_rows(info_ref, qkv_ref, groups, rows, width, q_scr, k_scr, v_scr)
+        gather_rows(info_ref[micro, 1], qkv_ref, groups, rows, width, q_scr, k_scr, v_scr)
         dk_scr[...] = jnp.zeros_like(dk_scr)
         dv_scr[...] = jnp.zeros_like(dv_scr)
 
@@ -779,7 +784,7 @@
         sums_ref[1:2, :] = jnp.sum(dv_scr[...], axis=0, keepdims=True)
         for g in range(groups):
             part = slice(g * rows, (g + 1) * rows)
-            dqkv_ref[(info_ref[1] + g) % groups] = jnp.concatenate(
+            dqkv_ref[(info_ref[micro, 1] + g) % groups] = jnp.concatenate(
                 [dq_scr[part], dk_scr[part] * scale, dv_scr[part]], axis=1
             ).astype(BF16)
 
@@ -789,10 +794,10 @@
     pieces, heads, piece, extent = attend.shape
     width = columns // 3
     per = rows // piece
-    rotated = pl.BlockSpec((1, piece, width), lambda j, i: ((j // per + i[1]) % groups, j % per, 0))
+    rotated = pl.BlockSpec((1, piece, width), lambda j, i: ((j // per + i[micro, 1]) % groups, j % per, 0))
     square = pl.BlockSpec((1, heads, piece, extent), lambda j, i: (j, 0, 0, 0))
     return pl.pallas_call(
-        functools.partial(backward_kernel, heads),
+        functools.partial(backward_kernel, heads, micro),
         out_shape=(
             jax.ShapeDtypeStruct(attend.shape, BF16),
             jax.ShapeDtypeStruct((groups, rows, columns), BF16),
@@ -839,7 +844,7 @@
 
 
 def rows_kernel(
-    cuts, con_ref, x_ref, cot_ref, w_ref, bup_ref, vec_ref,
+    cuts, micro, con_ref, x_ref, w_ref, bup_ref, vec_ref,
     y_ref, dz_ref, dcon_ref, h1_ref, act_ref, b1_ref, b2_ref, b0_ref, sums_ref, dbup_ref,
     slope, acc, hidden, unit_scr, inv_scr,
 ):
@@ -848,7 +853,7 @@
     b_out, gain_one, shift_one = vec_ref[0:1, :], vec_ref[1:2, :], vec_ref[2:3, :]
     b_down, gain_two, shift_two = vec_ref[3:4, :], vec_ref[4:5, :], vec_ref[5:6, :]
 
-    branch = b_out + x_ref[...].astype(F32)
+    branch = b_out + x_ref[micro].astype(F32)
     for h in range(groups):
         branch = branch + dot(con_ref[h], w_ref[h, :, qkv_end:out_end], 1, 1)
     unit_one, inverse_one = normal(branch)
@@ -870,7 +875,7 @@
     lax.fori_loop(0, groups, up, 0)
     unit_two, inverse_two = normal(acc[...])
     y_ref[...] = (unit_two * gain_two + shift_two).astype(BF16)
-    cot = cot_ref[...].astype(F32)
+    cot = x_ref[x_ref.shape[0] // 2 + micro].astype(F32)
     sums_ref[4:5, :] = jnp.sum(cot * unit_two, axis=0, keepdims=True)
     sums_ref[5:6, :] = jnp.sum(cot, axis=0, keepdims=True)
     dz_two = normal_back(cot, gain_two, unit_two, inverse_two)
@@ -899,14 +904,15 @@
         dcon_ref[h] = dot(b0_ref[...], w_ref[h, :, qkv_end:out_end], 1, 0).astype(BF16)
 
 
-def row_work(cuts, context, x, cot, weights, bias_up, vectors):
+def row_work(cuts, micro, context, x, weights, bias_up, vectors):
     groups, rows, width = context.shape
-    model = x.shape[1]
+    model = x.shape[2]
+    in_vmem = pl.BlockSpec(memory_space=pltpu.VMEM)
     unit = bias_up.shape[2]
     shape = jax.ShapeDtypeStruct
-    args = (context, x, cot, weights, bias_up, vectors)
+    args = (context, x, weights, bias_up, vectors)
     return pl.pallas_call(
-        functools.partial(rows_kernel, cuts),
+        functools.partial(rows_kernel, cuts, micro),
         out_shape=(
             shape((rows, model), BF16),
             shape((rows, model), F32),
@@ -919,8 +925,8 @@
             shape((8, model), F32),
             shape((groups, 1, unit), F32),
         ),
-        in_specs=[pl.BlockSpec(memory_space=pltpu.VMEM)] * len(args),
-        out_specs=(pl.BlockSpec(memory_space=pltpu.VMEM),) * 10,
+        in_specs=[in_vmem] * len(args),
+        out_specs=(in_vmem,) * 10,
         scratch_shapes=[
             pltpu.VMEM((groups, rows, unit), F32),
             pltpu.VMEM((rows, model), F32),
@@ -975,7 +981,7 @@
     def product(lefts, rights):
         total = None
         for left, right in zip(lefts, rights):
-            term = dot(left[...], right[0], 0, 0)
+            term = dot(left[...].reshape(left.shape[-2:]), right[0], 0, 0)
             total = term if total is None else total + term
         return total.astype(BF16)
 
@@ -1007,7 +1013,7 @@
         )
 
 
-def weight_grads(cuts, heads, slots, lefts, rights, own, plain, up):
+def weight_grads(cuts, heads, slots, x, lefts, rights, own, plain, up):
     micros = len(lefts[0])
     groups = rights[0][0].shape[0]
     model = lefts[0][0].shape[1]
@@ -1016,6 +1022,9 @@
     rows = flat_left[0].shape[0]
     columns = cuts[-1] + 128
 
+    def of_micro(m):
+        return pl.BlockSpec((1, rows, model), lambda h: (m, 0, 0))
+
     def per_group(a):
         return pl.BlockSpec((1, *a.shape[1:]), lambda h: (h, 0, 0))
 
@@ -1023,7 +1032,8 @@
         functools.partial(weight_kernel, cuts, micros, heads, slots),
         out_shape=jax.ShapeDtypeStruct((groups, model, columns), BF16),
         grid=(groups,),
-        in_specs=[whole(a) for a in flat_left]
+        in_specs=[of_micro(m) for m in range(micros)]
+        + [whole(a) for a in flat_left]
         + [per_group(a) for a in flat_right]
         + [whole(a) for a in (*own, *plain)]
         + [per_group(a) for a in up],
@@ -1032,7 +1042,7 @@
         compiler_params=params(),
         cost_estimate=cost(2 * micros * groups * rows * model * cuts[-1], 2 * groups * model * cuts[-1]),
         name="weight_grads",
-    )(*flat_left, *flat_right, *own, *plain, *up)
+    )(*([x] * micros), *flat_left, *flat_right, *own, *plain, *up)
 
 
 MESH = pl.DeviceIdType.MESH
@@ -1110,6 +1120,7 @@
         self.over = {"head": (1 - self.y) * 2 + self.c}
         self.beside = {"head": self.y * 2 + (1 - self.c)}
         self.not_last, self.not_first = self.z < LINE - 1, self.z > 0
+        self.is_end = jnp.logical_or(jnp.logical_not(self.not_last), jnp.logical_not(self.not_first))
         half = (LINE - 1 - self.z) // 2
         self.order = [self.z, self.z + 1 - 2 * lax.rem(self.z, 2), 1 + half, (LINE - 1) * half]
 
@@ -1189,10 +1200,11 @@
         pl.when(goes_down(k))(lambda k=k: downward(k).start())
         over_x(k).start()
         over_y(k).start()
-        if k == 2:
+        turn = {0: me.is_end, LINE - 1: jnp.logical_not(me.is_end)}.get(k)
+        if turn is not None:
             for step, target in enumerate(targets):
-                pl.when(target != here)(lambda step=step: piece(step).start())
-                pl.when(target == here)(lambda step=step: piece_here(step).start())
+                pl.when(turn & (target != here))(lambda step=step: piece(step).start())
+                pl.when(turn & (target == here))(lambda step=step: piece_here(step).start())
     for k in range(LINE):
         i = me.order[k]
         arrived(at(i, 1 - x, y), x_s.at[i], x_r.at[i], me.across)
@@ -1310,7 +1322,7 @@
 
 
 def finish_kernel(
-    slots, groups, micros, part_ref, y_ref, dx_ref, sum_ref, tokens_ref, grads_ref,
+    slots, groups, micros, part_ref, y_refs, dx_refs, sum_ref, tokens_ref, grads_ref,
     held, first, second, line,
     c_s, c_r, x_s, x_r, y_s, y_r, z_s, z_r, home_s, home_r, over_s, over_r, near_s, near_r, pass_s, pass_r,
     grad_s, grad_r, own_sem,
@@ -1414,21 +1426,21 @@
     def home_copy(m, p):
         n = m * SIDE + p
         return remote(
-            y_ref.at[m, p], tokens_ref.at[m, here], home_s.at[n], home_r.at[m * 2 + here // groups], {"seq": homes[p]}
+            y_refs[m].at[p], tokens_ref.at[m, here], home_s.at[n], home_r.at[m * 2 + here // groups], {"seq": homes[p]}
         )
 
     def home_here(m, p):
-        return pltpu.make_async_copy(y_ref.at[m, p], tokens_ref.at[m, here], own_sem.at[m])
+        return pltpu.make_async_copy(y_refs[m].at[p], tokens_ref.at[m, here], own_sem.at[m])
 
     def grad_copy(m, p, h):
         n = (m * SIDE + p) * groups + h
         return remote(
-            dx_ref.at[m, h, p], grads_ref.at[m, here], grad_s.at[n], grad_r.at[m * slots + here],
+            dx_refs[m].at[h, p], grads_ref.at[m, here], grad_s.at[n], grad_r.at[m * slots + here],
             {"seq": homes[p], "head": h},
         )
 
     def grad_here(m, p, h):
-        return pltpu.make_async_copy(dx_ref.at[m, h, p], grads_ref.at[m, here], own_sem.at[micros + m])
+        return pltpu.make_async_copy(dx_refs[m].at[h, p], grads_ref.at[m, here], own_sem.at[micros + m])
 
     def slot_of(other, j):
         return lax.rem(other - z + groups, groups) + groups * j
@@ -1520,21 +1532,28 @@
             pl.when(i < z)(lambda k=k: downward(k).wait_send())
 
 
-def finish(part, y, dx, slots, groups, number):
+def finish(part, ys, dxs, slots, groups, number):
     columns = part.shape[-1]
-    micros, _, piece, model = y.shape
+    micros = len(ys)
+    _, piece, model = ys[0].shape
+
+    def body(part_ref, *refs):
+        finish_kernel(
+            slots, groups, micros, part_ref, refs[:micros], refs[micros : 2 * micros], *refs[2 * micros :]
+        )
+
     rows = part.shape[-2]
     dma = pltpu.SemaphoreType.DMA
     vmem = pltpu.VMEM
     part = part.reshape(groups, LINE, SIDES, rows, columns)
     return pl.pallas_call(
-        functools.partial(finish_kernel, slots, groups, micros),
+        body,
         out_shape=(
             jax.ShapeDtypeStruct((rows, columns), F32),
             jax.ShapeDtypeStruct((micros, slots, piece, model), BF16),
-            jax.ShapeDtypeStruct((micros, slots, piece, dx.shape[-1]), BF16),
+            jax.ShapeDtypeStruct((micros, slots, piece, dxs[0].shape[-1]), BF16),
         ),
-        in_specs=[pl.BlockSpec(memory_space=pltpu.VMEM)] * 3,
+        in_specs=[pl.BlockSpec(memory_space=pltpu.VMEM)] * (1 + 2 * micros),
         out_specs=(pl.BlockSpec(memory_space=pltpu.VMEM),) + (pl.BlockSpec(memory_space=pl.ANY),) * 2,
         scratch_shapes=[
             vmem((LINE, 2, SIDES, rows, columns), BF16),
@@ -1548,37 +1567,93 @@
         compiler_params=params(collective_id=number, has_side_effects=True),
         cost_estimate=cost(0, 3000000 * 40),
         name="finish",
-    )(part, y, dx)
-
-
-def order_kernel(micros, slots, index_ref, *refs):
-    count = (len(refs) - 2) // 3
-    inputs, outputs, buffers = refs[:count], refs[count : 2 * count], refs[2 * count : 3 * count]
-    in_sem, out_sem = refs[-2:]
-    where = [(n, m, i) for m in range(micros) for n in range(count) for i in range(slots)]
-    move_blocks(
-        [inputs[n].at[m, index_ref[m, i]] for n, m, i in where],
-        [outputs[n].at[m, i] for n, m, i in where],
-        [buffers[n].at[m, i] for n, m, i in where],
-        in_sem,
-        out_sem,
-    )
-
-
-def in_order(arrays, index):
-    micros, slots = arrays[0].shape[:2]
-    total = len(arrays) * micros * slots
+    )(part, *ys, *dxs)
+
+
+def deliver_kernel(
+    cuts, micros, slots, index_ref, sum_ref, y_ref, dx_ref, out_ref, grad_ref,
+    q_ref, k_ref, v_ref, wo_ref, wu_ref, wd_ref, bq_ref, bv_ref, bu_ref, *rest,
+):
+    plain_refs = rest[:PLAIN]
+    y_buffer, dx_buffer, in_sem, out_sem, dx_sem = rest[PLAIN:]
+    where = [(m, i) for m in range(micros) for i in range(slots)]
+
+    def take(n):
+        m, i = where[n]
+        return pltpu.make_async_copy(y_ref.at[m, index_ref[m, i]], y_buffer.at[m, i], in_sem.at[n])
+
+    def give(n):
+        m, i = where[n]
+        return pltpu.make_async_copy(y_buffer.at[m, i], out_ref.at[m, i], out_sem.at[n])
+
+    def take_dx(n):
+        m, i = where[n]
+        return pltpu.make_async_copy(dx_ref.at[m, index_ref[m, i]], dx_buffer.at[m, i], dx_sem.at[n])
+
+    for n in range(len(where)):
+        take(n).start()
+    for n in range(len(where)):
+        take_dx(n).start()
+    width = q_ref.shape[1]
+    for n, ref in enumerate((q_ref, k_ref, v_ref)):
+        ref[...] = sum_ref[:, n * width : (n + 1) * width]
+    wo_ref[...] = sum_ref[:, cuts[0] : cuts[1]].T
+    wu_ref[...] = sum_ref[:, cuts[1] : cuts[2]]
+    wd_ref[...] = sum_ref[:, cuts[2] : cuts[3]]
+    block = sum_ref[:VECTOR_ROWS, cuts[3] :]
+    for i, ref in enumerate(plain_refs):
+        ref[...] = block[i : i + 1, : ref.shape[1]]
+    for first, ref in ((QUERY_AT, bq_ref), (VALUE_AT, bv_ref), (UP_AT, bu_ref)):
+        ref[...] = block[first : first + ref.shape[0], : ref.shape[1]]
+    for n in range(len(where)):
+        take(n).wait()
+        give(n).start()
+    for n, (m, i) in enumerate(where):
+        take_dx(n).wait()
+        grad_ref[m, i] = dx_buffer[m, i].astype(F32).T.astype(BF16)
+    for n in range(len(where)):
+        give(n).wait()
+
+
+def deliver(cuts, heads, unit, index, sums, y, dx):
+    micros, slots, piece, share = dx.shape
+    rows, width = sums.shape[0], heads * HEAD_DIM
+    total = micros * slots
     dma = pltpu.SemaphoreType.DMA
+    in_vmem = pl.BlockSpec(memory_space=pltpu.VMEM)
+
+    def f32(*shape):
+        return jax.ShapeDtypeStruct(shape, F32)
+
     return pl.pallas_call(
-        functools.partial(order_kernel, micros, slots),
-        out_shape=tuple(jax.ShapeDtypeStruct(a.shape, a.dtype) for a in arrays),
-        in_specs=[SMALL] + [ANYWHERE for _ in arrays],
-        out_specs=tuple(ANYWHERE for _ in arrays),
-        scratch_shapes=[pltpu.VMEM(a.shape, a.dtype) for a in arrays] + [dma((total,)), dma((total,))],
+        functools.partial(deliver_kernel, cuts, micros, slots),
+        out_shape=(
+            jax.ShapeDtypeStruct(y.shape, BF16),
+            jax.ShapeDtypeStruct((micros, slots, share, piece), BF16),
+            f32(rows, width),
+            f32(rows, width),
+            f32(rows, width),
+            f32(width, rows),
+            f32(rows, unit),
+            f32(rows, unit),
+            f32(heads, HEAD_DIM // slots),
+            f32(heads, HEAD_DIM // slots),
+            f32(heads, unit // heads // slots),
+        )
+        + (f32(1, rows),) * PLAIN,
+        in_specs=[SMALL, in_vmem, ANYWHERE, ANYWHERE],
+        out_specs=(ANYWHERE,) + (in_vmem,) * (10 + PLAIN),
+        scratch_shapes=[
+            pltpu.VMEM(y.shape, BF16),
+            pltpu.VMEM(dx.shape, BF16),
+            dma((total,)),
+            dma((total,)),
+            dma((total,)),
+        ],
         compiler_params=params(),
-        cost_estimate=cost(0, 4 * sum(a.size for a in arrays)),
-        name="in_order",
-    )(index, *arrays)
+        cost_estimate=cost(0, 4 * y.size),
+        name="deliver",
+    )(index, sums, y, dx)
 
 
 def fits(mesh):
@@ -1620,30 +1695,16 @@
     cuts = (3 * width, 3 * width + width, 3 * width + width + unit, 3 * width + width + 2 * unit)
     own_rows = model // slots
 
-    inverse = [
-        jnp.sum(
-            jnp.where(
-                dealing[m][None, :] == jnp.arange(slots, dtype=jnp.int32)[:, None],
-                jnp.arange(slots, dtype=jnp.int32)[None, :],
-                0,
-            ),
-            axis=1,
-        ).astype(jnp.int32)
-        for m in range(micros)
-    ]
-    info = [
-        jnp.stack([lengths[m, inverse[m][here]], here % groups]).astype(jnp.int32)
-        for m in range(micros)
-    ]
     prev = jnp.transpose(prev_logits, (0, 1, 3, 2, 4))
     cot_square = jnp.transpose(cot_logits[:, 0], (0, 2, 1, 3))
 
-    first_send, pieces, packed = prepare(
+    first_send, pieces, packed, info = prepare(
+        lengths,
         dealing,
         prev,
         tokens,
         cot_tokens,
-        (w_query, w_key, w_value, w_out.T, w_up, w_down.T),
+        (w_query, w_key, w_value, w_out, w_up, w_down.T),
         (b_query, b_value, b_up),
         [v.reshape(1, -1) for v in (b_out, gain_one, shift_one, b_down, gain_two, shift_two)],
         groups,
@@ -1651,93 +1712,86 @@
     line, arrived_rows = gather_line(packed, pieces, slots, groups, 1)
     rows = per * piece
     rows_all = arrived_rows.reshape(2 * micros, rows, model)
-    rows_in, cot_rows = rows_all[:micros], rows_all[micros:]
 
     weights = gather_plane(line, 2)
     weights = weights.reshape(groups, slots, own_rows, -1)
     bias_qkv, bias_up, row_vectors = unpack_vectors(weights, heads, width, unit, model)
     weights = weights.reshape(groups, model, -1)
 
-    projected = project(rows_in, weights, bias_qkv)
+    projected = project(rows_all, weights, bias_qkv)
     first_qkv = across_heads(projected[0], 3)
+    second_qkv = [across_heads(projected[m], 3) for m in range(1, micros)]
     got_prev, after = [], arrived_rows
     for m in range(micros):
         send = pick_blocks(prev, m, dealing) if m else first_send
         send, _ = lax.optimization_barrier((send, after))
         got = lax.all_to_all(send, "seq", split_axis=0, concat_axis=0, tiled=True)
         got_prev.append(got)
-        after = (got, first_qkv)
-
-    second_qkv = [across_heads(projected[m], 3) for m in range(1, micros)]
+        after = (got, first_qkv, second_qkv)
+
     logits, grad_logits = None, None
     kept, sums_own, sums_rows, sums_up, returned, sent = [], [], [], [], [], []
     for m in range(micros):
         qkv = second_qkv[m - 1] if m else first_qkv
-        logits, attend, context = attention_forward(info[m], qkv, got_prev[m], m, micros, logits)
+        logits, attend, context = attention_forward(info, qkv, got_prev[m], m, micros, logits)
         context_rows = across_heads(context, 4)
         y, dz, dcon, h1, act, b1, b2, b0, sums, dbup = row_work(
-            cuts, context_rows, rows_in[m], cot_rows[m], weights, bias_up, row_vectors
+            cuts, m, context_rows, rows_all, weights, bias_up, row_vectors
         )
         dcontext = across_heads(dcon, 4)
         send, dqkv, own = attention_backward(
-            info[m], qkv, attend, context, dcontext, cot_square, m
+            info, qkv, attend, context, dcontext, cot_square, m
         )
         dqkv = across_heads(dqkv, 5)
         dx = input_grad(dqkv, weights, dz)
-        kept.append((rows_in[m], b0, h1, b2, dqkv, context_rows, b1, act))
+        kept.append((b0, h1, b2, dqkv, context_rows, b1, act))
         sums_own.append(own)
         sums_rows.append(sums)
         sums_up.append(dbup)
         returned.append((y, dx))
         if m == 0:
-            send, _ = lax.optimization_barrier((send, (dx, second_qkv)))
+            send, _ = lax.optimization_barrier((send, dx))
             after = lax.all_to_all(send, "seq", split_axis=0, concat_axis=0, tiled=True)
             sent.append(after)
         else:
             sent.append(send)
 
     families = list(zip(*kept))
-    part = weight_grads(cuts, heads, slots, families[:4], families[4:], sums_own, sums_rows, sums_up)
+    part = weight_grads(cuts, heads, slots, rows_all, families[:3], families[3:], sums_own, sums_rows, sums_up)
     for m in range(micros):
         if m:
             send, _ = lax.optimization_barrier((sent[m], (sent[m - 1], part)))
             sent[m] = lax.all_to_all(send, "seq", split_axis=0, concat_axis=0, tiled=True)
-        grad_logits = place_blocks(sent[m], m, micros, dealing[m], grad_logits)
-    ys = jnp.stack([y for y, _ in returned]).reshape(micros, per, piece, model)
-    dxs = jnp.stack([dx for _, dx in returned]).reshape(micros, groups, per, piece, -1)
+        if m == 0:
+            grad_logits = place_blocks(sent[m], m, micros, dealing, grad_logits)
+    ys = [y.reshape(per, piece, model) for y, _ in returned]
+    dxs = [dx.reshape(groups, per, piece, -1) for _, dx in returned]
     part = part.reshape(groups, slots, own_rows, -1)
+    part, _ = lax.optimization_barrier((part, grad_logits))
     part, all_y, all_dx = finish(part, ys, dxs, slots, groups, 7)
-    out_tokens, grad_tokens = in_order((all_y, all_dx), dealing)
-
-    def plain_out(i):
-        return part[i, cuts[-1] : cuts[-1] + own_rows]
-
-    def head_out(first, count):
-        return part[first : first + heads, cuts[-1] : cuts[-1] + count]
-
-    def columns(start, count):
-        return part[:, start : start + count]
-
+    out_tokens, grad_tokens, dq, dk, dv, dwo, dwu, dwd, dbq, dbv, dbu, *plain = deliver(
+        cuts, heads, unit, dealing, part, all_y, all_dx
+    )
+    for m in range(1, micros):
+        grad_logits = place_blocks(sent[m], m, micros, dealing, grad_logits)
+
+    plain = [row.reshape(-1) for row in plain]
     return (
         out_tokens,
         jnp.transpose(logits, (0, 2, 1, 3))[:, None],
-        grad_tokens,
+        jnp.transpose(grad_tokens, (0, 1, 3, 2)),
         jnp.transpose(grad_logits, (0, 1, 3, 2, 4)),
-        columns(0, width),
-        head_out(QUERY_AT, HEAD_DIM // slots),
-        columns(width, width),
-        columns(2 * width, width),
-        head_out(VALUE_AT, HEAD_DIM // slots),
-        columns(3 * width, width).T,
-        plain_out(0),
-        plain_out(1),
-        plain_out(2),
-        columns(cuts[1], unit),
-        head_out(UP_AT, unit // heads // slots),
-        columns(cuts[2], unit).T,
-        plain_out(3),
-        plain_out(4),
-        plain_out(5),
+        dq,
+        dbq,
+        dk,
+        dv,
+        dbv,
+        dwo,
+        *plain[:3],
+        dwu,
+        dbu,
+        dwd.T,
+        *plain[3:],
     )
 
 

time: 626 us -> 615 us (0.982)
  local copies, waits for them, and re-layouts: 13.3 us -> 0 us
  starting transfers between devices: 30.6 us -> 43.1 us
  Pallas kernels: 557 us -> 547 us
  waiting for transfers between devices: 13.3 us -> 22.8 us
    all_to_all x2, starting transfers between devices: 17.1 us -> 30 us  [on_device(): got = lax.all_to_all(send, 'seq', split_axis=0, concat_axis=0, tiled=True)]
    pallas_call x1, Pallas kernels: 56.4 us -> 45.5 us  [gather_plane(): pl.pallas_call(plane_kernel, out_shape=jax.ShapeDtypeStruct(shards.shape,...]
    all_to_all x2, waiting for transfers between devices: 11.8 us -> 22.6 us  [on_device(): got = lax.all_to_all(send, 'seq', split_axis=0, concat_axis=0, tiled=True)]
  transfers between devices with their start and end apart: 4 -> 4, of which waited for: 2 -> 3; matrix products, arithmetic and copies ran while one was open for 3% -> 0% of each run, Pallas kernels for 77% -> 76%
where the time goes in v4:
time: 615 us; the launch traced here: 613 us
  Pallas kernels  547 us (89%)
  starting transfers between devices  43.1 us (7%)
  waiting for transfers between devices  22.8 us (4%)
    pallas_call x1, Pallas kernels, finish(): pl.pallas_call(body, out_shape=(jax.ShapeDtypeStruct((rows, columns), F32...  164 us
    pallas_call x8, Pallas kernels, across_heads(): pl.pallas_call(functools.partial(cross_kernel, groups), out_shape=jax.Sha...  103 us
    pallas_call x1, Pallas kernels, gather_line(): pl.pallas_call(functools.partial(line_kernel, slots, groups), out_shape=(...  65.5 us
    pallas_call x1, Pallas kernels, gather_plane(): pl.pallas_call(plane_kernel, out_shape=jax.ShapeDtypeStruct(shards.shape,...  45.5 us
    pallas_call x2, Pallas kernels, attention_backward(): pl.pallas_call(functools.partial(backward_kernel, heads, micro), out_shap...  36.5 us
    pallas_call x2, Pallas kernels, attention_forward(): pl.pallas_call(functools.partial(forward_kernel, heads, micro), out_shape...  35.9 us
    pallas_call x2, Pallas kernels, row_work(): pl.pallas_call(functools.partial(rows_kernel, cuts, micro), out_shape=(sh...  33.9 us
    all_to_all x2, starting transfers between devices, on_device(): got = lax.all_to_all(send, 'seq', split_axis=0, concat_axis=0, tiled=True)  30 us
  transfers between devices with their start and end apart: 4, of which 3 were waited for; matrix products, arithmetic and copies ran while one was open for 0% of the time, Pallas kernels for 76%

profile of v4, /device:TPU:15, one launch (start us, length us, event | category | flops | bytes accessed | tf_op | source)
XLA Modules:
  0.0 613.4 jit_solution(3849376318858632785)
XLA Ops:
  0.7 7.4 %prepare.1 = (bf16[8,3,112,896]{3,2,1,0:T(8,128)(2,1)}, bf16[2,4,112,768]{3,2,1,0:T(8,128)(2,1)}, bf16[96,2432]{1,0:T(8,128)(2,1)}, s32[2,2]{1,0:T(2,128)}) custom-call(s32[2,8]{1,0:T(2,128)} %lengths_ref.1, s32[2,8]{1,0:T(2,128)} %index_ref.5, bf16[2,8,3,112,896]{4,3,2,1,0:T(8,128)(2,1)} %bitcast.39, bf16[2,8,112,768]{3,2,1,0:T(8,128)(2,1)} %refs_2_.1, ...), custom_call_target="tpu_custom_call" | custom-call | bytes 96337 | tf_op jit(solution)/shard_map/prepare/pallas_call | solution.py:545
  8.0 65.5 %gather_line.1 = (bf16[4,8,96,2432]{3,2,1,0:T(8,128)(2,1)}, bf16[4,2,112,768]{3,2,1,0:T(8,128)(2,1)}) custom-call(bf16[96,2432]{1,0:T(8,128)(2,1)} %get-tuple-element.87.pack_ref, bf16[2,4,112,768]{3,2,1,0:T(8,128)(2,1)} %get-tuple-element.88.piece_ref), custom_call_target="tpu_custom_call" | custom-call | bytes 600000 | tf_op jit(solution)/shard_map/gather_line/pallas_call | solution.py:1232
  73.5 22.4 %all-to-all-start = ((bf16[8,3,112,896]{3,2,1,0:T(8,128)(2,1)}), bf16[8,3,112,896]{3,2,1,0:T(8,128)(2,1)}, u32[]{:S(2)}, u32[]{:S(2)}) async-start(bf16[8,3,112,896]{3,2,1,0:T(8,128)(2,1)} %get-tuple-element.95), calls=%async_computation | async-start | bytes 9633792 | tf_op jit(solution)/shard_map/all_to_all | solution.py:1728
  95.9 4.9 pick_blocks.1
  100.9 45.5 %gather_plane.1.x_ref = bf16[4,8,96,2432]{3,2,1,0:T(8,128)(2,1)} custom-call(bf16[4,8,96,2432]{3,2,1,0:T(8,128)(2,1)} %get-tuple-element.91.in_ref), custom_call_target="tpu_custom_call", output_to_operand_aliasing={{}: (0, {})} | custom-call | bytes 1200000 | tf_op jit(solution)/shard_map/gather_plane/pallas_call | solution.py:1286
  146.4 1.9 unpack_vectors.1
  148.3 6.2 %project.1 = (bf16[4,224,576]{2,1,0:T(8,128)(2,1)}, bf16[4,224,576]{2,1,0:T(8,128)(2,1)}) custom-call(bf16[4,224,768]{2,1,0:T(8,128)(2,1)} %bitcast.44, bf16[4,768,2432]{2,1,0:T(8,128)(2,1)} %bitcast.33, f32[4,1,576]{2,1,0:T(1,128)} %get-tuple-element.92.b_ref), custom_call_target="tpu_custom_call" | custom-call | flops 15854469 | bytes 45711 | tf_op jit(solution)/shard_map/project/pallas_call | solution.py:652
  154.5 16.4 %across_heads.8.qkv_ref = bf16[4,224,576]{2,1,0:T(8,128)(2,1)} custom-call(bf16[4,224,576]{2,1,0:T(8,128)(2,1)} %get-tuple-element.93.x_ref), custom_call_target="tpu_custom_call" | custom-call | bytes 206438 | tf_op jit(solution)/shard_map/across_heads/pallas_call | solution.py:1093
  170.9 16.1 %across_heads.10.qkv_ref = bf16[4,224,576]{2,1,0:T(8,128)(2,1)} custom-call(bf16[4,224,576]{2,1,0:T(8,128)(2,1)} %get-tuple-element.100.x_ref), custom_call_target="tpu_custom_call" | custom-call | bytes 206438 | tf_op jit(solution)/shard_map/across_heads/pallas_call | solution.py:1093
  187.0 12.1 %all-to-all-done.prev_ref = bf16[8,3,112,896]{3,2,1,0:T(8,128)(2,1)} async-done(((bf16[8,3,112,896]{3,2,1,0:T(8,128)(2,1)}), bf16[8,3,112,896]{3,2,1,0:T(8,128)(2,1)}, u32[]{:S(2)}, u32[]{:S(2)}) %all-to-all-start) | async-done | bytes 4816928 | tf_op jit(solution)/shard_map/all_to_all | solution.py:1728
  199.1 7.6 %all-to-all-start.1 = ((bf16[8,3,112,896]{3,2,1,0:T(8,128)(2,1)}), bf16[8,3,112,896]{3,2,1,0:T(8,128)(2,1)}, u32[]{:S(2)}, u32[]{:S(2)}) async-start(bf16[8,3,112,896]{3,2,1,0:T(8,128)(2,1)} %pick_blocks.1), calls=%async_computation.1 | async-start | bytes 9633792 | tf_op jit(solution)/shard_map/all_to_all | solution.py:1728
  206.7 18.0 %attention_forward.2 = (bf16[2,3,896,896]{3,2,1,0:T(8,128)(2,1)}, bf16[8,3,112,896]{3,2,1,0:T(8,128)(2,1)}, bf16[4,224,192]{2,1,0:T(8,128)(2,1)}) custom-call(s32[2,2]{1,0:T(2,128)} %get-tuple-element.90.info_ref, bf16[4,224,576]{2,1,0:T(8,128)(2,1)} %across_heads.8.qkv_ref, bf16[8,3,112,896]{3,2,1,0:T(8,128)(2,1)} %all-to-all-done.prev_ref), custom_call_target="tpu_custom_call" | custom-call | flops 24662508 | bytes 144506 | tf_op jit(solution)/shard_map/attention_forward/pallas_call | solution.py:716
  224.7 10.3 %across_heads.9.con_ref.refs_10_ = bf16[4,224,192]{2,1,0:T(8,128)(2,1)} custom-call(bf16[4,224,192]{2,1,0:T(8,128)(2,1)} %get-tuple-element.96.x_ref.context_ref), custom_call_target="tpu_custom_call" | custom-call | bytes 68812 | tf_op jit(solution)/shard_map/across_heads/pallas_call | solution.py:1093
  235.0 16.9 %row_work.2 = (bf16[224,768]{1,0:T(8,128)(2,1)}, f32[224,768]{1,0:T(8,128)}, bf16[4,224,192]{2,1,0:T(8,128)(2,1)}, bf16[224,768]{1,0:T(8,128)(2,1)}, bf16[4,224,...) custom-call(bf16[4,224,192]{2,1,0:T(8,128)(2,1)} %across_heads.9.con, ...), custom_call_target="tpu_custom_call" | custom-call | flops 52848232 | bytes 149422 | tf_op jit(solution)/shard_map/row_work/pallas_call | solution.py:914
  251.9 8.8 %across_heads.12.dcon_ref = bf16[4,224,192]{2,1,0:T(8,128)(2,1)} custom-call(bf16[4,224,192]{2,1,0:T(8,128)(2,1)} %get-tuple-element.110.x_ref), custom_call_target="tpu_custom_call" | custom-call | bytes 68812 | tf_op jit(solution)/shard_map/across_heads/pallas_call | solution.py:1093
  260.8 18.2 %attention_backward.2 = (bf16[8,3,112,896]{3,2,1,0:T(8,128)(2,1)}, bf16[4,224,576]{2,1,0:T(8,128)(2,1)}, f32[2,192]{1,0:T(2,128)}) custom-call(s32[2,2]{1,0:T(2,128)} %get-tuple-element.90.info_ref, bf16[4,224,576]{2,1,0:T(8,128)(2,1)} %across_heads.8.qkv_ref, bf16[8,3,112,896]{3,2,1,0:T(8,128)(2,1)} %get-tuple-element.109.attend_ref, ...), custom_call_target="tpu_custom_call" | custom-call | flops 49325016 | bytes 144506 | tf_op jit(solution)/shard_map/attention_backward/pallas_call | solution.py:799
  279.0 16.1 %across_heads.13.refs_8_.dqkv_ref = bf16[4,224,576]{2,1,0:T(8,128)(2,1)} custom-call(bf16[4,224,576]{2,1,0:T(8,128)(2,1)} %get-tuple-element.111.x_ref), custom_call_target="tpu_custom_call" | custom-call | bytes 206438 | tf_op jit(solution)/shard_map/across_heads/pallas_call | solution.py:1093
  295.1 5.1 input_grad.2
  300.2 10.5 %all-to-all-done.1.prev_ref = bf16[8,3,112,896]{3,2,1,0:T(8,128)(2,1)} async-done(((bf16[8,3,112,896]{3,2,1,0:T(8,128)(2,1)}), bf16[8,3,112,896]{3,2,1,0:T(8,128)(2,1)}, u32[]{:S(2)}, u32[]{:S(2)}) %all-to-all-start.1) | async-done | bytes 4816928 | tf_op jit(solution)/shard_map/all_to_all | solution.py:1728
  310.7 6.5 %all-to-all-start.2 = ((bf16[8,3,112,896]{3,2,1,0:T(8,128)(2,1)}), bf16[8,3,112,896]{3,2,1,0:T(8,128)(2,1)}, u32[]{:S(2)}, u32[]{:S(2)}) async-start(bf16[8,3,112,896]{3,2,1,0:T(8,128)(2,1)} %get-tuple-element.127), calls=%async_computation.2 | async-start | bytes 9633792 | tf_op jit(solution)/shard_map/all_to_all | solution.py:1754
  317.2 18.0 %attention_forward.3 = (bf16[2,3,896,896]{3,2,1,0:T(8,128)(2,1)}, bf16[8,3,112,896]{3,2,1,0:T(8,128)(2,1)}, bf16[4,224,192]{2,1,0:T(8,128)(2,1)}) custom-call(s32[2,2]{1,0:T(2,128)} %get-tuple-element.90.info_ref, bf16[4,224,576]{2,1,0:T(8,128)(2,1)} %across_heads.10.qkv_ref, ...), custom_call_target="tpu_custom_call", output_to_operand_aliasing={{0}: (3, {})} | custom-call | flops 24662508 | bytes 144506 | tf_op jit(solution)/shard_map/attention_forward/pallas_call | solution.py:716
  335.1 10.7 %across_heads.11.con_ref.refs_11_ = bf16[4,224,192]{2,1,0:T(8,128)(2,1)} custom-call(bf16[4,224,192]{2,1,0:T(8,128)(2,1)} %get-tuple-element.103.x_ref.context_ref), custom_call_target="tpu_custom_call" | custom-call | bytes 68812 | tf_op jit(solution)/shard_map/across_heads/pallas_call | solution.py:1093
  345.8 16.9 %row_work.3 = (bf16[224,768]{1,0:T(8,128)(2,1)}, f32[224,768]{1,0:T(8,128)}, bf16[4,224,192]{2,1,0:T(8,128)(2,1)}, bf16[224,768]{1,0:T(8,128)(2,1)}, bf16[4,224,...) custom-call(bf16[4,224,192]{2,1,0:T(8,128)(2,1)} %across_heads.11.co, ...), custom_call_target="tpu_custom_call" | custom-call | flops 52848232 | bytes 149422 | tf_op jit(solution)/shard_map/row_work/pallas_call | solution.py:914
  362.7 8.8 %across_heads.14.dcon_ref = bf16[4,224,192]{2,1,0:T(8,128)(2,1)} custom-call(bf16[4,224,192]{2,1,0:T(8,128)(2,1)} %get-tuple-element.113.x_ref), custom_call_target="tpu_custom_call" | custom-call | bytes 68812 | tf_op jit(solution)/shard_map/across_heads/pallas_call | solution.py:1093
  371.6 18.3 %attention_backward.3 = (bf16[8,3,112,896]{3,2,1,0:T(8,128)(2,1)}, bf16[4,224,576]{2,1,0:T(8,128)(2,1)}, f32[2,192]{1,0:T(2,128)}) custom-call(s32[2,2]{1,0:T(2,128)} %get-tuple-element.90.info_ref, bf16[4,224,576]{2,1,0:T(8,128)(2,1)} %across_heads.10.qkv_ref, bf16[8,3,112,896]{3,2,1,0:T(8,128)(2,1)} %get-tuple-element.112.attend_ref, ...), custom_call_target="tpu_custom_call" | custom-call | flops 49325016 | bytes 144506 | tf_op jit(solution)/shard_map/attention_backward/pallas_call | solution.py:799
  389.8 16.1 %across_heads.15.refs_9_.dqkv_ref = bf16[4,224,576]{2,1,0:T(8,128)(2,1)} custom-call(bf16[4,224,576]{2,1,0:T(8,128)(2,1)} %get-tuple-element.114.x_ref), custom_call_target="tpu_custom_call" | custom-call | bytes 206438 | tf_op jit(solution)/shard_map/across_heads/pallas_call | solution.py:1093
  406.0 14.7 %weight_grads.1 = bf16[4,768,2432]{2,1,0:T(8,128)(2,1)} custom-call(bf16[4,224,768]{2,1,0:T(8,128)(2,1)} %bitcast.47, bf16[4,224,768]{2,1,0:T(8,128)(2,1)} %bitcast.48, bf16[224,768]{1,0:T(8,128)(2,1)} %get-tuple-element.99.refs_2_, bf16[224,768]{1,0:T(8,128)(2,1)} %get-tuple-element.104.refs_3_, bf16[224,768]{1,0:T(8,128)(2,1)} %get-tuple-element.105.refs_4_, ...), custom_call_target="tpu_custom_call" | custom-call | flops 63417876 | bytes 141557 | tf_op jit(solution)/shard_map/weight_grads/pallas_call | solution.py:1031
  420.7 0.2 all-to-all-done.2.x_ref
  421.0 6.6 %all-to-all-start.3 = ((bf16[8,3,112,896]{3,2,1,0:T(8,128)(2,1)}), bf16[8,3,112,896]{3,2,1,0:T(8,128)(2,1)}, u32[]{:S(2)}, u32[]{:S(2)}) async-start(bf16[8,3,112,896]{3,2,1,0:T(8,128)(2,1)} %get-tuple-element.139), calls=%async_computation.3 | async-start | bytes 9633792 | tf_op jit(solution)/shard_map/all_to_all | solution.py:1764
  427.6 4.9 place_blocks.2.rest_0_
  432.5 5.1 input_grad.3
  437.6 163.8 %finish.1 = (f32[96,2432]{1,0:T(8,128)}, bf16[2,8,112,768]{3,2,1,0:T(8,128)(2,1)}, bf16[2,8,112,192]{3,2,1,0:T(8,128)(2,1)}) custom-call(bf16[4,4,2,96,2432]{4,3,2,1,0:T(8,128)(2,1)} %bitcast.38, bf16[2,112,768]{2,1,0:T(8,128)(2,1)} %bitcast.52, bf16[2,112,768]{2,1,0:T(8,128)(2,1)} %bitcast.53, bf16[4,2,112,192]{3,2,1,0:T(8,128)(2,1)} %bitcast.50, ...), custom_call_target="tpu_custom_call" | custom-call | bytes 1200000 | tf_op jit(solution)/shard_map/finish/pallas_call | solution.py:1549
  601.4 6.9 %deliver.1 = (bf16[2,8,112,768]{3,2,1,0:T(8,128)(2,1)}, bf16[2,8,192,112]{3,2,1,0:T(8,128)(2,1)}, f32[96,192]{1,0:T(8,128)}, f32[96,192]{1,0:T(8,128)}, f32[96,1...) custom-call(s32[2,8]{1,0:T(2,128)} %index_ref.5, ...), custom_call_target="tpu_custom_call" | custom-call | bytes 55050 | tf_op jit(solution)/shard_map/deliver/pallas_call | solution.py:1628
  608.4 0.0 all-to-all-done.3.x_ref
  608.4 4.9 place_blocks.3
Async XLA Ops:
  73.5 125.6 %all-to-all-start = ((bf16[8,3,112,896]{3,2,1,0:T(8,128)(2,1)}), bf16[8,3,112,896]{3,2,1,0:T(8,128)(2,1)}, u32[]{:S(2)}, u32[]{:S(2)}) async-start(bf16[8,3,112,896]{3,2,1,0:T(8,128)(2,1)} %get-tuple-element.95), calls=%async_computation | async-start | bytes 9633792 | tf_op jit(solution)/shard_map/all_to_all | solution.py:1728
  199.1 111.6 %all-to-all-start.1 = ((bf16[8,3,112,896]{3,2,1,0:T(8,128)(2,1)}), bf16[8,3,112,896]{3,2,1,0:T(8,128)(2,1)}, u32[]{:S(2)}, u32[]{:S(2)}) async-start(bf16[8,3,112,896]{3,2,1,0:T(8,128)(2,1)} %pick_blocks.1), calls=%async_computation.1 | async-start | bytes 9633792 | tf_op jit(solution)/shard_map/all_to_all | solution.py:1728
  310.7 110.3 %all-to-all-start.2 = ((bf16[8,3,112,896]{3,2,1,0:T(8,128)(2,1)}), bf16[8,3,112,896]{3,2,1,0:T(8,128)(2,1)}, u32[]{:S(2)}, u32[]{:S(2)}) async-start(bf16[8,3,112,896]{3,2,1,0:T(8,128)(2,1)} %get-tuple-element.127), calls=%async_computation.2 | async-start | bytes 9633792 | tf_op jit(solution)/shard_map/all_to_all | solution.py:1754
  421.0 187.4 %all-to-all-start.3 = ((bf16[8,3,112,896]{3,2,1,0:T(8,128)(2,1)}), bf16[8,3,112,896]{3,2,1,0:T(8,128)(2,1)}, u32[]{:S(2)}, u32[]{:S(2)}) async-start(bf16[8,3,112,896]{3,2,1,0:T(8,128)(2,1)} %get-tuple-element.139), calls=%async_computation.3 | async-start | bytes 9633792 | tf_op jit(solution)/shard_map/all_to_all | solution.py:1764

commit v5 on v4

--- a/solution.py
+++ b/solution.py
@@ -944,24 +944,27 @@
     total = dz_ref[...]
     for h in range(dqkv_ref.shape[0]):
         total = total + dot(dqkv_ref[h], w_ref[h, :, : dqkv_ref.shape[2]], 1, 1)
-    share = o_ref.shape[2]
+    _, pieces, share, piece = o_ref.shape
+    turned = total.T
     for h in range(o_ref.shape[0]):
-        o_ref[h] = total[:, h * share : (h + 1) * share].astype(BF16)
-
-
-def input_grad(dqkv, weights, dz):
+        for p in range(pieces):
+            block = turned[h * share : (h + 1) * share, p * piece : (p + 1) * piece]
+            o_ref[h, p] = block.astype(BF16)
+
+
+def input_grad(dqkv, weights, dz, pieces):
     groups, rows, columns = dqkv.shape
     model = dz.shape[1]
     return pl.pallas_call(
         input_kernel,
-        out_shape=jax.ShapeDtypeStruct((groups, rows, model // groups), BF16),
+        out_shape=jax.ShapeDtypeStruct((groups, pieces, model // groups, rows // pieces), BF16),
         grid=(1,),
         in_specs=[
             whole(dqkv),
             pl.BlockSpec((groups, model, model), lambda i: (0, 0, 0)),
             whole(dz),
         ],
-        out_specs=pl.BlockSpec((groups, rows, model // groups), lambda i: (0, 0, 0)),
+        out_specs=pl.BlockSpec((groups, pieces, model // groups, rows // pieces), lambda i: (0, 0, 0, 0)),
         compiler_params=params(),
         cost_estimate=cost(2 * groups * rows * columns * model, 2 * groups * columns * model),
         name="input_grad",
@@ -1551,7 +1554,7 @@
         out_shape=(
             jax.ShapeDtypeStruct((rows, columns), F32),
             jax.ShapeDtypeStruct((micros, slots, piece, model), BF16),
-            jax.ShapeDtypeStruct((micros, slots, piece, dxs[0].shape[-1]), BF16),
+            jax.ShapeDtypeStruct((micros, slots, *dxs[0].shape[-2:]), BF16),
         ),
         in_specs=[pl.BlockSpec(memory_space=pltpu.VMEM)] * (1 + 2 * micros),
         out_specs=(pl.BlockSpec(memory_space=pltpu.VMEM),) + (pl.BlockSpec(memory_space=pl.ANY),) * 2,
@@ -1571,29 +1574,30 @@
 
 
 def deliver_kernel(
-    cuts, micros, slots, index_ref, sum_ref, y_ref, dx_ref, out_ref, grad_ref,
+    cuts, micros, slots, index_ref, sum_ref, y_ref, dx_ref, block_ref, _, out_ref, grad_ref, logits_ref,
     q_ref, k_ref, v_ref, wo_ref, wu_ref, wd_ref, bq_ref, bv_ref, bu_ref, *rest,
 ):
     plain_refs = rest[:PLAIN]
-    y_buffer, dx_buffer, in_sem, out_sem, dx_sem = rest[PLAIN:]
-    where = [(m, i) for m in range(micros) for i in range(slots)]
+    y_buffer, dx_buffer, block_buffer, in_sem, out_sem = rest[PLAIN:]
+    last = micros - 1
+    reads = [block_ref.at[index_ref[last, i]] for i in range(slots)]
+    writes = [logits_ref.at[last, i] for i in range(slots)]
+    buffers = [block_buffer.at[i] for i in range(slots)]
+    for source, target, buffer in ((y_ref, out_ref, y_buffer), (dx_ref, grad_ref, dx_buffer)):
+        for m in range(micros):
+            for i in range(slots):
+                reads.append(source.at[m, index_ref[m, i]])
+                writes.append(target.at[m, i])
+                buffers.append(buffer.at[m, i])
 
     def take(n):
-        m, i = where[n]
-        return pltpu.make_async_copy(y_ref.at[m, index_ref[m, i]], y_buffer.at[m, i], in_sem.at[n])
+        return pltpu.make_async_copy(reads[n], buffers[n], in_sem.at[n])
 
     def give(n):
-        m, i = where[n]
-        return pltpu.make_async_copy(y_buffer.at[m, i], out_ref.at[m, i], out_sem.at[n])
-
-    def take_dx(n):
-        m, i = where[n]
-        return pltpu.make_async_copy(dx_ref.at[m, index_ref[m, i]], dx_buffer.at[m, i], dx_sem.at[n])
-
-    for n in range(len(where)):
+        return pltpu.make_async_copy(buffers[n], writes[n], out_sem.at[n])
+
+    for n in range(len(reads)):
         take(n).start()
-    for n in range(len(where)):
-        take_dx(n).start()
     width = q_ref.shape[1]
     for n, ref in enumerate((q_ref, k_ref, v_ref)):
         ref[...] = sum_ref[:, n * width : (n + 1) * width]
@@ -1605,20 +1609,17 @@
         ref[...] = block[i : i + 1, : ref.shape[1]]
     for first, ref in ((QUERY_AT, bq_ref), (VALUE_AT, bv_ref), (UP_AT, bu_ref)):
         ref[...] = block[first : first + ref.shape[0], : ref.shape[1]]
-    for n in range(len(where)):
+    for n in range(len(reads)):
         take(n).wait()
         give(n).start()
-    for n, (m, i) in enumerate(where):
-        take_dx(n).wait()
-        grad_ref[m, i] = dx_buffer[m, i].astype(F32).T.astype(BF16)
-    for n in range(len(where)):
+    for n in range(len(reads)):
         give(n).wait()
 
 
-def deliver(cuts, heads, unit, index, sums, y, dx):
-    micros, slots, piece, share = dx.shape
+def deliver(cuts, heads, unit, index, sums, y, dx, blocks, logits):
+    micros, slots = dx.shape[:2]
     rows, width = sums.shape[0], heads * HEAD_DIM
-    total = micros * slots
+    total = slots + 2 * micros * slots
     dma = pltpu.SemaphoreType.DMA
     in_vmem = pl.BlockSpec(memory_space=pltpu.VMEM)
 
@@ -1629,7 +1630,8 @@
         functools.partial(deliver_kernel, cuts, micros, slots),
         out_shape=(
             jax.ShapeDtypeStruct(y.shape, BF16),
-            jax.ShapeDtypeStruct((micros, slots, share, piece), BF16),
+            jax.ShapeDtypeStruct(dx.shape, BF16),
+            jax.ShapeDtypeStruct(logits.shape, BF16),
             f32(rows, width),
             f32(rows, width),
             f32(rows, width),
@@ -1641,19 +1643,20 @@
             f32(heads, unit // heads // slots),
         )
         + (f32(1, rows),) * PLAIN,
-        in_specs=[SMALL, in_vmem, ANYWHERE, ANYWHERE],
-        out_specs=(ANYWHERE,) + (in_vmem,) * (10 + PLAIN),
+        in_specs=[SMALL, in_vmem] + [ANYWHERE] * 4,
+        out_specs=(ANYWHERE,) * 3 + (in_vmem,) * (9 + PLAIN),
         scratch_shapes=[
             pltpu.VMEM(y.shape, BF16),
             pltpu.VMEM(dx.shape, BF16),
-            dma((total,)),
+            pltpu.VMEM(blocks.shape, BF16),
             dma((total,)),
             dma((total,)),
         ],
+        input_output_aliases={5: 2},
         compiler_params=params(),
         cost_estimate=cost(0, 4 * y.size),
         name="deliver",
-    )(index, sums, y, dx)
+    )(index, sums, y, dx, blocks, logits)
 
 
 def fits(mesh):
@@ -1743,7 +1746,7 @@
             info, qkv, attend, context, dcontext, cot_square, m
         )
         dqkv = across_heads(dqkv, 5)
-        dx = input_grad(dqkv, weights, dz)
+        dx = input_grad(dqkv, weights, dz, per)
         kept.append((b0, h1, b2, dqkv, context_rows, b1, act))
         sums_own.append(own)
         sums_rows.append(sums)
@@ -1765,16 +1768,13 @@
         if m == 0:
             grad_logits = place_blocks(sent[m], m, micros, dealing, grad_logits)
     ys = [y.reshape(per, piece, model) for y, _ in returned]
-    dxs = [dx.reshape(groups, per, piece, -1) for _, dx in returned]
+    dxs = [dx for _, dx in returned]
     part = part.reshape(groups, slots, own_rows, -1)
     part, _ = lax.optimization_barrier((part, grad_logits))
     part, all_y, all_dx = finish(part, ys, dxs, slots, groups, 7)
-    out_tokens, grad_tokens, dq, dk, dv, dwo, dwu, dwd, dbq, dbv, dbu, *plain = deliver(
-        cuts, heads, unit, dealing, part, all_y, all_dx
+    out_tokens, grad_tokens, grad_logits, dq, dk, dv, dwo, dwu, dwd, dbq, dbv, dbu, *plain = deliver(
+        cuts, heads, unit, dealing, part, all_y, all_dx, sent[-1], grad_logits
     )
-    for m in range(1, micros):
-        grad_logits = place_blocks(sent[m], m, micros, dealing, grad_logits)
-
     plain = [row.reshape(-1) for row in plain]
     return (
         out_tokens,

time: 615 us -> 608 us (0.989)
  no operation moved by 1% of the time
where the time goes in v5:
time: 608 us; the launch traced here: 607 us
  Pallas kernels  541 us (89%)
  starting transfers between devices  43.1 us (7%)
  waiting for transfers between devices  22.4 us (4%)
    pallas_call x1, Pallas kernels, finish(): pl.pallas_call(body, out_shape=(jax.ShapeDtypeStruct((rows, columns), F32...  160 us
    pallas_call x8, Pallas kernels, across_heads(): pl.pallas_call(functools.partial(cross_kernel, groups), out_shape=jax.Sha...  104 us
    pallas_call x1, Pallas kernels, gather_line(): pl.pallas_call(functools.partial(line_kernel, slots, groups), out_shape=(...  65.5 us
    pallas_call x1, Pallas kernels, gather_plane(): pl.pallas_call(plane_kernel, out_shape=jax.ShapeDtypeStruct(shards.shape,...  45.5 us
    pallas_call x2, Pallas kernels, attention_backward(): pl.pallas_call(functools.partial(backward_kernel, heads, micro), out_shap...  36.5 us
    pallas_call x2, Pallas kernels, attention_forward(): pl.pallas_call(functools.partial(forward_kernel, heads, micro), out_shape...  35.9 us
    pallas_call x2, Pallas kernels, row_work(): pl.pallas_call(functools.partial(rows_kernel, cuts, micro), out_shape=(sh...  33.9 us
    all_to_all x2, starting transfers between devices, on_device(): got = lax.all_to_all(send, 'seq', split_axis=0, concat_axis=0, tiled=True)  30 us
  transfers between devices with their start and end apart: 4, of which 3 were waited for; matrix products, arithmetic and copies ran while one was open for 0% of the time, Pallas kernels for 76%

profile of v5, /device:TPU:15, one launch (start us, length us, event | category | flops | bytes accessed | tf_op | source)
XLA Modules:
  0.0 607.0 jit_solution(105272724841056531)
XLA Ops:
  0.7 7.4 %prepare.1 = (bf16[8,3,112,896]{3,2,1,0:T(8,128)(2,1)}, bf16[2,4,112,768]{3,2,1,0:T(8,128)(2,1)}, bf16[96,2432]{1,0:T(8,128)(2,1)}, s32[2,2]{1,0:T(2,128)}) custom-call(s32[2,8]{1,0:T(2,128)} %lengths_ref.1, s32[2,8]{1,0:T(2,128)} %index_ref.3, bf16[2,8,3,112,896]{4,3,2,1,0:T(8,128)(2,1)} %bitcast.37, bf16[2,8,112,768]{3,2,1,0:T(8,128)(2,1)} %refs_2_.1, ...), custom_call_target="tpu_custom_call" | custom-call | bytes 96337 | tf_op jit(solution)/shard_map/prepare/pallas_call | solution.py:545
  8.0 65.5 %gather_line.1 = (bf16[4,8,96,2432]{3,2,1,0:T(8,128)(2,1)}, bf16[4,2,112,768]{3,2,1,0:T(8,128)(2,1)}) custom-call(bf16[96,2432]{1,0:T(8,128)(2,1)} %get-tuple-element.88.pack_ref, bf16[2,4,112,768]{3,2,1,0:T(8,128)(2,1)} %get-tuple-element.89.piece_ref), custom_call_target="tpu_custom_call" | custom-call | bytes 600000 | tf_op jit(solution)/shard_map/gather_line/pallas_call | solution.py:1235
  73.5 22.4 %all-to-all-start = ((bf16[8,3,112,896]{3,2,1,0:T(8,128)(2,1)}), bf16[8,3,112,896]{3,2,1,0:T(8,128)(2,1)}, u32[]{:S(2)}, u32[]{:S(2)}) async-start(bf16[8,3,112,896]{3,2,1,0:T(8,128)(2,1)} %get-tuple-element.96), calls=%async_computation | async-start | bytes 9633792 | tf_op jit(solution)/shard_map/all_to_all | solution.py:1731
  95.9 4.9 pick_blocks.1
  100.9 45.5 %gather_plane.1.x_ref = bf16[4,8,96,2432]{3,2,1,0:T(8,128)(2,1)} custom-call(bf16[4,8,96,2432]{3,2,1,0:T(8,128)(2,1)} %get-tuple-element.92.in_ref), custom_call_target="tpu_custom_call", output_to_operand_aliasing={{}: (0, {})} | custom-call | bytes 1200000 | tf_op jit(solution)/shard_map/gather_plane/pallas_call | solution.py:1289
  146.4 1.9 unpack_vectors.1
  148.3 6.2 %project.1 = (bf16[4,224,576]{2,1,0:T(8,128)(2,1)}, bf16[4,224,576]{2,1,0:T(8,128)(2,1)}) custom-call(bf16[4,224,768]{2,1,0:T(8,128)(2,1)} %bitcast.42, bf16[4,768,2432]{2,1,0:T(8,128)(2,1)} %bitcast.31, f32[4,1,576]{2,1,0:T(1,128)} %get-tuple-element.93.b_ref), custom_call_target="tpu_custom_call" | custom-call | flops 15854469 | bytes 45711 | tf_op jit(solution)/shard_map/project/pallas_call | solution.py:652
  154.5 16.4 %across_heads.8.qkv_ref = bf16[4,224,576]{2,1,0:T(8,128)(2,1)} custom-call(bf16[4,224,576]{2,1,0:T(8,128)(2,1)} %get-tuple-element.94.x_ref), custom_call_target="tpu_custom_call" | custom-call | bytes 206438 | tf_op jit(solution)/shard_map/across_heads/pallas_call | solution.py:1096
  170.9 16.1 %across_heads.10.qkv_ref = bf16[4,224,576]{2,1,0:T(8,128)(2,1)} custom-call(bf16[4,224,576]{2,1,0:T(8,128)(2,1)} %get-tuple-element.101.x_ref), custom_call_target="tpu_custom_call" | custom-call | bytes 206438 | tf_op jit(solution)/shard_map/across_heads/pallas_call | solution.py:1096
  187.0 12.1 %all-to-all-done.prev_ref = bf16[8,3,112,896]{3,2,1,0:T(8,128)(2,1)} async-done(((bf16[8,3,112,896]{3,2,1,0:T(8,128)(2,1)}), bf16[8,3,112,896]{3,2,1,0:T(8,128)(2,1)}, u32[]{:S(2)}, u32[]{:S(2)}) %all-to-all-start) | async-done | bytes 4816928 | tf_op jit(solution)/shard_map/all_to_all | solution.py:1731
  199.1 7.6 %all-to-all-start.1 = ((bf16[8,3,112,896]{3,2,1,0:T(8,128)(2,1)}), bf16[8,3,112,896]{3,2,1,0:T(8,128)(2,1)}, u32[]{:S(2)}, u32[]{:S(2)}) async-start(bf16[8,3,112,896]{3,2,1,0:T(8,128)(2,1)} %pick_blocks.1), calls=%async_computation.1 | async-start | bytes 9633792 | tf_op jit(solution)/shard_map/all_to_all | solution.py:1731
  206.7 18.0 %attention_forward.2 = (bf16[2,3,896,896]{3,2,1,0:T(8,128)(2,1)}, bf16[8,3,112,896]{3,2,1,0:T(8,128)(2,1)}, bf16[4,224,192]{2,1,0:T(8,128)(2,1)}) custom-call(s32[2,2]{1,0:T(2,128)} %get-tuple-element.91.info_ref, bf16[4,224,576]{2,1,0:T(8,128)(2,1)} %across_heads.8.qkv_ref, bf16[8,3,112,896]{3,2,1,0:T(8,128)(2,1)} %all-to-all-done.prev_ref), custom_call_target="tpu_custom_call" | custom-call | flops 24662508 | bytes 144506 | tf_op jit(solution)/shard_map/attention_forward/pallas_call | solution.py:716
  224.7 10.3 %across_heads.9.con_ref.refs_10_ = bf16[4,224,192]{2,1,0:T(8,128)(2,1)} custom-call(bf16[4,224,192]{2,1,0:T(8,128)(2,1)} %get-tuple-element.97.x_ref.context_ref), custom_call_target="tpu_custom_call" | custom-call | bytes 68812 | tf_op jit(solution)/shard_map/across_heads/pallas_call | solution.py:1096
  235.0 16.9 %row_work.2 = (bf16[224,768]{1,0:T(8,128)(2,1)}, f32[224,768]{1,0:T(8,128)}, bf16[4,224,192]{2,1,0:T(8,128)(2,1)}, bf16[224,768]{1,0:T(8,128)(2,1)}, bf16[4,224,...) custom-call(bf16[4,224,192]{2,1,0:T(8,128)(2,1)} %across_heads.9.con, ...), custom_call_target="tpu_custom_call" | custom-call | flops 52848232 | bytes 149422 | tf_op jit(solution)/shard_map/row_work/pallas_call | solution.py:914
  251.9 8.8 %across_heads.12.dcon_ref = bf16[4,224,192]{2,1,0:T(8,128)(2,1)} custom-call(bf16[4,224,192]{2,1,0:T(8,128)(2,1)} %get-tuple-element.111.x_ref), custom_call_target="tpu_custom_call" | custom-call | bytes 68812 | tf_op jit(solution)/shard_map/across_heads/pallas_call | solution.py:1096
  260.8 18.2 %attention_backward.2 = (bf16[8,3,112,896]{3,2,1,0:T(8,128)(2,1)}, bf16[4,224,576]{2,1,0:T(8,128)(2,1)}, f32[2,192]{1,0:T(2,128)}) custom-call(s32[2,2]{1,0:T(2,128)} %get-tuple-element.91.info_ref, bf16[4,224,576]{2,1,0:T(8,128)(2,1)} %across_heads.8.qkv_ref, bf16[8,3,112,896]{3,2,1,0:T(8,128)(2,1)} %get-tuple-element.110.attend_ref, ...), custom_call_target="tpu_custom_call" | custom-call | flops 49325016 | bytes 144506 | tf_op jit(solution)/shard_map/attention_backward/pallas_call | solution.py:799
  279.0 16.1 %across_heads.13.refs_8_.dqkv_ref = bf16[4,224,576]{2,1,0:T(8,128)(2,1)} custom-call(bf16[4,224,576]{2,1,0:T(8,128)(2,1)} %get-tuple-element.112.x_ref), custom_call_target="tpu_custom_call" | custom-call | bytes 206438 | tf_op jit(solution)/shard_map/across_heads/pallas_call | solution.py:1096
  295.2 5.3 input_grad.2.refs_2_
  300.4 10.3 %all-to-all-done.1.prev_ref = bf16[8,3,112,896]{3,2,1,0:T(8,128)(2,1)} async-done(((bf16[8,3,112,896]{3,2,1,0:T(8,128)(2,1)}), bf16[8,3,112,896]{3,2,1,0:T(8,128)(2,1)}, u32[]{:S(2)}, u32[]{:S(2)}) %all-to-all-start.1) | async-done | bytes 4816928 | tf_op jit(solution)/shard_map/all_to_all | solution.py:1731
  310.7 6.5 %all-to-all-start.2 = ((bf16[8,3,112,896]{3,2,1,0:T(8,128)(2,1)}), bf16[8,3,112,896]{3,2,1,0:T(8,128)(2,1)}, u32[]{:S(2)}, u32[]{:S(2)}) async-start(bf16[8,3,112,896]{3,2,1,0:T(8,128)(2,1)} %get-tuple-element.128), calls=%async_computation.2 | async-start | bytes 9633792 | tf_op jit(solution)/shard_map/all_to_all | solution.py:1757
  317.2 18.0 %attention_forward.3 = (bf16[2,3,896,896]{3,2,1,0:T(8,128)(2,1)}, bf16[8,3,112,896]{3,2,1,0:T(8,128)(2,1)}, bf16[4,224,192]{2,1,0:T(8,128)(2,1)}) custom-call(s32[2,2]{1,0:T(2,128)} %get-tuple-element.91.info_ref, bf16[4,224,576]{2,1,0:T(8,128)(2,1)} %across_heads.10.qkv_ref, ...), custom_call_target="tpu_custom_call", output_to_operand_aliasing={{0}: (3, {})} | custom-call | flops 24662508 | bytes 144506 | tf_op jit(solution)/shard_map/attention_forward/pallas_call | solution.py:716
  335.1 10.8 %across_heads.11.con_ref.refs_11_ = bf16[4,224,192]{2,1,0:T(8,128)(2,1)} custom-call(bf16[4,224,192]{2,1,0:T(8,128)(2,1)} %get-tuple-element.104.x_ref.context_ref), custom_call_target="tpu_custom_call" | custom-call | bytes 68812 | tf_op jit(solution)/shard_map/across_heads/pallas_call | solution.py:1096
  346.0 16.9 %row_work.3 = (bf16[224,768]{1,0:T(8,128)(2,1)}, f32[224,768]{1,0:T(8,128)}, bf16[4,224,192]{2,1,0:T(8,128)(2,1)}, bf16[224,768]{1,0:T(8,128)(2,1)}, bf16[4,224,...) custom-call(bf16[4,224,192]{2,1,0:T(8,128)(2,1)} %across_heads.11.co, ...), custom_call_target="tpu_custom_call" | custom-call | flops 52848232 | bytes 149422 | tf_op jit(solution)/shard_map/row_work/pallas_call | solution.py:914
  362.9 8.8 %across_heads.14.dcon_ref = bf16[4,224,192]{2,1,0:T(8,128)(2,1)} custom-call(bf16[4,224,192]{2,1,0:T(8,128)(2,1)} %get-tuple-element.114.x_ref), custom_call_target="tpu_custom_call" | custom-call | bytes 68812 | tf_op jit(solution)/shard_map/across_heads/pallas_call | solution.py:1096
  371.7 18.3 %attention_backward.3 = (bf16[8,3,112,896]{3,2,1,0:T(8,128)(2,1)}, bf16[4,224,576]{2,1,0:T(8,128)(2,1)}, f32[2,192]{1,0:T(2,128)}) custom-call(s32[2,2]{1,0:T(2,128)} %get-tuple-element.91.info_ref, bf16[4,224,576]{2,1,0:T(8,128)(2,1)} %across_heads.10.qkv_ref, bf16[8,3,112,896]{3,2,1,0:T(8,128)(2,1)} %get-tuple-element.113.attend_ref, ...), custom_call_target="tpu_custom_call" | custom-call | flops 49325016 | bytes 144506 | tf_op jit(solution)/shard_map/attention_backward/pallas_call | solution.py:799
  390.0 16.1 %across_heads.15.refs_9_.dqkv_ref = bf16[4,224,576]{2,1,0:T(8,128)(2,1)} custom-call(bf16[4,224,576]{2,1,0:T(8,128)(2,1)} %get-tuple-element.115.x_ref), custom_call_target="tpu_custom_call" | custom-call | bytes 206438 | tf_op jit(solution)/shard_map/across_heads/pallas_call | solution.py:1096
  406.2 14.7 %weight_grads.1 = bf16[4,768,2432]{2,1,0:T(8,128)(2,1)} custom-call(bf16[4,224,768]{2,1,0:T(8,128)(2,1)} %bitcast.45, bf16[4,224,768]{2,1,0:T(8,128)(2,1)} %bitcast.46, bf16[224,768]{1,0:T(8,128)(2,1)} %get-tuple-element.100.refs_2_, bf16[224,768]{1,0:T(8,128)(2,1)} %get-tuple-element.105.refs_3_, bf16[224,768]{1,0:T(8,128)(2,1)} %get-tuple-element.106.refs_4_, ...), custom_call_target="tpu_custom_call" | custom-call | flops 63417876 | bytes 141557 | tf_op jit(solution)/shard_map/weight_grads/pallas_call | solution.py:1034
  420.9 0.1 all-to-all-done.2.x_ref
  421.0 6.6 %all-to-all-start.3 = ((bf16[8,3,112,896]{3,2,1,0:T(8,128)(2,1)}), bf16[8,3,112,896]{3,2,1,0:T(8,128)(2,1)}, u32[]{:S(2)}, u32[]{:S(2)}) async-start(bf16[8,3,112,896]{3,2,1,0:T(8,128)(2,1)} %get-tuple-element.137), calls=%async_computation.3 | async-start | bytes 9633792 | tf_op jit(solution)/shard_map/all_to_all | solution.py:1767
  427.6 4.9 place_blocks.1._
  432.5 5.3 input_grad.3.refs_3_
  437.8 160.1 %finish.1 = (f32[96,2432]{1,0:T(8,128)}, bf16[2,8,112,768]{3,2,1,0:T(8,128)(2,1)}, bf16[2,8,192,112]{3,2,1,0:T(8,128)(2,1)}) custom-call(bf16[4,4,2,96,2432]{4,3,2,1,0:T(8,128)(2,1)} %bitcast.36, bf16[2,112,768]{2,1,0:T(8,128)(2,1)} %bitcast.48, bf16[2,112,768]{2,1,0:T(8,128)(2,1)} %bitcast.49, bf16[4,2,192,112]{3,2,1,0:T(8,128)(2,1)} %input_grad.2.refs_2_, ...), custom_call_target="tpu_custom_call" | custom-call | bytes 1200000 | tf_op jit(solution)/shard_map/finish/pallas_call | solution.py:1552
  597.8 0.0 all-to-all-done.3.block_ref
  597.9 9.0 %deliver.1 = (bf16[2,8,112,768]{3,2,1,0:T(8,128)(2,1)}, bf16[2,8,192,112]{3,2,1,0:T(8,128)(2,1)}, bf16[2,8,3,112,896]{4,3,2,1,0:T(8,128)(2,1)}, f32[96,192]{1,0:...) custom-call(s32[2,8]{1,0:T(2,128)} %index_ref.3, ...), custom_call_target="tpu_custom_call", output_to_operand_aliasing={{2}: (5, {})} | custom-call | bytes 55050 | tf_op jit(solution)/shard_map/deliver/pallas_call | solution.py:1629
Async XLA Ops:
  73.5 125.6 %all-to-all-start = ((bf16[8,3,112,896]{3,2,1,0:T(8,128)(2,1)}), bf16[8,3,112,896]{3,2,1,0:T(8,128)(2,1)}, u32[]{:S(2)}, u32[]{:S(2)}) async-start(bf16[8,3,112,896]{3,2,1,0:T(8,128)(2,1)} %get-tuple-element.96), calls=%async_computation | async-start | bytes 9633792 | tf_op jit(solution)/shard_map/all_to_all | solution.py:1731
  199.1 111.6 %all-to-all-start.1 = ((bf16[8,3,112,896]{3,2,1,0:T(8,128)(2,1)}), bf16[8,3,112,896]{3,2,1,0:T(8,128)(2,1)}, u32[]{:S(2)}, u32[]{:S(2)}) async-start(bf16[8,3,112,896]{3,2,1,0:T(8,128)(2,1)} %pick_blocks.1), calls=%async_computation.1 | async-start | bytes 9633792 | tf_op jit(solution)/shard_map/all_to_all | solution.py:1731
  310.7 110.3 %all-to-all-start.2 = ((bf16[8,3,112,896]{3,2,1,0:T(8,128)(2,1)}), bf16[8,3,112,896]{3,2,1,0:T(8,128)(2,1)}, u32[]{:S(2)}, u32[]{:S(2)}) async-start(bf16[8,3,112,896]{3,2,1,0:T(8,128)(2,1)} %get-tuple-element.128), calls=%async_computation.2 | async-start | bytes 9633792 | tf_op jit(solution)/shard_map/all_to_all | solution.py:1757
  421.0 176.9 %all-to-all-start.3 = ((bf16[8,3,112,896]{3,2,1,0:T(8,128)(2,1)}), bf16[8,3,112,896]{3,2,1,0:T(8,128)(2,1)}, u32[]{:S(2)}, u32[]{:S(2)}) async-start(bf16[8,3,112,896]{3,2,1,0:T(8,128)(2,1)} %get-tuple-element.137), calls=%async_computation.3 | async-start | bytes 9633792 | tf_op jit(solution)/shard_map/all_to_all | solution.py:1767

commit v6 on v5

--- a/solution.py
+++ b/solution.py
@@ -1470,16 +1470,19 @@
         for p, home in enumerate(homes):
             pl.when(home != here)(lambda m=m, p=p: home_copy(m, p).start())
             pl.when(home == here)(lambda m=m, p=p: home_here(m, p).start())
-            for h in range(groups):
-                same = is_me(home, h)
-                pl.when(jnp.logical_not(same))(lambda m=m, p=p, h=h: grad_copy(m, p, h).start())
-                pl.when(same)(lambda m=m, p=p, h=h: grad_here(m, p, h).start())
     for k in range(LINE):
         begin(k)
         if k >= 1:
             middle(k - 1)
         if k >= 2:
             end(k - 2)
+        if k == 2:
+            for m in range(micros):
+                for p, home in enumerate(homes):
+                    for h in range(groups):
+                        same = is_me(home, h)
+                        pl.when(jnp.logical_not(same))(lambda m=m, p=p, h=h: grad_copy(m, p, h).start())
+                        pl.when(same)(lambda m=m, p=p, h=h: grad_here(m, p, h).start())
     middle(LINE - 1)
     end(LINE - 2)
     for m in range(micros):

time: 608 us -> 607 us (level); the launches traced: 607 us -> 599 us
  Pallas kernels: 541 us -> 533 us
    pallas_call x1, Pallas kernels: 160 us -> 152 us  [finish(): pl.pallas_call(body, out_shape=(jax.ShapeDtypeStruct((rows, columns), F32...]
  transfers between devices with their start and end apart: 4 -> 4, of which waited for: 3 -> 3; matrix products, arithmetic and copies ran while one was open for 0% -> 0% of each run, Pallas kernels for 76% -> 75%
where the time goes in v6:
time: 607 us; the launch traced here: 599 us
  Pallas kernels  533 us (88%)
  starting transfers between devices  43.1 us (7%)
  waiting for transfers between devices  22.4 us (4%)
    pallas_call x1, Pallas kernels, finish(): pl.pallas_call(body, out_shape=(jax.ShapeDtypeStruct((rows, columns), F32...  152 us
    pallas_call x8, Pallas kernels, across_heads(): pl.pallas_call(functools.partial(cross_kernel, groups), out_shape=jax.Sha...  104 us
    pallas_call x1, Pallas kernels, gather_line(): pl.pallas_call(functools.partial(line_kernel, slots, groups), out_shape=(...  65.5 us
    pallas_call x1, Pallas kernels, gather_plane(): pl.pallas_call(plane_kernel, out_shape=jax.ShapeDtypeStruct(shards.shape,...  45.5 us
    pallas_call x2, Pallas kernels, attention_backward(): pl.pallas_call(functools.partial(backward_kernel, heads, micro), out_shap...  36.5 us
    pallas_call x2, Pallas kernels, attention_forward(): pl.pallas_call(functools.partial(forward_kernel, heads, micro), out_shape...  35.9 us
    pallas_call x2, Pallas kernels, row_work(): pl.pallas_call(functools.partial(rows_kernel, cuts, micro), out_shape=(sh...  33.9 us
    all_to_all x2, starting transfers between devices, on_device(): got = lax.all_to_all(send, 'seq', split_axis=0, concat_axis=0, tiled=True)  30 us
  transfers between devices with their start and end apart: 4, of which 3 were waited for; matrix products, arithmetic and copies ran while one was open for 0% of the time, Pallas kernels for 75%

profile of v6, /device:TPU:15, one launch (start us, length us, event | category | flops | bytes accessed | tf_op | source)
XLA Modules:
  0.0 599.3 jit_solution(5700847925680046963)
XLA Ops:
  0.7 7.4 %prepare.1 = (bf16[8,3,112,896]{3,2,1,0:T(8,128)(2,1)}, bf16[2,4,112,768]{3,2,1,0:T(8,128)(2,1)}, bf16[96,2432]{1,0:T(8,128)(2,1)}, s32[2,2]{1,0:T(2,128)}) custom-call(s32[2,8]{1,0:T(2,128)} %lengths_ref.1, s32[2,8]{1,0:T(2,128)} %index_ref.3, bf16[2,8,3,112,896]{4,3,2,1,0:T(8,128)(2,1)} %bitcast.37, bf16[2,8,112,768]{3,2,1,0:T(8,128)(2,1)} %refs_2_.1, ...), custom_call_target="tpu_custom_call" | custom-call | bytes 96337 | tf_op jit(solution)/shard_map/prepare/pallas_call | solution.py:545
  8.0 65.5 %gather_line.1 = (bf16[4,8,96,2432]{3,2,1,0:T(8,128)(2,1)}, bf16[4,2,112,768]{3,2,1,0:T(8,128)(2,1)}) custom-call(bf16[96,2432]{1,0:T(8,128)(2,1)} %get-tuple-element.88.pack_ref, bf16[2,4,112,768]{3,2,1,0:T(8,128)(2,1)} %get-tuple-element.89.piece_ref), custom_call_target="tpu_custom_call" | custom-call | bytes 600000 | tf_op jit(solution)/shard_map/gather_line/pallas_call | solution.py:1235
  73.5 22.4 %all-to-all-start = ((bf16[8,3,112,896]{3,2,1,0:T(8,128)(2,1)}), bf16[8,3,112,896]{3,2,1,0:T(8,128)(2,1)}, u32[]{:S(2)}, u32[]{:S(2)}) async-start(bf16[8,3,112,896]{3,2,1,0:T(8,128)(2,1)} %get-tuple-element.96), calls=%async_computation | async-start | bytes 9633792 | tf_op jit(solution)/shard_map/all_to_all | solution.py:1734
  95.9 4.9 pick_blocks.1
  100.9 45.5 %gather_plane.1.x_ref = bf16[4,8,96,2432]{3,2,1,0:T(8,128)(2,1)} custom-call(bf16[4,8,96,2432]{3,2,1,0:T(8,128)(2,1)} %get-tuple-element.92.in_ref), custom_call_target="tpu_custom_call", output_to_operand_aliasing={{}: (0, {})} | custom-call | bytes 1200000 | tf_op jit(solution)/shard_map/gather_plane/pallas_call | solution.py:1289
  146.4 1.9 unpack_vectors.1
  148.3 6.2 %project.1 = (bf16[4,224,576]{2,1,0:T(8,128)(2,1)}, bf16[4,224,576]{2,1,0:T(8,128)(2,1)}) custom-call(bf16[4,224,768]{2,1,0:T(8,128)(2,1)} %bitcast.42, bf16[4,768,2432]{2,1,0:T(8,128)(2,1)} %bitcast.31, f32[4,1,576]{2,1,0:T(1,128)} %get-tuple-element.93.b_ref), custom_call_target="tpu_custom_call" | custom-call | flops 15854469 | bytes 45711 | tf_op jit(solution)/shard_map/project/pallas_call | solution.py:652
  154.5 16.4 %across_heads.8.qkv_ref = bf16[4,224,576]{2,1,0:T(8,128)(2,1)} custom-call(bf16[4,224,576]{2,1,0:T(8,128)(2,1)} %get-tuple-element.94.x_ref), custom_call_target="tpu_custom_call" | custom-call | bytes 206438 | tf_op jit(solution)/shard_map/across_heads/pallas_call | solution.py:1096
  170.9 16.1 %across_heads.10.qkv_ref = bf16[4,224,576]{2,1,0:T(8,128)(2,1)} custom-call(bf16[4,224,576]{2,1,0:T(8,128)(2,1)} %get-tuple-element.101.x_ref), custom_call_target="tpu_custom_call" | custom-call | bytes 206438 | tf_op jit(solution)/shard_map/across_heads/pallas_call | solution.py:1096
  187.0 12.1 %all-to-all-done.prev_ref = bf16[8,3,112,896]{3,2,1,0:T(8,128)(2,1)} async-done(((bf16[8,3,112,896]{3,2,1,0:T(8,128)(2,1)}), bf16[8,3,112,896]{3,2,1,0:T(8,128)(2,1)}, u32[]{:S(2)}, u32[]{:S(2)}) %all-to-all-start) | async-done | bytes 4816928 | tf_op jit(solution)/shard_map/all_to_all | solution.py:1734
  199.1 7.6 %all-to-all-start.1 = ((bf16[8,3,112,896]{3,2,1,0:T(8,128)(2,1)}), bf16[8,3,112,896]{3,2,1,0:T(8,128)(2,1)}, u32[]{:S(2)}, u32[]{:S(2)}) async-start(bf16[8,3,112,896]{3,2,1,0:T(8,128)(2,1)} %pick_blocks.1), calls=%async_computation.1 | async-start | bytes 9633792 | tf_op jit(solution)/shard_map/all_to_all | solution.py:1734
  206.7 18.0 %attention_forward.2 = (bf16[2,3,896,896]{3,2,1,0:T(8,128)(2,1)}, bf16[8,3,112,896]{3,2,1,0:T(8,128)(2,1)}, bf16[4,224,192]{2,1,0:T(8,128)(2,1)}) custom-call(s32[2,2]{1,0:T(2,128)} %get-tuple-element.91.info_ref, bf16[4,224,576]{2,1,0:T(8,128)(2,1)} %across_heads.8.qkv_ref, bf16[8,3,112,896]{3,2,1,0:T(8,128)(2,1)} %all-to-all-done.prev_ref), custom_call_target="tpu_custom_call" | custom-call | flops 24662508 | bytes 144506 | tf_op jit(solution)/shard_map/attention_forward/pallas_call | solution.py:716
  224.7 10.3 %across_heads.9.con_ref.refs_10_ = bf16[4,224,192]{2,1,0:T(8,128)(2,1)} custom-call(bf16[4,224,192]{2,1,0:T(8,128)(2,1)} %get-tuple-element.97.x_ref.context_ref), custom_call_target="tpu_custom_call" | custom-call | bytes 68812 | tf_op jit(solution)/shard_map/across_heads/pallas_call | solution.py:1096
  235.0 16.9 %row_work.2 = (bf16[224,768]{1,0:T(8,128)(2,1)}, f32[224,768]{1,0:T(8,128)}, bf16[4,224,192]{2,1,0:T(8,128)(2,1)}, bf16[224,768]{1,0:T(8,128)(2,1)}, bf16[4,224,...) custom-call(bf16[4,224,192]{2,1,0:T(8,128)(2,1)} %across_heads.9.con, ...), custom_call_target="tpu_custom_call" | custom-call | flops 52848232 | bytes 149422 | tf_op jit(solution)/shard_map/row_work/pallas_call | solution.py:914
  251.9 8.8 %across_heads.12.dcon_ref = bf16[4,224,192]{2,1,0:T(8,128)(2,1)} custom-call(bf16[4,224,192]{2,1,0:T(8,128)(2,1)} %get-tuple-element.111.x_ref), custom_call_target="tpu_custom_call" | custom-call | bytes 68812 | tf_op jit(solution)/shard_map/across_heads/pallas_call | solution.py:1096
  260.8 18.2 %attention_backward.2 = (bf16[8,3,112,896]{3,2,1,0:T(8,128)(2,1)}, bf16[4,224,576]{2,1,0:T(8,128)(2,1)}, f32[2,192]{1,0:T(2,128)}) custom-call(s32[2,2]{1,0:T(2,128)} %get-tuple-element.91.info_ref, bf16[4,224,576]{2,1,0:T(8,128)(2,1)} %across_heads.8.qkv_ref, bf16[8,3,112,896]{3,2,1,0:T(8,128)(2,1)} %get-tuple-element.110.attend_ref, ...), custom_call_target="tpu_custom_call" | custom-call | flops 49325016 | bytes 144506 | tf_op jit(solution)/shard_map/attention_backward/pallas_call | solution.py:799
  279.0 16.1 %across_heads.13.refs_8_.dqkv_ref = bf16[4,224,576]{2,1,0:T(8,128)(2,1)} custom-call(bf16[4,224,576]{2,1,0:T(8,128)(2,1)} %get-tuple-element.112.x_ref), custom_call_target="tpu_custom_call" | custom-call | bytes 206438 | tf_op jit(solution)/shard_map/across_heads/pallas_call | solution.py:1096
  295.2 5.3 input_grad.2.refs_2_
  300.4 10.3 %all-to-all-done.1.prev_ref = bf16[8,3,112,896]{3,2,1,0:T(8,128)(2,1)} async-done(((bf16[8,3,112,896]{3,2,1,0:T(8,128)(2,1)}), bf16[8,3,112,896]{3,2,1,0:T(8,128)(2,1)}, u32[]{:S(2)}, u32[]{:S(2)}) %all-to-all-start.1) | async-done | bytes 4816928 | tf_op jit(solution)/shard_map/all_to_all | solution.py:1734
  310.7 6.5 %all-to-all-start.2 = ((bf16[8,3,112,896]{3,2,1,0:T(8,128)(2,1)}), bf16[8,3,112,896]{3,2,1,0:T(8,128)(2,1)}, u32[]{:S(2)}, u32[]{:S(2)}) async-start(bf16[8,3,112,896]{3,2,1,0:T(8,128)(2,1)} %get-tuple-element.128), calls=%async_computation.2 | async-start | bytes 9633792 | tf_op jit(solution)/shard_map/all_to_all | solution.py:1760
  317.2 18.0 %attention_forward.3 = (bf16[2,3,896,896]{3,2,1,0:T(8,128)(2,1)}, bf16[8,3,112,896]{3,2,1,0:T(8,128)(2,1)}, bf16[4,224,192]{2,1,0:T(8,128)(2,1)}) custom-call(s32[2,2]{1,0:T(2,128)} %get-tuple-element.91.info_ref, bf16[4,224,576]{2,1,0:T(8,128)(2,1)} %across_heads.10.qkv_ref, ...), custom_call_target="tpu_custom_call", output_to_operand_aliasing={{0}: (3, {})} | custom-call | flops 24662508 | bytes 144506 | tf_op jit(solution)/shard_map/attention_forward/pallas_call | solution.py:716
  335.1 10.8 %across_heads.11.con_ref.refs_11_ = bf16[4,224,192]{2,1,0:T(8,128)(2,1)} custom-call(bf16[4,224,192]{2,1,0:T(8,128)(2,1)} %get-tuple-element.104.x_ref.context_ref), custom_call_target="tpu_custom_call" | custom-call | bytes 68812 | tf_op jit(solution)/shard_map/across_heads/pallas_call | solution.py:1096
  346.0 16.9 %row_work.3 = (bf16[224,768]{1,0:T(8,128)(2,1)}, f32[224,768]{1,0:T(8,128)}, bf16[4,224,192]{2,1,0:T(8,128)(2,1)}, bf16[224,768]{1,0:T(8,128)(2,1)}, bf16[4,224,...) custom-call(bf16[4,224,192]{2,1,0:T(8,128)(2,1)} %across_heads.11.co, ...), custom_call_target="tpu_custom_call" | custom-call | flops 52848232 | bytes 149422 | tf_op jit(solution)/shard_map/row_work/pallas_call | solution.py:914
  362.9 8.8 %across_heads.14.dcon_ref = bf16[4,224,192]{2,1,0:T(8,128)(2,1)} custom-call(bf16[4,224,192]{2,1,0:T(8,128)(2,1)} %get-tuple-element.114.x_ref), custom_call_target="tpu_custom_call" | custom-call | bytes 68812 | tf_op jit(solution)/shard_map/across_heads/pallas_call | solution.py:1096
  371.7 18.3 %attention_backward.3 = (bf16[8,3,112,896]{3,2,1,0:T(8,128)(2,1)}, bf16[4,224,576]{2,1,0:T(8,128)(2,1)}, f32[2,192]{1,0:T(2,128)}) custom-call(s32[2,2]{1,0:T(2,128)} %get-tuple-element.91.info_ref, bf16[4,224,576]{2,1,0:T(8,128)(2,1)} %across_heads.10.qkv_ref, bf16[8,3,112,896]{3,2,1,0:T(8,128)(2,1)} %get-tuple-element.113.attend_ref, ...), custom_call_target="tpu_custom_call" | custom-call | flops 49325016 | bytes 144506 | tf_op jit(solution)/shard_map/attention_backward/pallas_call | solution.py:799
  390.0 16.1 %across_heads.15.refs_9_.dqkv_ref = bf16[4,224,576]{2,1,0:T(8,128)(2,1)} custom-call(bf16[4,224,576]{2,1,0:T(8,128)(2,1)} %get-tuple-element.115.x_ref), custom_call_target="tpu_custom_call" | custom-call | bytes 206438 | tf_op jit(solution)/shard_map/across_heads/pallas_call | solution.py:1096
  406.2 14.7 %weight_grads.1 = bf16[4,768,2432]{2,1,0:T(8,128)(2,1)} custom-call(bf16[4,224,768]{2,1,0:T(8,128)(2,1)} %bitcast.45, bf16[4,224,768]{2,1,0:T(8,128)(2,1)} %bitcast.46, bf16[224,768]{1,0:T(8,128)(2,1)} %get-tuple-element.100.refs_2_, bf16[224,768]{1,0:T(8,128)(2,1)} %get-tuple-element.105.refs_3_, bf16[224,768]{1,0:T(8,128)(2,1)} %get-tuple-element.106.refs_4_, ...), custom_call_target="tpu_custom_call" | custom-call | flops 63417876 | bytes 141557 | tf_op jit(solution)/shard_map/weight_grads/pallas_call | solution.py:1034
  420.9 0.1 all-to-all-done.2.x_ref
  421.0 6.6 %all-to-all-start.3 = ((bf16[8,3,112,896]{3,2,1,0:T(8,128)(2,1)}), bf16[8,3,112,896]{3,2,1,0:T(8,128)(2,1)}, u32[]{:S(2)}, u32[]{:S(2)}) async-start(bf16[8,3,112,896]{3,2,1,0:T(8,128)(2,1)} %get-tuple-element.137), calls=%async_computation.3 | async-start | bytes 9633792 | tf_op jit(solution)/shard_map/all_to_all | solution.py:1770
  427.6 4.9 place_blocks.1._
  432.5 5.3 input_grad.3.refs_3_
  437.8 152.3 %finish.1 = (f32[96,2432]{1,0:T(8,128)}, bf16[2,8,112,768]{3,2,1,0:T(8,128)(2,1)}, bf16[2,8,192,112]{3,2,1,0:T(8,128)(2,1)}) custom-call(bf16[4,4,2,96,2432]{4,3,2,1,0:T(8,128)(2,1)} %bitcast.36, bf16[2,112,768]{2,1,0:T(8,128)(2,1)} %bitcast.48, bf16[2,112,768]{2,1,0:T(8,128)(2,1)} %bitcast.49, bf16[4,2,192,112]{3,2,1,0:T(8,128)(2,1)} %input_grad.2.refs_2_, ...), custom_call_target="tpu_custom_call" | custom-call | bytes 1200000 | tf_op jit(solution)/shard_map/finish/pallas_call | solution.py:1555
  590.1 0.0 all-to-all-done.3.block_ref
  590.1 9.0 %deliver.1 = (bf16[2,8,112,768]{3,2,1,0:T(8,128)(2,1)}, bf16[2,8,192,112]{3,2,1,0:T(8,128)(2,1)}, bf16[2,8,3,112,896]{4,3,2,1,0:T(8,128)(2,1)}, f32[96,192]{1,0:...) custom-call(s32[2,8]{1,0:T(2,128)} %index_ref.3, ...), custom_call_target="tpu_custom_call", output_to_operand_aliasing={{2}: (5, {})} | custom-call | bytes 55050 | tf_op jit(solution)/shard_map/deliver/pallas_call | solution.py:1632
Async XLA Ops:
  73.5 125.6 %all-to-all-start = ((bf16[8,3,112,896]{3,2,1,0:T(8,128)(2,1)}), bf16[8,3,112,896]{3,2,1,0:T(8,128)(2,1)}, u32[]{:S(2)}, u32[]{:S(2)}) async-start(bf16[8,3,112,896]{3,2,1,0:T(8,128)(2,1)} %get-tuple-element.96), calls=%async_computation | async-start | bytes 9633792 | tf_op jit(solution)/shard_map/all_to_all | solution.py:1734
  199.1 111.6 %all-to-all-start.1 = ((bf16[8,3,112,896]{3,2,1,0:T(8,128)(2,1)}), bf16[8,3,112,896]{3,2,1,0:T(8,128)(2,1)}, u32[]{:S(2)}, u32[]{:S(2)}) async-start(bf16[8,3,112,896]{3,2,1,0:T(8,128)(2,1)} %pick_blocks.1), calls=%async_computation.1 | async-start | bytes 9633792 | tf_op jit(solution)/shard_map/all_to_all | solution.py:1734
  310.7 110.3 %all-to-all-start.2 = ((bf16[8,3,112,896]{3,2,1,0:T(8,128)(2,1)}), bf16[8,3,112,896]{3,2,1,0:T(8,128)(2,1)}, u32[]{:S(2)}, u32[]{:S(2)}) async-start(bf16[8,3,112,896]{3,2,1,0:T(8,128)(2,1)} %get-tuple-element.128), calls=%async_computation.2 | async-start | bytes 9633792 | tf_op jit(solution)/shard_map/all_to_all | solution.py:1760
  421.0 169.1 %all-to-all-start.3 = ((bf16[8,3,112,896]{3,2,1,0:T(8,128)(2,1)}), bf16[8,3,112,896]{3,2,1,0:T(8,128)(2,1)}, u32[]{:S(2)}, u32[]{:S(2)}) async-start(bf16[8,3,112,896]{3,2,1,0:T(8,128)(2,1)} %get-tuple-element.137), calls=%async_computation.3 | async-start | bytes 9633792 | tf_op jit(solution)/shard_map/all_to_all | solution.py:1770
